TPU v7x, 32 devices: a whole 2x2x4 slice. The times are simulated.
32 devices in a mesh: win: 4 (over y, x), lat: 8 (over z, core).
Axes of the slice: x: 2, y: 2, z: 4, core: 2. Of those that a mesh axis runs over, the one named last changes fastest.
Arguments:
- state: float32 [4, 1, 1024, 2048], P('win', None, 'lat'), may hold values from -6 to 6
- multipliers: float32 [4, 1, 1024, 2048], P('win', None, 'lat'), may hold values from -3 to 3
- observations: float32 [4, 2, 1, 1024, 2048], P('win', None, None, 'lat'), may hold values from -6 to 6
- obs_mask: int32 [4, 2, 1024, 2048], P('win', None, 'lat'), may hold values 0 or 1
- speed: float32 [1], replicated, may hold values from 0.1 to 0.3
- drift: float32 [1], replicated, may hold values from 0.1 to 0.4
- kappa: float32 [1], replicated, may hold values from 0.05 to 0.2
- lat_spectrum: float32 [1, 1024], replicated, may hold values from 0.05 to 1
- lon_spectrum: float32 [1, 2048], replicated, may hold values from 0.05 to 1
Outputs:
- new_state: float32 [4, 1, 1024, 2048], P('win', None, 'lat')
- new_multipliers: float32 [4, 1, 1024, 2048], P('win', None, 'lat')
All inputs are finite; a program needn't handle non-finite values. No bound on the sum of `obs_mask` on one device may be relied on, other than what follows from the above.
Results may differ from a plain program's by a relative error of at most 0.0001.
Values sent between devices are 32-bit elements; how exact they have to be, the bound alone decides.
No kernel may reach another device: no remote copies, remote signals or barrier semaphores. Data moves between devices by JAX's collectives and lax.ppermute only.
A program may use at most 64 MiB of HBM per device.

v0:
```python
import functools
import math

import numpy as np
import jax
import jax.numpy as jnp
from jax import lax
from jax.experimental import pallas as pl
from jax.experimental.pallas import tpu as pltpu
from jax.sharding import PartitionSpec as P


LANES = 128
ROWS = 8
VMEM = pl.BlockSpec(memory_space=pltpu.VMEM)
SMEM = pl.BlockSpec(memory_space=pltpu.SMEM)
ANY = pl.BlockSpec(memory_space=pl.ANY)
LIMIT = pltpu.CompilerParams(vmem_limit_bytes=16 * 2**20)


def trig_tables(count):
    low = count // LANES
    blocks = low // 2
    turn = 2.0 * math.pi
    fine = np.arange(LANES)
    coarse = np.arange(low)
    inner = turn * ((coarse[:, None] * fine[None, :]) % low) / low
    middle = turn * (((fine // low)[:, None] * fine[None, :]) % LANES) / LANES
    member = (coarse[:, None] == (fine % low)[None, :]).astype(np.float32)
    twist = turn * (coarse[:, None] * fine[None, :]) / count
    outer = turn * ((np.arange(blocks)[:, None] * coarse[None, :]) % low) / low
    even = (coarse % 2 == 0)[None, :]
    keep = np.concatenate([np.broadcast_to(even, outer.shape), np.broadcast_to(~even, outer.shape)])
    outer = np.concatenate([outer, outer])
    pack = lambda angle, scale: np.concatenate([np.cos(angle), np.sin(angle)], axis=1) * scale
    return (pack(inner, 1.0).astype(np.float32), pack(middle, 1.0).astype(np.float32), member, pack(twist, 1.0 / count).astype(np.float32),
            (np.cos(outer) * keep).astype(np.float32), (np.sin(outer) * keep).astype(np.float32))


def build_kernel(count, d_ref, inner_ref, middle_ref, member_ref, twist_ref, cos_ref, sin_ref, even_hi, even_lo, odd_hi, odd_lo, toep, hank):
    blocks = count // LANES // 2
    high = lax.Precision.HIGHEST
    mm = functools.partial(jnp.dot, precision=high, preferred_element_type=jnp.float32)

    def turned(value, table):
        real, imag = value[:, :LANES], value[:, LANES:]
        tc, ts = table[:, :LANES], table[:, LANES:]
        return jnp.concatenate([real * tc - imag * ts, real * ts + imag * tc], axis=1)

    spectrum = jnp.concatenate([d_ref[:, at:at + LANES] for at in range(0, count, LANES)], axis=0)
    g = lax.dot_general(spectrum, inner_ref[...], (((0,), (0,)), ((), ())), precision=high,
                        preferred_element_type=jnp.float32)
    g = turned(mm(member_ref[...], turned(g, middle_ref)), twist_ref)
    gc, gs = g[:, :LANES], g[:, LANES:]
    c = mm(cos_ref[...], gc) - mm(sin_ref[...], gs)
    s = mm(sin_ref[...], gc) + mm(cos_ref[...], gs)
    rows = lax.broadcasted_iota(jnp.int32, (LANES, LANES), 0)
    cols = lax.broadcasted_iota(jnp.int32, (LANES, LANES), 1)
    flip = jnp.where(rows + cols == LANES - 1, 1.0, 0.0)
    for part in range(2):
        wrap = 1.0 if part == 0 else -1.0
        hi_ref, lo_ref = (even_hi, even_lo) if part == 0 else (odd_hi, odd_lo)

        def row(table, at):
            sign = 1.0
            if at < 0 or at >= blocks:
                sign, at = wrap, at % blocks
            at += part * blocks
            return sign * table[at:at + 1]

        for b in range(blocks):
            window = jnp.concatenate([row(c, b - 1), row(c, b)], axis=1)
            window = jnp.broadcast_to(window, (LANES, 2 * LANES))
            toep[b] = pltpu.roll(window, 0, 1, stride=1, stride_axis=0)[:, LANES:]
            window = jnp.concatenate([row(s, b), row(s, b + 1)], axis=1)
            window = jnp.broadcast_to(window, (LANES, 2 * LANES))
            window = pltpu.roll(window, LANES + 1, 1, stride=1, stride_axis=0)[:, :LANES]
            hank[b] = mm(flip, window)

        def body(i, _):
            for j in range(blocks):
                t = toep[lax.rem(j - i + blocks, blocks)]
                h = hank[lax.rem(i + j, blocks)]
                if part == 1:
                    t = t * jnp.where(j < i, -1.0, 1.0)
                    h = h * jnp.where(i + j >= blocks, -1.0, 1.0)
                a = t + h
                hi = a.astype(jnp.bfloat16)
                at = (pl.ds(pl.multiple_of(i * LANES, LANES), LANES), pl.ds(j * LANES, LANES))
                hi_ref[at] = hi
                lo_ref[at] = (a - hi.astype(jnp.float32)).astype(jnp.bfloat16)
            return 0

        lax.fori_loop(0, blocks, body, 0)


def build(spectrum):
    count = spectrum.shape[1]
    half = count // 2
    tables = trig_tables(count)
    shape = jax.ShapeDtypeStruct((half, half), jnp.bfloat16)
    return pl.pallas_call(
        functools.partial(build_kernel, count),
        out_shape=[shape] * 4, in_specs=[VMEM] * 7, out_specs=[VMEM] * 4,
        scratch_shapes=[pltpu.VMEM((half // LANES, LANES, LANES), jnp.float32)] * 2,
        compiler_params=LIMIT,
        cost_estimate=pl.CostEstimate(flops=2 * half * half * 8, bytes_accessed=8 * half * half, transcendentals=0),
    )(spectrum, *tables)


def extended(block, sides, width):
    for axis, dim in sides:
        count = lax.axis_size(axis)
        forward = [(i, i + 1) for i in range(count - 1)]
        backward = [(target, source) for source, target in forward]
        low = lax.ppermute(
            lax.slice_in_dim(block, block.shape[dim] - width, None, axis=dim), axis, forward
        )
        high = lax.ppermute(lax.slice_in_dim(block, 0, width, axis=dim), axis, backward)
        block = jnp.concatenate([low, block, high], axis=dim)
    return block


def passed_along(value, axis, steps):
    count = lax.axis_size(axis)
    first, last = (max(0, -steps), min(count, count - steps))
    return lax.ppermute(value, axis, [(source, source + steps) for source in range(first, last)])


def prefix(array, axis, combine, identity):
    peers, here = (lax.axis_size(axis), lax.axis_index(axis))
    everything = lax.all_gather(array, axis)
    start = jnp.broadcast_to(jnp.asarray(identity, array.dtype), array.shape)

    def turn(k, before):
        reached = k < here
        new = combine(before, everything[k])
        return jnp.where(reached, new, before)

    return lax.fori_loop(0, peers, turn, start)


def hartley(count):
    index = jnp.arange(count, dtype=jnp.int32)
    product = index[:, None] * index[None, :] % count
    angle = product.astype(jnp.float32) * (2.0 * math.pi / count)
    return jnp.cos(angle) + jnp.sin(angle)


def advance(padded, speed, drift, kappa):
    field = padded[:, 1:-1]
    north = padded[:, 2:]
    south = padded[:, :-2]
    east = jnp.roll(field, -1, axis=-1)
    west = jnp.roll(field, 1, axis=-1)
    speed_c = speed[:, None, None]
    drift_c = drift[:, None, None]
    kappa_c = kappa[:, None, None]
    return (
        field
        - speed_c * field * (east - west) * 0.5
        - drift_c * (north - south) * 0.5
        + kappa_c * (east + west + north + south - 4.0 * field)
    )


def per_device_any(
    state, multipliers, observations, obs_mask, speed, drift, kappa, lat_spectrum, lon_spectrum
):
    high = lax.Precision.HIGHEST
    field = state[0]
    lam = multipliers[0]
    observed = observations[0]
    mask = obs_mask[0].astype(jnp.float32)
    band = field.shape[1]
    nlon = field.shape[2]
    bands = lax.axis_size("lat")
    nlat = band * bands
    columns = nlon // bands
    lat_index = lax.axis_index("lat")
    win_index = lax.axis_index("win")
    h_lon = hartley(nlon)
    h_lat = hartley(nlat)
    lon_part = lax.dynamic_slice_in_dim(lon_spectrum, lat_index * columns, columns, 1)
    weight = lat_spectrum[:, :, None] * lon_part[:, None, :]
    divisor = jnp.maximum(win_index, 1).astype(jnp.float32)
    rows_global = lat_index * band + jnp.arange(-1, band + 1, dtype=jnp.int32)
    inside = ((rows_global >= 0) & (rows_global < nlat))[None, :, None]
    padded = extended(field, (("lat", 1),), 2)
    widened = advance(padded, speed, drift, kappa)
    widened = jnp.where(inside, widened, jnp.float32(0.0))
    first = widened[:, 1:-1]
    second = advance(widened, speed, drift, kappa)
    defect = mask[0][None] * (observed[0] - first) + mask[1][None] * (observed[1] - second)
    prior_end = passed_along(second, "win", 1)
    mismatch = jnp.where(win_index > 0, field - prior_end, jnp.float32(0.0))
    lam = lam + 0.5 * mismatch
    carried = prefix(lam, "win", lambda earlier, later: earlier + later, jnp.zeros_like(lam))
    resid = defect + lam - carried / divisor
    spectral = jnp.matmul(resid, h_lon, precision=high)
    spectral = lax.all_to_all(spectral, "lat", split_axis=2, concat_axis=1, tiled=True)
    spectral = jnp.einsum("ij,ljk->lik", h_lat, spectral, precision=high) * weight
    spectral = jnp.einsum("ij,ljk->lik", h_lat, spectral, precision=high)
    spectral = lax.all_to_all(spectral, "lat", split_axis=1, concat_axis=2, tiled=True)
    increment = jnp.matmul(spectral, h_lon, precision=high) / (nlat * nlon)
    field = field + 0.5 * increment
    return (field[None], lam[None])


def split(value):
    hi = value.astype(jnp.bfloat16)
    return hi, (value - hi.astype(jnp.float32)).astype(jnp.bfloat16)


def stencil(scal, field, north, south):
    width = field.shape[1]
    east = pltpu.roll(field, width - 1, 1)
    west = pltpu.roll(field, 1, 1)
    return (
        field
        - scal[0] * field * (east - west) * 0.5
        - scal[1] * (north - south) * 0.5
        + scal[2] * (east + west + north + south - 4.0 * field)
    )


def weight_of(here_ref, table):
    return lambda number: table[here_ref[1], number]


def windowed(weight, x, mult, ended):
    half = x.shape[1] // 2
    sent = weight(SIGN) * ended + weight(SHARE) * (mult + weight(OWN) * x)
    return [part for value in (ended, sent) for part in
            (value[:, :half] + value[:, half:], value[:, :half] - value[:, half:])]


def forecast_kernel(here_ref, table, speed, drift, kappa, x_ref, mult_ref, x1_ref, *outs):
    band = x_ref.shape[0]
    weight, scal = weight_of(here_ref, table), (speed[0], drift[0], kappa[0])

    def step(source, at, count):
        return stencil(scal, source[at:at + count], source[at + 1:at + count + 1], source[at - 1:at + count - 1])

    x1_ref[ROWS - 1:ROWS] = step(x_ref, ROWS - 1, 1)
    x1_ref[band - ROWS:band - ROWS + 1] = step(x_ref, band - ROWS, 1)
    for at in range(ROWS, band - ROWS, ROWS):
        x1_ref[at:at + ROWS] = step(x_ref, at, ROWS)
    for at in range(ROWS, band - ROWS, ROWS):
        rows = slice(at, at + ROWS)
        parts = windowed(weight, x_ref[rows], mult_ref[rows], 0.5 * step(x1_ref, at, ROWS))
        for out, part in zip(outs, parts):
            out[rows] = part


def edge_kernel(bands, here_ref, table, speed, drift, kappa, x_ref, mult_ref, low_ref, high_ref, *refs):
    outs, (ext, mid, whole, parts, sems) = refs[5:10], refs[10:]
    band = x_ref.shape[0]
    edge = low_ref.shape[0]
    weight, scal = weight_of(here_ref, table), (speed[0], drift[0], kappa[0])
    copies = []
    for end in range(2):
        at = 0 if end == 0 else band - ROWS
        if end == 0:
            ext[end, ROWS - edge:ROWS] = low_ref[...]
            ext[end, ROWS:3 * ROWS] = x_ref[:2 * ROWS]
        else:
            ext[end, :2 * ROWS] = x_ref[band - 2 * ROWS:]
            ext[end, 2 * ROWS:2 * ROWS + edge] = high_ref[...]

        def step(source, row, count):
            return stencil(scal, source[end, row:row + count], source[end, row + 1:row + count + 1],
                           source[end, row - 1:row + count - 1])

        before, after = step(ext, ROWS - 1, 1), step(ext, 2 * ROWS, 1)
        if end == 0:
            before = before * jnp.where(here_ref[0] > 0, 1.0, 0.0)
        else:
            after = after * jnp.where(here_ref[0] < bands - 1, 1.0, 0.0)
        mid[end, ROWS - 1:ROWS] = before
        mid[end, 2 * ROWS:2 * ROWS + 1] = after
        mid[end, ROWS:2 * ROWS] = step(ext, ROWS, ROWS)
        rows = slice(at, at + ROWS)
        whole[end] = mid[end, ROWS:2 * ROWS]
        for number, part in enumerate(windowed(weight, x_ref[rows], mult_ref[rows], 0.5 * step(mid, ROWS, ROWS))):
            parts[end, number] = part
        sources = [whole.at[end]] + [parts.at[end, number] for number in range(4)]
        for number, (source, out) in enumerate(zip(sources, outs)):
            copies.append(pltpu.make_async_copy(source, out.at[rows], sems.at[end, number]))
            copies[-1].start()
    for copy in copies:
        copy.wait()


def forecast(here, bands, scal, x, mult, exchange_edges):
    band, width = x.shape
    shapes = [jax.ShapeDtypeStruct((band, width), jnp.float32)]
    shapes += [jax.ShapeDtypeStruct((band, width // 2), jnp.float32)] * 4
    table = jnp.asarray(WEIGHTS)
    inner = pl.pallas_call(
        forecast_kernel,
        out_shape=shapes,
        in_specs=[SMEM] * 5 + [VMEM] * 2,
        out_specs=[VMEM] * 5,
        compiler_params=LIMIT,
        cost_estimate=pl.CostEstimate(flops=40 * band * width, bytes_accessed=20 * band * width, transcendentals=0),
        name="forecast",
    )(here, table, *scal, x, mult)
    low, high = exchange_edges
    return pl.pallas_call(
        functools.partial(edge_kernel, bands),
        out_shape=shapes,
        in_specs=[SMEM] * 5 + [VMEM] * 4 + [ANY] * 5,
        out_specs=[ANY] * 5,
        input_output_aliases={9 + number: number for number in range(5)},
        scratch_shapes=[pltpu.VMEM((2, 4 * ROWS, width), jnp.float32)] * 2 + [
            pltpu.VMEM((2, ROWS, width), jnp.float32),
            pltpu.VMEM((2, 4, ROWS, width // 2), jnp.float32),
            pltpu.SemaphoreType.DMA((2, 5)),
        ],
        compiler_params=LIMIT,
        cost_estimate=pl.CostEstimate(flops=1000 * width, bytes_accessed=400 * width, transcendentals=0),
        name="edges",
    )(here, table, *scal, x, mult, low, high, *inner)


def defect_kernel(here_ref, table, x_ref, mult_ref, obs_ref, mask_ref, x1_ref, plus_ref, minus_ref,
                  base_plus, base_minus, step_plus, second_ref, third_ref):
    half = x_ref.shape[1] // 2
    weight = weight_of(here_ref, table)
    for at in range(0, x_ref.shape[0], ROWS):
        rows = slice(at, at + ROWS)
        plus, minus = plus_ref[rows], minus_ref[rows]
        base, own = [], []
        for cols, end in ((slice(0, half), plus + minus), (slice(half, 2 * half), plus - minus)):
            part = mult_ref[rows, cols] + weight(OWN) * x_ref[rows, cols]
            own.append(part)
            seen = mask_ref[:, rows, cols].astype(jnp.float32)
            base.append(
                part + seen[0] * (obs_ref[0, rows, cols] - x1_ref[rows, cols])
                + seen[1] * (obs_ref[1, rows, cols] - end)
            )
        base_plus[rows] = base[0] + base[1]
        base_minus[rows] = base[0] - base[1]
        own_plus, own_minus = own[0] + own[1], own[0] - own[1]
        step_plus[rows] = own_plus - plus
        second_ref[rows] = jnp.where(weight(FIRST) > 0.0, plus + own_plus * weight(SHARE), minus + own_minus * weight(SHARE))
        third_ref[rows] = jnp.where(weight(FIRST) > 0.0, minus + own_minus * weight(SHARE), own_minus - minus)


def defect(here, x, mult, obs, mask, x1, plus, minus):
    band, width = x.shape
    rows = 4 * ROWS
    whole = pl.BlockSpec((rows, width), lambda i: (i, 0))
    pair = pl.BlockSpec((2, rows, width), lambda i: (0, i, 0))
    part = pl.BlockSpec((rows, width // 2), lambda i: (i, 0))
    return pl.pallas_call(
        defect_kernel,
        grid=(band // rows,),
        out_shape=[jax.ShapeDtypeStruct((band, width // 2), jnp.float32)] * 5,
        in_specs=[SMEM, SMEM, whole, whole, pair, pair, whole, part, part],
        out_specs=[part] * 5,
        compiler_params=LIMIT,
        cost_estimate=pl.CostEstimate(flops=30 * band * width, bytes_accessed=40 * band * width, transcendentals=0),
        name="defect",
    )(here, jnp.asarray(WEIGHTS), x, mult, obs, mask, x1, plus, minus)


def resid_kernel(bands, first, here_ref, table, base_ref, *refs):
    weight = weight_of(here_ref, table)
    terms, outs = refs[:-bands], refs[-bands:]
    columns = outs[0].shape[1]
    for shift in range(bands):
        target = lax.rem(here_ref[0] + shift, bands)
        at = pl.ds(pl.multiple_of(target * columns, columns), columns)
        value = base_ref[:, at]
        for number, term in enumerate(terms):
            value = value - weight(first + number) * term[:, at]
        outs[shift][...] = value


def resid_blocks(here, bands, first, base, terms):
    band, half = base.shape
    columns = half // bands
    return pl.pallas_call(
        functools.partial(resid_kernel, bands, first),
        out_shape=[jax.ShapeDtypeStruct((band, columns), jnp.float32)] * bands,
        in_specs=[SMEM, SMEM] + [VMEM] * (1 + len(terms)),
        out_specs=[VMEM] * bands,
        compiler_params=LIMIT,
        cost_estimate=pl.CostEstimate(flops=8 * band * half, bytes_accessed=24 * band * half, transcendentals=0),
        name="resid_blocks",
    )(here, jnp.asarray(WEIGHTS), base, *terms)


def lat_kernel(bands, here_ref, *refs):
    blocks, (ehi, elo, ohi, olo) = refs[:bands], refs[bands:bands + 4]
    outs, (gathered, mixed) = refs[bands + 4:2 * bands + 4], refs[2 * bands + 4:]
    here = here_ref[0]
    pairs = bands // 2
    band, columns = blocks[0].shape
    for shift in range(pairs):
        source = lax.rem(here - shift + bands, bands)
        rows = pl.ds(pl.multiple_of(lax.rem(source, pairs) * band, band), band)
        first, other = blocks[shift][...], blocks[shift + pairs][...]
        sign = jnp.where(source < pairs, 1.0, -1.0)
        for part, value in enumerate((first + other, (first - other) * sign)):
            hi, lo = split(value)
            gathered[part, rows, :columns] = hi
            gathered[part, rows, columns:] = lo
    dot = functools.partial(jnp.dot, preferred_element_type=jnp.float32)
    for part, (hi, lo) in enumerate(((ehi, elo), (ohi, olo))):
        both = dot(hi[...], gathered[part])
        mixed[part] = both[:, :columns] + both[:, columns:] + dot(lo[...], gathered[part, :, :columns])
    for shift in range(bands):
        target = lax.rem(here + shift, bands)
        rows = pl.ds(pl.multiple_of(lax.rem(target, pairs) * band, band), band)
        sign = jnp.where(target < pairs, 1.0, -1.0)
        outs[shift][...] = mixed[0, rows] + sign * mixed[1, rows]


def lat_apply(here, blocks, matrices):
    bands = len(blocks)
    band, columns = blocks[0].shape
    half = matrices[0].shape[0]
    return pl.pallas_call(
        functools.partial(lat_kernel, bands),
        out_shape=[jax.ShapeDtypeStruct((band, columns), jnp.float32)] * bands,
        in_specs=[SMEM] + [VMEM] * (bands + 4),
        out_specs=[VMEM] * bands,
        scratch_shapes=[
            pltpu.VMEM((2, half, 2 * columns), jnp.bfloat16),
            pltpu.VMEM((2, half, columns), jnp.float32),
        ],
        compiler_params=LIMIT,
        cost_estimate=pl.CostEstimate(
            flops=12 * half * half * columns, bytes_accessed=8 * half * half, transcendentals=0
        ),
        name="lat_apply",
    )(here, *blocks, *matrices)


def gather_rows(here, bands, blocks, gathered):
    band, columns = blocks[0].shape
    for shift in range(bands):
        source = lax.rem(here - shift + bands, bands)
        at = pl.ds(pl.multiple_of(source * columns, columns), columns)
        hi, lo = split(blocks[shift][...])
        gathered[:band, at] = hi
        gathered[band:, at] = lo


def lon_product(band, hi, lo, gathered):
    dot = functools.partial(jnp.dot, preferred_element_type=jnp.float32)
    both = dot(gathered[...], hi[...])
    return both[:band] + both[band:] + dot(gathered[:band], lo[...])


def lon_even_kernel(bands, here_ref, *refs):
    blocks, (hi, lo, out, gathered) = refs[:bands], refs[bands:]
    gather_rows(here_ref[0], bands, blocks, gathered)
    out[...] = lon_product(blocks[0].shape[0], hi, lo, gathered)


def lon_odd_kernel(bands, here_ref, *refs):
    blocks, (hi, lo, even, field, out, gathered) = refs[:bands], refs[bands:]
    gather_rows(here_ref[0], bands, blocks, gathered)
    half = hi.shape[0]
    odd = lon_product(blocks[0].shape[0], hi, lo, gathered)
    out[:, :half] = field[:, :half] + 0.5 * (even[...] + odd)
    out[:, half:] = field[:, half:] + 0.5 * (even[...] - odd)


def lon_apply(here, blocks, matrices, extra=()):
    bands = len(blocks)
    band, _ = blocks[0].shape
    half = matrices[0].shape[0]
    return pl.pallas_call(
        functools.partial(lon_odd_kernel if extra else lon_even_kernel, bands),
        out_shape=jax.ShapeDtypeStruct((band, 2 * half if extra else half), jnp.float32),
        in_specs=[SMEM] + [VMEM] * (bands + 2 + len(extra)),
        out_specs=VMEM,
        scratch_shapes=[pltpu.VMEM((2 * band, half), jnp.bfloat16)],
        compiler_params=LIMIT,
        cost_estimate=pl.CostEstimate(
            flops=6 * band * half * half, bytes_accessed=4 * half * half, transcendentals=0
        ),
        name="lon_apply",
    )(here, *blocks, *matrices, *extra)


def mix_kernel(here_ref, table, near_ref, side_ref, step_ref, second_ref, far_ref, cross_ref):
    weight = weight_of(here_ref, table)
    for at in range(0, near_ref.shape[0], ROWS):
        rows = slice(at, at + ROWS)
        far_ref[rows] = near_ref[rows] + weight(ONWARD) * step_ref[rows]
        cross_ref[rows] = weight(SECOND) * second_ref[rows] + weight(SIDE) * side_ref[rows]


def mix(here, near, side, step_plus, second):
    shape = jax.ShapeDtypeStruct(near.shape, jnp.float32)
    return pl.pallas_call(
        mix_kernel,
        out_shape=[shape] * 2,
        in_specs=[SMEM] * 2 + [VMEM] * 4,
        out_specs=[VMEM] * 2,
        compiler_params=LIMIT,
        cost_estimate=pl.CostEstimate(flops=5 * near.size, bytes_accessed=24 * near.size, transcendentals=0),
        name="mix",
    )(here, jnp.asarray(WEIGHTS), near, side, step_plus, second)


def multiplier_kernel(here_ref, table, x_ref, mult_ref, plus_ref, minus_ref, near_ref, cross_ref, out_ref):
    weight = weight_of(here_ref, table)
    half = x_ref.shape[1] // 2
    known = weight(KNOWN)
    for at in range(0, x_ref.shape[0], ROWS):
        rows = slice(at, at + ROWS)
        plus = plus_ref[rows] + known * (cross_ref[rows] - near_ref[rows])
        minus = minus_ref[rows]
        for cols, end in ((slice(0, half), plus + minus), (slice(half, 2 * half), plus - minus)):
            out_ref[rows, cols] = mult_ref[rows, cols] + weight(OWN) * x_ref[rows, cols] - 0.5 * end


def new_multipliers(here, x, mult, plus, minus, near, cross):
    band, width = x.shape
    rows = 4 * ROWS
    whole = pl.BlockSpec((rows, width), lambda i: (i, 0))
    part = pl.BlockSpec((rows, width // 2), lambda i: (i, 0))
    return pl.pallas_call(
        multiplier_kernel,
        grid=(band // rows,),
        out_shape=jax.ShapeDtypeStruct((band, width), jnp.float32),
        in_specs=[SMEM] * 2 + [whole] * 2 + [part] * 4,
        out_specs=whole,
        compiler_params=LIMIT,
        cost_estimate=pl.CostEstimate(flops=6 * band * width, bytes_accessed=20 * band * width, transcendentals=0),
        name="new_multipliers",
    )(here, jnp.asarray(WEIGHTS), x, mult, plus, minus, near, cross)


def exchange(blocks):
    bands = len(blocks)
    moved = [blocks[0]]
    for shift in range(1, bands):
        route = [(source, (source + shift) % bands) for source in range(bands)]
        moved.append(lax.ppermute(blocks[shift], "lat", route))
    return moved


WEIGHTS = np.array([
    [0.0, 1.0, -1.0, 1.0, 0.5, 1.0, 0.0, 0.0, 0.0, 0.0, 0.0, 0.0, 0.0, 0.0],
    [0.5, 1 / 2, 1.0, 0.0, 1.0, 0.0, 0.0, 0.0, 0.0, 1.0, 0.0, 0.0, 1.0, 0.5],
    [0.5, 1 / 3, 1.0, 0.0, 0.0, 1.0, 1 / 3, 0.0, 1.0, 0.0, 0.5, 1.0, 0.0, 0.0],
    [0.5, 1 / 4, 1.0, 0.0, 0.0, 0.0, 1.0, 1.0, 1 / 3, 0.0, 0.0, 1.0, 1 / 3, 0.0],
], np.float32)
OWN, SHARE, SIGN, FIRST, ONWARD, SECOND, SIDE, EVEN, ODD, KNOWN = 0, 1, 2, 3, 4, 5, 6, 7, 10, 13


def per_device(
    state, multipliers, observations, obs_mask, speed, drift, kappa, lat_spectrum, lon_spectrum
):
    bands, windows = lax.axis_size("lat"), lax.axis_size("win")
    band, nlon = state.shape[2:]
    columns = nlon // 2 // bands
    if windows != 4 or state.shape[1] != 1 or bands % 2 or band % LANES or columns % LANES:
        return per_device_any(
            state, multipliers, observations, obs_mask, speed, drift, kappa, lat_spectrum, lon_spectrum
        )
    return per_device_hops(
        state, multipliers, observations, obs_mask, speed, drift, kappa, lat_spectrum, lon_spectrum
    )


def per_device_hops(
    state, multipliers, observations, obs_mask, speed, drift, kappa, lat_spectrum, lon_spectrum
):
    bands = lax.axis_size("lat")
    here = jnp.stack([lax.axis_index("lat"), lax.axis_index("win")]).astype(jnp.int32)
    x, mult = state[0, 0], multipliers[0, 0]
    edges = (
        lax.ppermute(x[-2:], "lat", [(i, i + 1) for i in range(bands - 1)]),
        lax.ppermute(x[:2], "lat", [(i + 1, i) for i in range(bands - 1)]),
    )
    x1, plus, minus, near, side = forecast(here, bands, (speed, drift, kappa), x, mult, edges)
    near = lax.ppermute(near, "win", [(0, 1), (1, 0), (2, 3)])
    side = lax.ppermute(side, "win", [(0, 2), (1, 3)])
    base_plus, base_minus, step_plus, second, third = defect(
        here, x, mult, observations[0, :, 0], obs_mask[0], x1, plus, minus
    )
    lat_matrices, step_plus, second = lax.optimization_barrier((build(lat_spectrum), step_plus, second))
    far, cross = mix(here, near, side, step_plus, second)
    far = lax.ppermute(far, "win", [(0, 2), (1, 3)])
    cross = lax.ppermute(cross, "win", [(0, 1), (2, 3), (3, 2)])
    even = list(resid_blocks(here, bands, EVEN, base_plus, (near, far, cross)))
    lon_matrices, third, even[0] = lax.optimization_barrier((build(lon_spectrum), third, even[0]))
    third = lax.ppermute(third, "win", [(0, 1), (1, 3)])
    odd = resid_blocks(here, bands, ODD, base_minus, (side, cross, third))
    plus = lax.ppermute(plus, "win", [(1, 2), (2, 3)])
    minus = lax.ppermute(minus, "win", [(0, 1), (1, 2), (2, 3)])
    even, odd = exchange(even), exchange(odd)
    even = exchange(lat_apply(here, even, lat_matrices))
    odd = exchange(lat_apply(here, odd, lat_matrices))
    even = lon_apply(here, even, lon_matrices[:2])
    field = lon_apply(here, odd, lon_matrices[2:], (even, x))
    lam = new_multipliers(here, x, mult, plus, minus, near, cross)
    return (field[None, None], lam[None, None])


def solution(mesh):
    return jax.shard_map(
        per_device,
        mesh=mesh,
        in_specs=(
            P("win", None, "lat", None),
            P("win", None, "lat", None),
            P("win", None, None, "lat", None),
            P("win", None, "lat", None),
            P(),
            P(),
            P(),
            P(),
            P(),
        ),
        out_specs=(P("win", None, "lat", None), P("win", None, "lat", None)),
        check_vma=False,
    )
```

profile of v0, /device:TPU:0, one launch (start us, length us, event | category | flops | bytes accessed | tf_op | source)
XLA Modules:
  0.0 124.8 jit_solution(2977741422827684630)
XLA Ops:
  0.6 0.9 slice_bitcast_fusion
  1.5 1.3 %collective-permute-start.1 = (f32[2,2048]{1,0:T(2,128)S(1)}, f32[2,2048]{1,0:T(2,128)S(1)}, u32[]{:S(2)}, u32[]{:S(2)}) collective-permute-start(f32[2,2048]{1,0:T(2,128)S(1)} %get-tuple-element.140), channel_id=1, source_target_pairs={{1,0},{2,1},{3,2},{4,3},{5,4},{6,5},{7,6},{9,8},{10,9},{11,10},{12... | collective-permute-start | bytes 49160 | tf_op jit(solution)/shard_map/ppermute | solution.py:583
  2.8 3.0 %collective-permute-start = (f32[2,2048]{1,0:T(2,128)S(1)}, f32[2,2048]{1,0:T(2,128)S(1)}, u32[]{:S(2)}, u32[]{:S(2)}) collective-permute-start(f32[2,2048]{1,0:T(2,128)S(1)} %get-tuple-element.141), channel_id=1, source_target_pairs={{0,1},{1,2},{2,3},{3,4},{4,5},{5,6},{6,7},{8,9},{9,10},{10,11},{11... | collective-permute-start | bytes 49160 | tf_op jit(solution)/shard_map/ppermute | solution.py:582
  5.9 0.1 pad_add_fusion.here_ref
  7.9 1.2 copy-done
  9.1 1.2 copy-done.2
  10.3 0.7 copy-done.8
  11.0 3.0 %forecast.1 = (f32[128,2048]{1,0:T(8,128)S(1)}, f32[128,1024]{1,0:T(8,128)S(1)}, f32[128,1024]{1,0:T(8,128)S(1)}, f32[128,1024]{1,0:T(8,128)S(1)}, f32[128,1024]{1,0:T(8,128)S(1)}) custom-call(s32[2]{0:T(128)S(1)} %pad_add_fusion.here_ref, f32[4,14]{1,0:T(4,128)S(1)} %copy-done.8, f32[1]{0:T(128)S(6)} %copy.34.speed, f32[1]{0:T(128)S(6)} %copy.35.drift, ...), custom_call_target="tpu_custom_call" | custom-call | flops 10485760 | bytes 5242880 | tf_op jit(solution)/shard_map/forecast/pallas_call | solution.py:300
  14.2 1.8 %edges.1 = (f32[128,2048]{1,0:T(8,128)S(1)}, f32[128,1024]{1,0:T(8,128)S(1)}, f32[128,1024]{1,0:T(8,128)S(1)}, f32[128,1024]{1,0:T(8,128)S(1)}, f32[128,1024]{1,0:T(8,128)S(1)}) custom-call(s32[2]{0:T(128)S(1)} %pad_add_fusion.here_ref, f32[4,14]{1,0:T(4,128)S(1)} %copy-done.8, ...), custom_call_target="tpu_custom_call", output_to_operand_aliasing={{0}: (9, {}), {1}: (10, {}), {2}: (11, {}), {3}: (12, {}), ... | custom-call | flops 2048000 | bytes 819200 | tf_op jit(solution)/shard_map/edges/pallas_call | solution.py:310
  16.0 4.9 %collective-permute-start.2 = (f32[128,1024]{1,0:T(8,128)S(1)}, f32[128,1024]{1,0:T(8,128)S(1)}, u32[]{:S(2)}, u32[]{:S(2)}) collective-permute-start(f32[128,1024]{1,0:T(8,128)S(1)} %get-tuple-element.80), channel_id=1, source_target_pairs={{0,16},{8,24},{1,17},{9,25},{2,18},{10,26},{3,19},{11,27},{4,20},{... | collective-permute-start | bytes 1572872 | tf_op jit(solution)/shard_map/ppermute | solution.py:587
  21.0 3.4 %collective-permute-start.3 = (f32[128,1024]{1,0:T(8,128)S(1)}, f32[128,1024]{1,0:T(8,128)S(1)}, u32[]{:S(2)}, u32[]{:S(2)}) collective-permute-start(f32[128,1024]{1,0:T(8,128)S(1)} %get-tuple-element.81), channel_id=1, source_target_pairs={{0,8},{8,0},{16,24},{1,9},{9,1},{17,25},{2,10},{10,2},{18,26},{3,1... | collective-permute-start | bytes 1572872 | tf_op jit(solution)/shard_map/ppermute | solution.py:586
  24.4 2.4 %shard_map.221 = (bf16[512,512]{1,0:T(8,128)(2,1)S(1)}, bf16[512,512]{1,0:T(8,128)(2,1)S(1)}, bf16[512,512]{1,0:T(8,128)(2,1)S(1)}, bf16[512,512]{1,0:T(8,128)(2,1)S(1)}) custom-call(f32[1,1024]{1,0:T(1,128)S(1)} %copy-done.18, f32[8,256]{1,0:T(8,128)S(1)} %copy-done.17, f32[128,256]{1,0:T(8,128)S(1)} %copy-done.6, f32[8,128]{1,0:T(8,128)S(1)} %copy-done.21, ...), custom_call_target="tpu_custom_call" | custom-call | flops 4194304 | bytes 2097152 | tf_op jit(solution)/shard_map/pallas_call | solution.py:102
  26.9 1.6 %defect.1 = (f32[128,1024]{1,0:T(8,128)S(1)}, f32[128,1024]{1,0:T(8,128)S(1)}, f32[128,1024]{1,0:T(8,128)S(1)}, f32[128,1024]{1,0:T(8,128)S(1)}, f32[128,1024]{1,0:T(8,128)S(1)}) custom-call(s32[2]{0:T(128)S(1)} %pad_add_fusion.here_ref, f32[4,14]{1,0:T(4,128)S(1)} %copy-done.9, f32[128,2048]{1,0:T(8,128)S(1)} %bitcast.14, f32[128,2048]{1,0:T(8,128)S(1)} %bitcast.19, ...), custom_call_target="tpu_custom_call" | custom-call | flops 7864320 | bytes 10485760 | tf_op jit(solution)/shard_map/defect/pallas_call | solution.py:357
  28.6 4.4 %collective-permute-done.2.side_ref.refs_0_ = f32[128,1024]{1,0:T(8,128)S(1)} collective-permute-done((f32[128,1024]{1,0:T(8,128)S(1)}, f32[128,1024]{1,0:T(8,128)S(1)}, u32[]{:S(2)}, u32[]{:S(2)}) %collective-permute-start.2) | collective-permute-done | bytes 524320 | tf_op jit(solution)/shard_map/ppermute | solution.py:587
  33.0 4.6 %collective-permute-done.3.near_ref.refs_0_ = f32[128,1024]{1,0:T(8,128)S(1)} collective-permute-done((f32[128,1024]{1,0:T(8,128)S(1)}, f32[128,1024]{1,0:T(8,128)S(1)}, u32[]{:S(2)}, u32[]{:S(2)}) %collective-permute-start.3) | collective-permute-done | bytes 524320 | tf_op jit(solution)/shard_map/ppermute | solution.py:586
  37.6 0.7 mix.1
  38.3 3.4 %collective-permute-start.4 = (f32[128,1024]{1,0:T(8,128)S(1)}, f32[128,1024]{1,0:T(8,128)S(1)}, u32[]{:S(2)}, u32[]{:S(2)}) collective-permute-start(f32[128,1024]{1,0:T(8,128)S(1)} %get-tuple-element.90), channel_id=1, source_target_pairs={{0,8},{16,24},{24,16},{1,9},{17,25},{25,17},{2,10},{18,26},{26,18}... | collective-permute-start | bytes 1572872 | tf_op jit(solution)/shard_map/ppermute | solution.py:594
  41.7 1.3 %collective-permute-start.5 = (f32[128,1024]{1,0:T(8,128)S(1)}, f32[128,1024]{1,0:T(8,128)S(1)}, u32[]{:S(2)}, u32[]{:S(2)}) collective-permute-start(f32[128,1024]{1,0:T(8,128)S(1)} %get-tuple-element.97), channel_id=1, source_target_pairs={{0,16},{8,24},{1,17},{9,25},{2,18},{10,26},{3,19},{11,27},{4,20},{... | collective-permute-start | bytes 1572872 | tf_op jit(solution)/shard_map/ppermute | solution.py:593
  43.1 4.8 %shard_map.222 = (bf16[1024,1024]{1,0:T(8,128)(2,1)S(1)}, bf16[1024,1024]{1,0:T(8,128)(2,1)S(1)}, bf16[1024,1024]{1,0:T(8,128)(2,1)S(1)}, bf16[1024,1024]{1,0:T(8,128)(2,1)S(1)}) custom-call(f32[1,2048]{1,0:T(1,128)S(1)} %copy-done.12, f32[16,256]{1,0:T(8,128)S(1)} %copy-done.11, f32[128,256]{1,0:T(8,128)S(1)} %copy-done.7, f32[16,128]{1,0:T(8,128)S(1)} %copy-done.15, ...), custom_call_target="tpu_custom_call" | custom-call | flops 16777216 | bytes 8388608 | tf_op jit(solution)/shard_map/pallas_call | solution.py:102
  47.9 0.7 collective-permute-start.35
  48.6 4.5 %collective-permute-done.4.refs_2_.refs_1_.cross_ref = f32[128,1024]{1,0:T(8,128)S(1)} collective-permute-done((f32[128,1024]{1,0:T(8,128)S(1)}, f32[128,1024]{1,0:T(8,128)S(1)}, u32[]{:S(2)}, u32[]{:S(2)}) %collective-permute-start.4) | collective-permute-done | bytes 524320 | tf_op jit(solution)/shard_map/ppermute | solution.py:594
  53.1 12.6 %collective-permute-done.5.refs_1_ = f32[128,1024]{1,0:T(8,128)S(1)} collective-permute-done((f32[128,1024]{1,0:T(8,128)S(1)}, f32[128,1024]{1,0:T(8,128)S(1)}, u32[]{:S(2)}, u32[]{:S(2)}) %collective-permute-start.5) | collective-permute-done | bytes 524320 | tf_op jit(solution)/shard_map/ppermute | solution.py:593
  65.7 0.8 resid_blocks.2
  66.5 1.3 %collective-permute-start.6 = (f32[128,1024]{1,0:T(8,128)S(1)}, f32[128,1024]{1,0:T(8,128)S(1)}, u32[]{:S(2)}, u32[]{:S(2)}) collective-permute-start(f32[128,1024]{1,0:T(8,128)S(1)} %get-tuple-element.99), channel_id=1, source_target_pairs={{0,8},{8,24},{1,9},{9,25},{2,10},{10,26},{3,11},{11,27},{4,12},{12... | collective-permute-start | bytes 1572872 | tf_op jit(solution)/shard_map/ppermute | solution.py:597
  67.8 1.3 %collective-permute-start.36 = (f32[128,1024]{1,0:T(8,128)S(1)}, f32[128,1024]{1,0:T(8,128)S(1)}, u32[]{:S(2)}, u32[]{:S(2)}) collective-permute-start(f32[128,1024]{1,0:T(8,128)S(1)} %get-tuple-element.78.minus_ref), channel_id=1, source_target_pairs={{0,8},{8,16},{16,24},{1,9},{9,17},{17,25},{2,10},{10,18},{18,26},{... | collective-permute-start | bytes 1572872 | tf_op jit(solution)/shard_map/ppermute | solution.py:600
  69.2 0.1 collective-permute-start.21
  69.2 1.6 %collective-permute-start.22 = (f32[128,128]{1,0:T(8,128)S(1)}, f32[128,128]{1,0:T(8,128)S(1)}, u32[]{:S(2)}, u32[]{:S(2)}) collective-permute-start(f32[128,128]{1,0:T(8,128)S(1)} %get-tuple-element.124), channel_id=1, source_target_pairs={{0,2},{1,3},{2,4},{3,5},{4,6},{5,7},{6,0},{7,1},{8,10},{9,11},{10,... | collective-permute-start | bytes 196616 | tf_op jit(solution)/shard_map/ppermute | solution.py:547
  70.9 1.2 collective-permute-start.23
  72.1 2.7 %collective-permute-done.21.refs_1_ = f32[128,128]{1,0:T(8,128)S(1)} collective-permute-done((f32[128,128]{1,0:T(8,128)S(1)}, f32[128,128]{1,0:T(8,128)S(1)}, u32[]{:S(2)}, u32[]{:S(2)}) %collective-permute-start.21) | collective-permute-done | bytes 65568 | tf_op jit(solution)/shard_map/ppermute | solution.py:547
  74.8 0.8 collective-permute-start.24
  75.6 0.0 collective-permute-done.22.refs_2_
  75.6 1.0 collective-permute-start.25
  76.6 3.5 %collective-permute-done.6.refs_2_ = f32[128,1024]{1,0:T(8,128)S(1)} collective-permute-done((f32[128,1024]{1,0:T(8,128)S(1)}, f32[128,1024]{1,0:T(8,128)S(1)}, u32[]{:S(2)}, u32[]{:S(2)}) %collective-permute-start.6) | collective-permute-done | bytes 524320 | tf_op jit(solution)/shard_map/ppermute | solution.py:597
  80.1 0.2 collective-permute-start.26
  80.3 0.8 resid_blocks.3
  81.2 0.4 collective-permute-start.27
  81.5 0.5 collective-permute-start.7
  82.1 1.7 %collective-permute-start.8 = (f32[128,128]{1,0:T(8,128)S(1)}, f32[128,128]{1,0:T(8,128)S(1)}, u32[]{:S(2)}, u32[]{:S(2)}) collective-permute-start(f32[128,128]{1,0:T(8,128)S(1)} %get-tuple-element.102), channel_id=1, source_target_pairs={{0,2},{1,3},{2,4},{3,5},{4,6},{5,7},{6,0},{7,1},{8,10},{9,11},{10,... | collective-permute-start | bytes 196616 | tf_op jit(solution)/shard_map/ppermute | solution.py:547
  83.8 0.6 collective-permute-done.26.refs_6_
  84.4 1.4 %collective-permute-start.9 = (f32[128,128]{1,0:T(8,128)S(1)}, f32[128,128]{1,0:T(8,128)S(1)}, u32[]{:S(2)}, u32[]{:S(2)}) collective-permute-start(f32[128,128]{1,0:T(8,128)S(1)} %get-tuple-element.103), channel_id=1, source_target_pairs={{0,3},{1,4},{2,5},{3,6},{4,7},{5,0},{6,1},{7,2},{8,11},{9,12},{10,... | collective-permute-start | bytes 196616 | tf_op jit(solution)/shard_map/ppermute | solution.py:547
  85.7 1.2 collective-permute-start.10
  87.0 0.7 collective-permute-done.7.refs_1_
  87.7 1.7 %collective-permute-start.11 = (f32[128,128]{1,0:T(8,128)S(1)}, f32[128,128]{1,0:T(8,128)S(1)}, u32[]{:S(2)}, u32[]{:S(2)}) collective-permute-start(f32[128,128]{1,0:T(8,128)S(1)} %get-tuple-element.105), channel_id=1, source_target_pairs={{0,5},{1,6},{2,7},{3,0},{4,1},{5,2},{6,3},{7,4},{8,13},{9,14},{10,... | collective-permute-start | bytes 196616 | tf_op jit(solution)/shard_map/ppermute | solution.py:547
  89.3 1.3 %collective-permute-start.12 = (f32[128,128]{1,0:T(8,128)S(1)}, f32[128,128]{1,0:T(8,128)S(1)}, u32[]{:S(2)}, u32[]{:S(2)}) collective-permute-start(f32[128,128]{1,0:T(8,128)S(1)} %get-tuple-element.106), channel_id=1, source_target_pairs={{0,6},{1,7},{2,0},{3,1},{4,2},{5,3},{6,4},{7,5},{8,14},{9,15},{10,... | collective-permute-start | bytes 196616 | tf_op jit(solution)/shard_map/ppermute | solution.py:547
  90.7 3.5 %collective-permute-done.9.refs_3_ = f32[128,128]{1,0:T(8,128)S(1)} collective-permute-done((f32[128,128]{1,0:T(8,128)S(1)}, f32[128,128]{1,0:T(8,128)S(1)}, u32[]{:S(2)}, u32[]{:S(2)}) %collective-permute-start.9) | collective-permute-done | bytes 65568 | tf_op jit(solution)/shard_map/ppermute | solution.py:547
  94.2 1.4 %lat_apply.3 = (f32[128,128]{1,0:T(8,128)S(1)}, f32[128,128]{1,0:T(8,128)S(1)}, f32[128,128]{1,0:T(8,128)S(1)}, f32[128,128]{1,0:T(8,128)S(1)}, f32[128,128]{1,0...) custom-call(s32[2]{0:T(128)S(1)} %pad_add_fusion.here_ref, ...), custom_call_target="tpu_custom_call" | custom-call | flops 402653184 | bytes 2097152 | tf_op jit(solution)/shard_map/lat_apply/pallas_call | solution.py:426
  95.6 0.6 collective-permute-start.28
  96.2 1.3 %collective-permute-start.29 = (f32[128,128]{1,0:T(8,128)S(1)}, f32[128,128]{1,0:T(8,128)S(1)}, u32[]{:S(2)}, u32[]{:S(2)}) collective-permute-start(f32[128,128]{1,0:T(8,128)S(1)} %get-tuple-element.132), channel_id=1, source_target_pairs={{0,2},{1,3},{2,4},{3,5},{4,6},{5,7},{6,0},{7,1},{8,10},{9,11},{10,... | collective-permute-start | bytes 196616 | tf_op jit(solution)/shard_map/ppermute | solution.py:547
  97.5 1.3 %collective-permute-start.30 = (f32[128,128]{1,0:T(8,128)S(1)}, f32[128,128]{1,0:T(8,128)S(1)}, u32[]{:S(2)}, u32[]{:S(2)}) collective-permute-start(f32[128,128]{1,0:T(8,128)S(1)} %get-tuple-element.133), channel_id=1, source_target_pairs={{0,3},{1,4},{2,5},{3,6},{4,7},{5,0},{6,1},{7,2},{8,11},{9,12},{10,... | collective-permute-start | bytes 196616 | tf_op jit(solution)/shard_map/ppermute | solution.py:547
  98.7 1.3 %collective-permute-start.31 = (f32[128,128]{1,0:T(8,128)S(1)}, f32[128,128]{1,0:T(8,128)S(1)}, u32[]{:S(2)}, u32[]{:S(2)}) collective-permute-start(f32[128,128]{1,0:T(8,128)S(1)} %get-tuple-element.134), channel_id=1, source_target_pairs={{0,4},{1,5},{2,6},{3,7},{4,0},{5,1},{6,2},{7,3},{8,12},{9,13},{10,... | collective-permute-start | bytes 196616 | tf_op jit(solution)/shard_map/ppermute | solution.py:547
  100.0 1.4 %lat_apply.2 = (f32[128,128]{1,0:T(8,128)S(1)}, f32[128,128]{1,0:T(8,128)S(1)}, f32[128,128]{1,0:T(8,128)S(1)}, f32[128,128]{1,0:T(8,128)S(1)}, f32[128,128]{1,0...) custom-call(s32[2]{0:T(128)S(1)} %pad_add_fusion.here_ref, ...), custom_call_target="tpu_custom_call" | custom-call | flops 402653184 | bytes 2097152 | tf_op jit(solution)/shard_map/lat_apply/pallas_call | solution.py:426
  101.5 1.2 collective-permute-start.32
  102.7 1.5 %collective-permute-start.33 = (f32[128,128]{1,0:T(8,128)S(1)}, f32[128,128]{1,0:T(8,128)S(1)}, u32[]{:S(2)}, u32[]{:S(2)}) collective-permute-start(f32[128,128]{1,0:T(8,128)S(1)} %get-tuple-element.136), channel_id=1, source_target_pairs={{0,6},{1,7},{2,0},{3,1},{4,2},{5,3},{6,4},{7,5},{8,14},{9,15},{10,... | collective-permute-start | bytes 196616 | tf_op jit(solution)/shard_map/ppermute | solution.py:547
  104.2 0.3 collective-permute-start.34
  104.5 2.9 %collective-permute-done.30.refs_3_ = f32[128,128]{1,0:T(8,128)S(1)} collective-permute-done((f32[128,128]{1,0:T(8,128)S(1)}, f32[128,128]{1,0:T(8,128)S(1)}, u32[]{:S(2)}, u32[]{:S(2)}) %collective-permute-start.30) | collective-permute-done | bytes 65568 | tf_op jit(solution)/shard_map/ppermute | solution.py:547
  107.5 0.2 collective-permute-done.31.refs_4_
  107.7 1.1 collective-permute-start.15
  108.8 2.2 %new_multipliers.1 = f32[128,2048]{1,0:T(8,128)} custom-call(s32[2]{0:T(128)S(1)} %pad_add_fusion.here_ref, f32[4,14]{1,0:T(4,128)S(1)} %copy-done.9, f32[128,2048]{1,0:T(8,128)S(1)} %bitcast.15, f32[128,2048]{1,0:T(8,128)S(1)} %bitcast.20, f32[128,1024]{1,0:T(8,128)S(1)} %collective-permute-done.35.plus_ref, ...), custom_call_target="tpu_custom_call" | custom-call | flops 1572864 | bytes 5242880 | tf_op jit(solution)/shard_map/new_multipliers/pallas_call | solution.py:530
  111.0 3.7 %collective-permute-start.17 = (f32[128,128]{1,0:T(8,128)S(1)}, f32[128,128]{1,0:T(8,128)S(1)}, u32[]{:S(2)}, u32[]{:S(2)}) collective-permute-start(f32[128,128]{1,0:T(8,128)S(1)} %get-tuple-element.116), channel_id=1, source_target_pairs={{0,4},{1,5},{2,6},{3,7},{4,0},{5,1},{6,2},{7,3},{8,12},{9,13},{10,... | collective-permute-start | bytes 196616 | tf_op jit(solution)/shard_map/ppermute | solution.py:547
  114.7 2.3 %collective-permute-start.18 = (f32[128,128]{1,0:T(8,128)S(1)}, f32[128,128]{1,0:T(8,128)S(1)}, u32[]{:S(2)}, u32[]{:S(2)}) collective-permute-start(f32[128,128]{1,0:T(8,128)S(1)} %get-tuple-element.117), channel_id=1, source_target_pairs={{0,5},{1,6},{2,7},{3,0},{4,1},{5,2},{6,3},{7,4},{8,13},{9,14},{10,... | collective-permute-start | bytes 196616 | tf_op jit(solution)/shard_map/ppermute | solution.py:547
  117.0 1.2 collective-permute-start.20
  118.3 1.7 %lon_apply.2.refs_10_ = f32[128,1024]{1,0:T(8,128)S(1)} custom-call(s32[2]{0:T(128)S(1)} %pad_add_fusion.here_ref, f32[128,128]{1,0:T(8,128)S(1)} %get-tuple-element.130.refs_0_, f32[128,128]{1,0:T(8,128)S(1)} %collective-permute-done.28.refs_1_, f32[128,128]{1,0:T(8,128)S(1)} %collective-permute-done.29.refs_2_, ...), custom_call_target="tpu_custom_call" | custom-call | flops 805306368 | bytes 4194304 | tf_op jit(solution)/shard_map/lon_apply/pallas_call | solution.py:478
  120.0 2.2 %collective-permute-done.19.refs_6_ = f32[128,128]{1,0:T(8,128)S(1)} collective-permute-done((f32[128,128]{1,0:T(8,128)S(1)}, f32[128,128]{1,0:T(8,128)S(1)}, u32[]{:S(2)}, u32[]{:S(2)}) %collective-permute-start.19) | collective-permute-done | bytes 65568 | tf_op jit(solution)/shard_map/ppermute | solution.py:547
  122.1 2.7 %lon_apply.3 = f32[128,2048]{1,0:T(8,128)} custom-call(s32[2]{0:T(128)S(1)} %pad_add_fusion.here_ref, f32[128,128]{1,0:T(8,128)S(1)} %get-tuple-element.112.refs_0_, f32[128,128]{1,0:T(8,128)S(1)} %collective-permute-done.14.refs_1_, f32[128,128]{1,0:T(8,128)S(1)} %collective-permute-done.15.refs_2_, f32[128,128]{1,0:T(8,128)S(1)} %collective-permute-done.16.refs_3_, ...), custom_call_target="tpu_custom_call" | custom-call | flops 805306368 | bytes 4194304 | tf_op jit(solution)/shard_map/lon_apply/pallas_call | solution.py:478
  (69 shorter events, 0.2 us)
Async XLA Ops:
  1.5 12.5 %collective-permute-start.1 = (f32[2,2048]{1,0:T(2,128)S(1)}, f32[2,2048]{1,0:T(2,128)S(1)}, u32[]{:S(2)}, u32[]{:S(2)}) collective-permute-start(f32[2,2048]{1,0:T(2,128)S(1)} %get-tuple-element.140), channel_id=1, source_target_pairs={{1,0},{2,1},{3,2},{4,3},{5,4},{6,5},{7,6},{9,8},{10,9},{11,10},{12... | collective-permute-start | bytes 49160 | tf_op jit(solution)/shard_map/ppermute | solution.py:583
  2.8 11.2 %collective-permute-start = (f32[2,2048]{1,0:T(2,128)S(1)}, f32[2,2048]{1,0:T(2,128)S(1)}, u32[]{:S(2)}, u32[]{:S(2)}) collective-permute-start(f32[2,2048]{1,0:T(2,128)S(1)} %get-tuple-element.141), channel_id=1, source_target_pairs={{0,1},{1,2},{2,3},{3,4},{4,5},{5,6},{6,7},{8,9},{9,10},{10,11},{11... | collective-permute-start | bytes 49160 | tf_op jit(solution)/shard_map/ppermute | solution.py:582
  7.9 1.2 copy-start
  9.1 1.2 copy-start.2
  10.3 0.7 copy-start.8
  11.0 15.8 %copy-start.5 = (s32[1,2,128,2048]{3,2,1,0:T(8,128)S(1)}, s32[1,2,128,2048]{3,2,1,0:T(8,128)}, u32[]{:S(2)}) copy-start(s32[1,2,128,2048]{3,2,1,0:T(8,128)} %param.25) | copy-start | bytes 6291460
  14.1 10.3 %copy-start.6 = (f32[128,256]{1,0:T(8,128)S(1)}, f32[128,256]{1,0:T(8,128)}, u32[]{:S(2)}) copy-start(f32[128,256]{1,0:T(8,128)} %constant.36.clone.middle_ref) | copy-start | bytes 393220
  14.1 10.3 %copy-start.16 = (f32[8,256]{1,0:T(8,128)S(1)}, f32[8,256]{1,0:T(8,128)}, u32[]{:S(2)}) copy-start(f32[8,256]{1,0:T(8,128)} %constant.38.clone.twist_ref) | copy-start | bytes 24580
  14.1 10.3 %copy-start.17 = (f32[8,256]{1,0:T(8,128)S(1)}, f32[8,256]{1,0:T(8,128)}, u32[]{:S(2)}) copy-start(f32[8,256]{1,0:T(8,128)} %constant.35.clone.inner_ref) | copy-start | bytes 24580
  14.1 10.3 %copy-start.18 = (f32[1,1024]{1,0:T(1,128)S(1)}, f32[1,1024]{1,0:T(1,128)}, u32[]{:S(2)}) copy-start(f32[1,1024]{1,0:T(1,128)} %d_ref.2) | copy-start | bytes 12292
  14.1 10.3 %copy-start.19 = (f32[8,8]{1,0:T(8,128)S(1)}, f32[8,8]{1,0:T(8,128)}, u32[]{:S(2)}) copy-start(f32[8,8]{1,0:T(8,128)} %constant.40.clone.sin_ref) | copy-start | bytes 772
  14.1 10.3 %copy-start.20 = (f32[8,8]{1,0:T(8,128)S(1)}, f32[8,8]{1,0:T(8,128)}, u32[]{:S(2)}) copy-start(f32[8,8]{1,0:T(8,128)} %constant.39.clone.cos_ref) | copy-start | bytes 772
  14.1 10.3 %copy-start.21 = (f32[8,128]{1,0:T(8,128)S(1)}, f32[8,128]{1,0:T(8,128)}, u32[]{:S(2)}) copy-start(f32[8,128]{1,0:T(8,128)} %constant.37.clone.member_ref) | copy-start | bytes 12292
  14.1 12.7 %copy-start.1 = (f32[1,1,128,2048]{3,2,1,0:T(8,128)S(1)}, f32[1,1,128,2048]{3,2,1,0:T(8,128)}, u32[]{:S(2)}) copy-start(f32[1,1,128,2048]{3,2,1,0:T(8,128)} %param.22) | copy-start | bytes 3145732
  14.2 12.7 %copy-start.3 = (f32[1,1,128,2048]{3,2,1,0:T(8,128)S(1)}, f32[1,1,128,2048]{3,2,1,0:T(8,128)}, u32[]{:S(2)}) copy-start(f32[1,1,128,2048]{3,2,1,0:T(8,128)} %param.23) | copy-start | bytes 3145732
  14.2 12.7 %copy-start.4 = (f32[1,2,1,128,2048]{4,3,2,1,0:T(8,128)S(1)}, f32[1,2,1,128,2048]{4,3,2,1,0:T(8,128)}, u32[]{:S(2)}) copy-start(f32[1,2,1,128,2048]{4,3,2,1,0:T(8,128)} %param.24) | copy-start | bytes 6291460
  14.2 12.7 %copy-start.9 = (f32[4,14]{1,0:T(4,128)S(1)}, f32[4,14]{1,0:T(4,128)}, u32[]{:S(2)}) copy-start(f32[4,14]{1,0:T(4,128)} %constant.34.clone.table) | copy-start | bytes 676
  16.0 17.0 %collective-permute-start.2 = (f32[128,1024]{1,0:T(8,128)S(1)}, f32[128,1024]{1,0:T(8,128)S(1)}, u32[]{:S(2)}, u32[]{:S(2)}) collective-permute-start(f32[128,1024]{1,0:T(8,128)S(1)} %get-tuple-element.80), channel_id=1, source_target_pairs={{0,16},{8,24},{1,17},{9,25},{2,18},{10,26},{3,19},{11,27},{4,20},{... | collective-permute-start | bytes 1572872 | tf_op jit(solution)/shard_map/ppermute | solution.py:587
  21.0 16.6 %collective-permute-start.3 = (f32[128,1024]{1,0:T(8,128)S(1)}, f32[128,1024]{1,0:T(8,128)S(1)}, u32[]{:S(2)}, u32[]{:S(2)}) collective-permute-start(f32[128,1024]{1,0:T(8,128)S(1)} %get-tuple-element.81), channel_id=1, source_target_pairs={{0,8},{8,0},{16,24},{1,9},{9,1},{17,25},{2,10},{10,2},{18,26},{3,1... | collective-permute-start | bytes 1572872 | tf_op jit(solution)/shard_map/ppermute | solution.py:586
  28.5 14.6 %copy-start.7 = (f32[128,256]{1,0:T(8,128)S(1)}, f32[128,256]{1,0:T(8,128)}, u32[]{:S(2)}) copy-start(f32[128,256]{1,0:T(8,128)} %constant.42.clone.middle_ref) | copy-start | bytes 393220
  28.5 14.5 %copy-start.10 = (f32[16,256]{1,0:T(8,128)S(1)}, f32[16,256]{1,0:T(8,128)}, u32[]{:S(2)}) copy-start(f32[16,256]{1,0:T(8,128)} %constant.44.clone.twist_ref) | copy-start | bytes 49156
  28.5 14.5 %copy-start.11 = (f32[16,256]{1,0:T(8,128)S(1)}, f32[16,256]{1,0:T(8,128)}, u32[]{:S(2)}) copy-start(f32[16,256]{1,0:T(8,128)} %constant.41.clone.inner_ref) | copy-start | bytes 49156
  28.6 14.5 %copy-start.12 = (f32[1,2048]{1,0:T(1,128)S(1)}, f32[1,2048]{1,0:T(1,128)}, u32[]{:S(2)}) copy-start(f32[1,2048]{1,0:T(1,128)} %d_ref.3) | copy-start | bytes 24580
  28.6 14.5 %copy-start.13 = (f32[16,16]{1,0:T(8,128)S(1)}, f32[16,16]{1,0:T(8,128)}, u32[]{:S(2)}) copy-start(f32[16,16]{1,0:T(8,128)} %constant.46.clone.sin_ref) | copy-start | bytes 3076
  28.6 14.5 %copy-start.14 = (f32[16,16]{1,0:T(8,128)S(1)}, f32[16,16]{1,0:T(8,128)}, u32[]{:S(2)}) copy-start(f32[16,16]{1,0:T(8,128)} %constant.45.clone.cos_ref) | copy-start | bytes 3076
  28.6 14.5 %copy-start.15 = (f32[16,128]{1,0:T(8,128)S(1)}, f32[16,128]{1,0:T(8,128)}, u32[]{:S(2)}) copy-start(f32[16,128]{1,0:T(8,128)} %constant.43.clone.member_ref) | copy-start | bytes 24580
  38.3 14.8 %collective-permute-start.4 = (f32[128,1024]{1,0:T(8,128)S(1)}, f32[128,1024]{1,0:T(8,128)S(1)}, u32[]{:S(2)}, u32[]{:S(2)}) collective-permute-start(f32[128,1024]{1,0:T(8,128)S(1)} %get-tuple-element.90), channel_id=1, source_target_pairs={{0,8},{16,24},{24,16},{1,9},{17,25},{25,17},{2,10},{18,26},{26,18}... | collective-permute-start | bytes 1572872 | tf_op jit(solution)/shard_map/ppermute | solution.py:594
  41.7 23.9 %collective-permute-start.5 = (f32[128,1024]{1,0:T(8,128)S(1)}, f32[128,1024]{1,0:T(8,128)S(1)}, u32[]{:S(2)}, u32[]{:S(2)}) collective-permute-start(f32[128,1024]{1,0:T(8,128)S(1)} %get-tuple-element.97), channel_id=1, source_target_pairs={{0,16},{8,24},{1,17},{9,25},{2,18},{10,26},{3,19},{11,27},{4,20},{... | collective-permute-start | bytes 1572872 | tf_op jit(solution)/shard_map/ppermute | solution.py:593
  47.9 22.9 %collective-permute-start.35 = (f32[128,1024]{1,0:T(8,128)S(1)}, f32[128,1024]{1,0:T(8,128)S(1)}, u32[]{:S(2)}, u32[]{:S(2)}) collective-permute-start(f32[128,1024]{1,0:T(8,128)S(1)} %get-tuple-element.77.plus_ref), channel_id=1, source_target_pairs={{8,16},{16,24},{9,17},{17,25},{10,18},{18,26},{11,19},{19,27},{12,... | collective-permute-start | bytes 1572872 | tf_op jit(solution)/shard_map/ppermute | solution.py:599
  66.5 13.6 %collective-permute-start.6 = (f32[128,1024]{1,0:T(8,128)S(1)}, f32[128,1024]{1,0:T(8,128)S(1)}, u32[]{:S(2)}, u32[]{:S(2)}) collective-permute-start(f32[128,1024]{1,0:T(8,128)S(1)} %get-tuple-element.99), channel_id=1, source_target_pairs={{0,8},{8,24},{1,9},{9,25},{2,10},{10,26},{3,11},{11,27},{4,12},{12... | collective-permute-start | bytes 1572872 | tf_op jit(solution)/shard_map/ppermute | solution.py:597
  67.8 33.7 %collective-permute-start.36 = (f32[128,1024]{1,0:T(8,128)S(1)}, f32[128,1024]{1,0:T(8,128)S(1)}, u32[]{:S(2)}, u32[]{:S(2)}) collective-permute-start(f32[128,1024]{1,0:T(8,128)S(1)} %get-tuple-element.78.minus_ref), channel_id=1, source_target_pairs={{0,8},{8,16},{16,24},{1,9},{9,17},{17,25},{2,10},{10,18},{18,26},{... | collective-permute-start | bytes 1572872 | tf_op jit(solution)/shard_map/ppermute | solution.py:600
  69.2 5.6 %collective-permute-start.21 = (f32[128,128]{1,0:T(8,128)S(1)}, f32[128,128]{1,0:T(8,128)S(1)}, u32[]{:S(2)}, u32[]{:S(2)}) collective-permute-start(f32[128,128]{1,0:T(8,128)S(1)} %get-tuple-element.123), channel_id=1, source_target_pairs={{0,1},{1,2},{2,3},{3,4},{4,5},{5,6},{6,7},{7,0},{8,9},{9,10},{10,1... | collective-permute-start | bytes 196616 | tf_op jit(solution)/shard_map/ppermute | solution.py:547
  69.2 6.4 %collective-permute-start.22 = (f32[128,128]{1,0:T(8,128)S(1)}, f32[128,128]{1,0:T(8,128)S(1)}, u32[]{:S(2)}, u32[]{:S(2)}) collective-permute-start(f32[128,128]{1,0:T(8,128)S(1)} %get-tuple-element.124), channel_id=1, source_target_pairs={{0,2},{1,3},{2,4},{3,5},{4,6},{5,7},{6,0},{7,1},{8,10},{9,11},{10,... | collective-permute-start | bytes 196616 | tf_op jit(solution)/shard_map/ppermute | solution.py:547
  70.9 10.3 %collective-permute-start.23 = (f32[128,128]{1,0:T(8,128)S(1)}, f32[128,128]{1,0:T(8,128)S(1)}, u32[]{:S(2)}, u32[]{:S(2)}) collective-permute-start(f32[128,128]{1,0:T(8,128)S(1)} %get-tuple-element.125), channel_id=1, source_target_pairs={{0,3},{1,4},{2,5},{3,6},{4,7},{5,0},{6,1},{7,2},{8,11},{9,12},{10,... | collective-permute-start | bytes 196616 | tf_op jit(solution)/shard_map/ppermute | solution.py:547
  74.8 6.8 %collective-permute-start.24 = (f32[128,128]{1,0:T(8,128)S(1)}, f32[128,128]{1,0:T(8,128)S(1)}, u32[]{:S(2)}, u32[]{:S(2)}) collective-permute-start(f32[128,128]{1,0:T(8,128)S(1)} %get-tuple-element.126), channel_id=1, source_target_pairs={{0,4},{1,5},{2,6},{3,7},{4,0},{5,1},{6,2},{7,3},{8,12},{9,13},{10,... | collective-permute-start | bytes 196616 | tf_op jit(solution)/shard_map/ppermute | solution.py:547
  75.6 6.4 %collective-permute-start.25 = (f32[128,128]{1,0:T(8,128)S(1)}, f32[128,128]{1,0:T(8,128)S(1)}, u32[]{:S(2)}, u32[]{:S(2)}) collective-permute-start(f32[128,128]{1,0:T(8,128)S(1)} %get-tuple-element.127), channel_id=1, source_target_pairs={{0,5},{1,6},{2,7},{3,0},{4,1},{5,2},{6,3},{7,4},{8,13},{9,14},{10,... | collective-permute-start | bytes 196616 | tf_op jit(solution)/shard_map/ppermute | solution.py:547
  80.1 4.3 %collective-permute-start.26 = (f32[128,128]{1,0:T(8,128)S(1)}, f32[128,128]{1,0:T(8,128)S(1)}, u32[]{:S(2)}, u32[]{:S(2)}) collective-permute-start(f32[128,128]{1,0:T(8,128)S(1)} %get-tuple-element.128), channel_id=1, source_target_pairs={{0,6},{1,7},{2,0},{3,1},{4,2},{5,3},{6,4},{7,5},{8,14},{9,15},{10,... | collective-permute-start | bytes 196616 | tf_op jit(solution)/shard_map/ppermute | solution.py:547
  81.2 4.6 %collective-permute-start.27 = (f32[128,128]{1,0:T(8,128)S(1)}, f32[128,128]{1,0:T(8,128)S(1)}, u32[]{:S(2)}, u32[]{:S(2)}) collective-permute-start(f32[128,128]{1,0:T(8,128)S(1)} %get-tuple-element.129), channel_id=1, source_target_pairs={{0,7},{1,0},{2,1},{3,2},{4,3},{5,4},{6,5},{7,6},{8,15},{9,8},{10,9... | collective-permute-start | bytes 196616 | tf_op jit(solution)/shard_map/ppermute | solution.py:547
  81.5 6.1 %collective-permute-start.7 = (f32[128,128]{1,0:T(8,128)S(1)}, f32[128,128]{1,0:T(8,128)S(1)}, u32[]{:S(2)}, u32[]{:S(2)}) collective-permute-start(f32[128,128]{1,0:T(8,128)S(1)} %get-tuple-element.101), channel_id=1, source_target_pairs={{0,1},{1,2},{2,3},{3,4},{4,5},{5,6},{6,7},{7,0},{8,9},{9,10},{10,1... | collective-permute-start | bytes 196616 | tf_op jit(solution)/shard_map/ppermute | solution.py:547
  82.1 7.3 %collective-permute-start.8 = (f32[128,128]{1,0:T(8,128)S(1)}, f32[128,128]{1,0:T(8,128)S(1)}, u32[]{:S(2)}, u32[]{:S(2)}) collective-permute-start(f32[128,128]{1,0:T(8,128)S(1)} %get-tuple-element.102), channel_id=1, source_target_pairs={{0,2},{1,3},{2,4},{3,5},{4,6},{5,7},{6,0},{7,1},{8,10},{9,11},{10,... | collective-permute-start | bytes 196616 | tf_op jit(solution)/shard_map/ppermute | solution.py:547
  84.4 9.8 %collective-permute-start.9 = (f32[128,128]{1,0:T(8,128)S(1)}, f32[128,128]{1,0:T(8,128)S(1)}, u32[]{:S(2)}, u32[]{:S(2)}) collective-permute-start(f32[128,128]{1,0:T(8,128)S(1)} %get-tuple-element.103), channel_id=1, source_target_pairs={{0,3},{1,4},{2,5},{3,6},{4,7},{5,0},{6,1},{7,2},{8,11},{9,12},{10,... | collective-permute-start | bytes 196616 | tf_op jit(solution)/shard_map/ppermute | solution.py:547
  85.7 9.9 %collective-permute-start.10 = (f32[128,128]{1,0:T(8,128)S(1)}, f32[128,128]{1,0:T(8,128)S(1)}, u32[]{:S(2)}, u32[]{:S(2)}) collective-permute-start(f32[128,128]{1,0:T(8,128)S(1)} %get-tuple-element.104), channel_id=1, source_target_pairs={{0,4},{1,5},{2,6},{3,7},{4,0},{5,1},{6,2},{7,3},{8,12},{9,13},{10,... | collective-permute-start | bytes 196616 | tf_op jit(solution)/shard_map/ppermute | solution.py:547
  87.7 8.5 %collective-permute-start.11 = (f32[128,128]{1,0:T(8,128)S(1)}, f32[128,128]{1,0:T(8,128)S(1)}, u32[]{:S(2)}, u32[]{:S(2)}) collective-permute-start(f32[128,128]{1,0:T(8,128)S(1)} %get-tuple-element.105), channel_id=1, source_target_pairs={{0,5},{1,6},{2,7},{3,0},{4,1},{5,2},{6,3},{7,4},{8,13},{9,14},{10,... | collective-permute-start | bytes 196616 | tf_op jit(solution)/shard_map/ppermute | solution.py:547
  89.3 8.1 %collective-permute-start.12 = (f32[128,128]{1,0:T(8,128)S(1)}, f32[128,128]{1,0:T(8,128)S(1)}, u32[]{:S(2)}, u32[]{:S(2)}) collective-permute-start(f32[128,128]{1,0:T(8,128)S(1)} %get-tuple-element.106), channel_id=1, source_target_pairs={{0,6},{1,7},{2,0},{3,1},{4,2},{5,3},{6,4},{7,5},{8,14},{9,15},{10,... | collective-permute-start | bytes 196616 | tf_op jit(solution)/shard_map/ppermute | solution.py:547
  94.2 4.6 %collective-permute-start.13 = (f32[128,128]{1,0:T(8,128)S(1)}, f32[128,128]{1,0:T(8,128)S(1)}, u32[]{:S(2)}, u32[]{:S(2)}) collective-permute-start(f32[128,128]{1,0:T(8,128)S(1)} %get-tuple-element.107), channel_id=1, source_target_pairs={{0,7},{1,0},{2,1},{3,2},{4,3},{5,4},{6,5},{7,6},{8,15},{9,8},{10,9... | collective-permute-start | bytes 196616 | tf_op jit(solution)/shard_map/ppermute | solution.py:547
  95.6 7.1 %collective-permute-start.28 = (f32[128,128]{1,0:T(8,128)S(1)}, f32[128,128]{1,0:T(8,128)S(1)}, u32[]{:S(2)}, u32[]{:S(2)}) collective-permute-start(f32[128,128]{1,0:T(8,128)S(1)} %get-tuple-element.131), channel_id=1, source_target_pairs={{0,1},{1,2},{2,3},{3,4},{4,5},{5,6},{6,7},{7,0},{8,9},{9,10},{10,1... | collective-permute-start | bytes 196616 | tf_op jit(solution)/shard_map/ppermute | solution.py:547
  96.2 8.0 %collective-permute-start.29 = (f32[128,128]{1,0:T(8,128)S(1)}, f32[128,128]{1,0:T(8,128)S(1)}, u32[]{:S(2)}, u32[]{:S(2)}) collective-permute-start(f32[128,128]{1,0:T(8,128)S(1)} %get-tuple-element.132), channel_id=1, source_target_pairs={{0,2},{1,3},{2,4},{3,5},{4,6},{5,7},{6,0},{7,1},{8,10},{9,11},{10,... | collective-permute-start | bytes 196616 | tf_op jit(solution)/shard_map/ppermute | solution.py:547
  97.5 10.0 %collective-permute-start.30 = (f32[128,128]{1,0:T(8,128)S(1)}, f32[128,128]{1,0:T(8,128)S(1)}, u32[]{:S(2)}, u32[]{:S(2)}) collective-permute-start(f32[128,128]{1,0:T(8,128)S(1)} %get-tuple-element.133), channel_id=1, source_target_pairs={{0,3},{1,4},{2,5},{3,6},{4,7},{5,0},{6,1},{7,2},{8,11},{9,12},{10,... | collective-permute-start | bytes 196616 | tf_op jit(solution)/shard_map/ppermute | solution.py:547
  98.7 8.9 %collective-permute-start.31 = (f32[128,128]{1,0:T(8,128)S(1)}, f32[128,128]{1,0:T(8,128)S(1)}, u32[]{:S(2)}, u32[]{:S(2)}) collective-permute-start(f32[128,128]{1,0:T(8,128)S(1)} %get-tuple-element.134), channel_id=1, source_target_pairs={{0,4},{1,5},{2,6},{3,7},{4,0},{5,1},{6,2},{7,3},{8,12},{9,13},{10,... | collective-permute-start | bytes 196616 | tf_op jit(solution)/shard_map/ppermute | solution.py:547
  101.5 9.5 %collective-permute-start.32 = (f32[128,128]{1,0:T(8,128)S(1)}, f32[128,128]{1,0:T(8,128)S(1)}, u32[]{:S(2)}, u32[]{:S(2)}) collective-permute-start(f32[128,128]{1,0:T(8,128)S(1)} %get-tuple-element.135), channel_id=1, source_target_pairs={{0,5},{1,6},{2,7},{3,0},{4,1},{5,2},{6,3},{7,4},{8,13},{9,14},{10,... | collective-permute-start | bytes 196616 | tf_op jit(solution)/shard_map/ppermute | solution.py:547
  102.7 8.3 %collective-permute-start.33 = (f32[128,128]{1,0:T(8,128)S(1)}, f32[128,128]{1,0:T(8,128)S(1)}, u32[]{:S(2)}, u32[]{:S(2)}) collective-permute-start(f32[128,128]{1,0:T(8,128)S(1)} %get-tuple-element.136), channel_id=1, source_target_pairs={{0,6},{1,7},{2,0},{3,1},{4,2},{5,3},{6,4},{7,5},{8,14},{9,15},{10,... | collective-permute-start | bytes 196616 | tf_op jit(solution)/shard_map/ppermute | solution.py:547
  104.2 10.5 %collective-permute-start.34 = (f32[128,128]{1,0:T(8,128)S(1)}, f32[128,128]{1,0:T(8,128)S(1)}, u32[]{:S(2)}, u32[]{:S(2)}) collective-permute-start(f32[128,128]{1,0:T(8,128)S(1)} %get-tuple-element.137), channel_id=1, source_target_pairs={{0,7},{1,0},{2,1},{3,2},{4,3},{5,4},{6,5},{7,6},{8,15},{9,8},{10,9... | collective-permute-start | bytes 196616 | tf_op jit(solution)/shard_map/ppermute | solution.py:547
  107.5 9.5 %collective-permute-start.14 = (f32[128,128]{1,0:T(8,128)S(1)}, f32[128,128]{1,0:T(8,128)S(1)}, u32[]{:S(2)}, u32[]{:S(2)}) collective-permute-start(f32[128,128]{1,0:T(8,128)S(1)} %get-tuple-element.113), channel_id=1, source_target_pairs={{0,1},{1,2},{2,3},{3,4},{4,5},{5,6},{6,7},{7,0},{8,9},{9,10},{10,1... | collective-permute-start | bytes 196616 | tf_op jit(solution)/shard_map/ppermute | solution.py:547
  107.7 9.3 %collective-permute-start.15 = (f32[128,128]{1,0:T(8,128)S(1)}, f32[128,128]{1,0:T(8,128)S(1)}, u32[]{:S(2)}, u32[]{:S(2)}) collective-permute-start(f32[128,128]{1,0:T(8,128)S(1)} %get-tuple-element.114), channel_id=1, source_target_pairs={{0,2},{1,3},{2,4},{3,5},{4,6},{5,7},{6,0},{7,1},{8,10},{9,11},{10,... | collective-permute-start | bytes 196616 | tf_op jit(solution)/shard_map/ppermute | solution.py:547
  111.0 8.9 %collective-permute-start.16 = (f32[128,128]{1,0:T(8,128)S(1)}, f32[128,128]{1,0:T(8,128)S(1)}, u32[]{:S(2)}, u32[]{:S(2)}) collective-permute-start(f32[128,128]{1,0:T(8,128)S(1)} %get-tuple-element.115), channel_id=1, source_target_pairs={{0,3},{1,4},{2,5},{3,6},{4,7},{5,0},{6,1},{7,2},{8,11},{9,12},{10,... | collective-permute-start | bytes 196616 | tf_op jit(solution)/shard_map/ppermute | solution.py:547
  111.0 8.9 %collective-permute-start.17 = (f32[128,128]{1,0:T(8,128)S(1)}, f32[128,128]{1,0:T(8,128)S(1)}, u32[]{:S(2)}, u32[]{:S(2)}) collective-permute-start(f32[128,128]{1,0:T(8,128)S(1)} %get-tuple-element.116), channel_id=1, source_target_pairs={{0,4},{1,5},{2,6},{3,7},{4,0},{5,1},{6,2},{7,3},{8,12},{9,13},{10,... | collective-permute-start | bytes 196616 | tf_op jit(solution)/shard_map/ppermute | solution.py:547
  114.7 5.2 %collective-permute-start.18 = (f32[128,128]{1,0:T(8,128)S(1)}, f32[128,128]{1,0:T(8,128)S(1)}, u32[]{:S(2)}, u32[]{:S(2)}) collective-permute-start(f32[128,128]{1,0:T(8,128)S(1)} %get-tuple-element.117), channel_id=1, source_target_pairs={{0,5},{1,6},{2,7},{3,0},{4,1},{5,2},{6,3},{7,4},{8,13},{9,14},{10,... | collective-permute-start | bytes 196616 | tf_op jit(solution)/shard_map/ppermute | solution.py:547
  117.0 5.1 %collective-permute-start.19 = (f32[128,128]{1,0:T(8,128)S(1)}, f32[128,128]{1,0:T(8,128)S(1)}, u32[]{:S(2)}, u32[]{:S(2)}) collective-permute-start(f32[128,128]{1,0:T(8,128)S(1)} %get-tuple-element.118), channel_id=1, source_target_pairs={{0,6},{1,7},{2,0},{3,1},{4,2},{5,3},{6,4},{7,5},{8,14},{9,15},{10,... | collective-permute-start | bytes 196616 | tf_op jit(solution)/shard_map/ppermute | solution.py:547
  117.0 5.1 %collective-permute-start.20 = (f32[128,128]{1,0:T(8,128)S(1)}, f32[128,128]{1,0:T(8,128)S(1)}, u32[]{:S(2)}, u32[]{:S(2)}) collective-permute-start(f32[128,128]{1,0:T(8,128)S(1)} %get-tuple-element.119), channel_id=1, source_target_pairs={{0,7},{1,0},{2,1},{3,2},{4,3},{5,4},{6,5},{7,6},{8,15},{9,8},{10,9... | collective-permute-start | bytes 196616 | tf_op jit(solution)/shard_map/ppermute | solution.py:547
where the time goes:
time: 126 us; the launch traced here: 125 us
  starting transfers between devices  49.5 us (39%)
  waiting for transfers between devices  42.5 us (34%)
  Pallas kernels  25.5 us (20%)
  local copies, waits for them, and re-layouts  4.14 us (3%)
  between operations  3.15 us (2%)
    ppermute x28, starting transfers between devices, exchange(): moved.append(lax.ppermute(blocks[shift], 'lat', route))  28.8 us
    ppermute x28, waiting for transfers between devices, exchange(): moved.append(lax.ppermute(blocks[shift], 'lat', route))  12.9 us
    ppermute x1, waiting for transfers between devices, per_device_hops(): far = lax.ppermute(far, 'win', [(0, 2), (1, 3)])  12.6 us
    pallas_call x2, Pallas kernels, build(): pl.pallas_call(functools.partial(build_kernel, count), out_shape=[shape]...  7.15 us
    ppermute x1, starting transfers between devices, per_device_hops(): side = lax.ppermute(side, 'win', [(0, 2), (1, 3)])  4.93 us
    ppermute x1, waiting for transfers between devices, per_device_hops(): near = lax.ppermute(near, 'win', [(0, 1), (1, 0), (2, 3)])  4.6 us
    ppermute x1, waiting for transfers between devices, per_device_hops(): cross = lax.ppermute(cross, 'win', [(0, 1), (2, 3), (3, 2)])  4.46 us
    ppermute x1, waiting for transfers between devices, per_device_hops(): side = lax.ppermute(side, 'win', [(0, 2), (1, 3)])  4.4 us
  transfers between devices with their start and end apart: 37, of which 12 were waited for; matrix products, arithmetic and copies ran while one was open for 0% of the time, Pallas kernels for 16%

commit v1 on v0

--- a/solution.py
+++ b/solution.py
@@ -12,9 +12,17 @@
 
 LANES = 128
 ROWS = 8
+WEIGHTS = (
+    (0.0, 1.0, -1.0, 1.0, 0.5, 1.0, 0.0, 0.0, 0.0, 0.0, 0.0, 0.0, 0.0, 0.0),
+    (0.5, 1 / 2, 1.0, 0.0, 1.0, 0.0, 0.0, 0.0, 0.0, 1.0, 0.0, 0.0, 1.0, 0.5),
+    (0.5, 1 / 3, 1.0, 0.0, 0.0, 1.0, 1 / 3, 0.0, 1.0, 0.0, 0.5, 1.0, 0.0, 0.0),
+    (0.5, 1 / 4, 1.0, 0.0, 0.0, 0.0, 1.0, 1.0, 1 / 3, 0.0, 0.0, 1.0, 1 / 3, 0.0),
+)
+OWN, SHARE, SIGN, FIRST, ONWARD, SECOND, SIDE, EVEN, ODD, KNOWN = 0, 1, 2, 3, 4, 5, 6, 7, 10, 13
 VMEM = pl.BlockSpec(memory_space=pltpu.VMEM)
 SMEM = pl.BlockSpec(memory_space=pltpu.SMEM)
 ANY = pl.BlockSpec(memory_space=pl.ANY)
+HBM = pl.BlockSpec(memory_space=pltpu.HBM)
 LIMIT = pltpu.CompilerParams(vmem_limit_bytes=16 * 2**20)
 
 
@@ -224,40 +232,64 @@
     )
 
 
-def weight_of(here_ref, table):
-    return lambda number: table[here_ref[1], number]
-
-
-def windowed(weight, x, mult, ended):
-    half = x.shape[1] // 2
-    sent = weight(SIGN) * ended + weight(SHARE) * (mult + weight(OWN) * x)
-    return [part for value in (ended, sent) for part in
+def weight_of(here_ref):
+    def pick(number):
+        value = WEIGHTS[0][number]
+        for window in range(1, len(WEIGHTS)):
+            value = jnp.where(here_ref[1] == window, WEIGHTS[window][number], value)
+        return value
+
+    return pick
+
+
+def windowed(weight, own, ended):
+    half = own.shape[1] // 2
+    values = (ended, weight(SIGN) * ended + weight(SHARE) * own)
+    return [part for value in values for part in
             (value[:, :half] + value[:, half:], value[:, :half] - value[:, half:])]
 
 
-def forecast_kernel(here_ref, table, speed, drift, kappa, x_ref, mult_ref, x1_ref, *outs):
+def forecast_kernel(here_ref, speed, drift, kappa, x_hbm, mult_hbm, x_ref, own_ref, x1_ref, *refs):
+    outs, (mult_ref, sems) = refs[:4], refs[4:]
     band = x_ref.shape[0]
-    weight, scal = weight_of(here_ref, table), (speed[0], drift[0], kappa[0])
+    chunk = band // 4
+    weight, scal = weight_of(here_ref), (speed[0], drift[0], kappa[0])
 
     def step(source, at, count):
         return stencil(scal, source[at:at + count], source[at + 1:at + count + 1], source[at - 1:at + count - 1])
 
-    x1_ref[ROWS - 1:ROWS] = step(x_ref, ROWS - 1, 1)
-    x1_ref[band - ROWS:band - ROWS + 1] = step(x_ref, band - ROWS, 1)
-    for at in range(ROWS, band - ROWS, ROWS):
-        x1_ref[at:at + ROWS] = step(x_ref, at, ROWS)
-    for at in range(ROWS, band - ROWS, ROWS):
-        rows = slice(at, at + ROWS)
-        parts = windowed(weight, x_ref[rows], mult_ref[rows], 0.5 * step(x1_ref, at, ROWS))
-        for out, part in zip(outs, parts):
-            out[rows] = part
-
-
-def edge_kernel(bands, here_ref, table, speed, drift, kappa, x_ref, mult_ref, low_ref, high_ref, *refs):
+    copies = []
+    for number, (source, target) in enumerate(((x_hbm, x_ref), (mult_hbm, mult_ref))):
+        for part in range(4):
+            rows = slice(part * chunk, (part + 1) * chunk)
+            copies.append(pltpu.make_async_copy(source.at[rows], target.at[rows], sems.at[number, part]))
+            copies[-1].start()
+    ready, stepped = 0, ROWS
+    for part in range(4):
+        copies[part].wait()
+        ready += chunk
+        if part == 0:
+            x1_ref[ROWS - 1:ROWS] = step(x_ref, ROWS - 1, 1)
+        while stepped + ROWS < ready:
+            x1_ref[stepped:stepped + ROWS] = step(x_ref, stepped, ROWS)
+            stepped += ROWS
+    x1_ref[stepped:stepped + 1] = step(x_ref, stepped, 1)
+    for part in range(4):
+        copies[4 + part].wait()
+        for at in range(part * chunk, (part + 1) * chunk, ROWS):
+            rows = slice(at, at + ROWS)
+            own = mult_ref[rows] + weight(OWN) * x_ref[rows]
+            own_ref[rows] = own
+            if 0 < at < band - ROWS:
+                for out, value in zip(outs, windowed(weight, own, 0.5 * step(x1_ref, at, ROWS))):
+                    out[rows] = value
+
+
+def edge_kernel(bands, here_ref, speed, drift, kappa, x_ref, own_ref, low_ref, high_ref, *refs):
     outs, (ext, mid, whole, parts, sems) = refs[5:10], refs[10:]
     band = x_ref.shape[0]
     edge = low_ref.shape[0]
-    weight, scal = weight_of(here_ref, table), (speed[0], drift[0], kappa[0])
+    weight, scal = weight_of(here_ref), (speed[0], drift[0], kappa[0])
     copies = []
     for end in range(2):
         at = 0 if end == 0 else band - ROWS
@@ -282,7 +314,7 @@
         mid[end, ROWS:2 * ROWS] = step(ext, ROWS, ROWS)
         rows = slice(at, at + ROWS)
         whole[end] = mid[end, ROWS:2 * ROWS]
-        for number, part in enumerate(windowed(weight, x_ref[rows], mult_ref[rows], 0.5 * step(mid, ROWS, ROWS))):
+        for number, part in enumerate(windowed(weight, own_ref[rows], 0.5 * step(mid, ROWS, ROWS))):
             parts[end, number] = part
         sources = [whole.at[end]] + [parts.at[end, number] for number in range(4)]
         for number, (source, out) in enumerate(zip(sources, outs)):
@@ -294,25 +326,25 @@
 
 def forecast(here, bands, scal, x, mult, exchange_edges):
     band, width = x.shape
-    shapes = [jax.ShapeDtypeStruct((band, width), jnp.float32)]
-    shapes += [jax.ShapeDtypeStruct((band, width // 2), jnp.float32)] * 4
-    table = jnp.asarray(WEIGHTS)
-    inner = pl.pallas_call(
+    whole = jax.ShapeDtypeStruct((band, width), jnp.float32)
+    shapes = [whole] + [jax.ShapeDtypeStruct((band, width // 2), jnp.float32)] * 4
+    x, own, *inner = pl.pallas_call(
         forecast_kernel,
-        out_shape=shapes,
-        in_specs=[SMEM] * 5 + [VMEM] * 2,
-        out_specs=[VMEM] * 5,
+        out_shape=[whole] * 2 + shapes,
+        in_specs=[SMEM] * 4 + [HBM] * 2,
+        out_specs=[VMEM] * 7,
+        scratch_shapes=[pltpu.VMEM((band, width), jnp.float32), pltpu.SemaphoreType.DMA((2, 4))],
         compiler_params=LIMIT,
         cost_estimate=pl.CostEstimate(flops=40 * band * width, bytes_accessed=20 * band * width, transcendentals=0),
         name="forecast",
-    )(here, table, *scal, x, mult)
+    )(here, *scal, pltpu.with_memory_space_constraint(x, pltpu.HBM), pltpu.with_memory_space_constraint(mult, pltpu.HBM))
     low, high = exchange_edges
-    return pl.pallas_call(
+    outs = pl.pallas_call(
         functools.partial(edge_kernel, bands),
         out_shape=shapes,
-        in_specs=[SMEM] * 5 + [VMEM] * 4 + [ANY] * 5,
+        in_specs=[SMEM] * 4 + [VMEM] * 4 + [ANY] * 5,
         out_specs=[ANY] * 5,
-        input_output_aliases={9 + number: number for number in range(5)},
+        input_output_aliases={8 + number: number for number in range(5)},
         scratch_shapes=[pltpu.VMEM((2, 4 * ROWS, width), jnp.float32)] * 2 + [
             pltpu.VMEM((2, ROWS, width), jnp.float32),
             pltpu.VMEM((2, 4, ROWS, width // 2), jnp.float32),
@@ -321,35 +353,37 @@
         compiler_params=LIMIT,
         cost_estimate=pl.CostEstimate(flops=1000 * width, bytes_accessed=400 * width, transcendentals=0),
         name="edges",
-    )(here, table, *scal, x, mult, low, high, *inner)
-
-
-def defect_kernel(here_ref, table, x_ref, mult_ref, obs_ref, mask_ref, x1_ref, plus_ref, minus_ref,
+    )(here, *scal, x, own, low, high, *inner)
+    return x, own, *outs
+
+
+def defect_kernel(here_ref, own_ref, obs_ref, mask_ref, x1_ref, plus_ref, minus_ref,
                   base_plus, base_minus, step_plus, second_ref, third_ref):
-    half = x_ref.shape[1] // 2
-    weight = weight_of(here_ref, table)
-    for at in range(0, x_ref.shape[0], ROWS):
+    half = own_ref.shape[1] // 2
+    weight = weight_of(here_ref)
+    for at in range(0, own_ref.shape[0], ROWS):
         rows = slice(at, at + ROWS)
         plus, minus = plus_ref[rows], minus_ref[rows]
         base, own = [], []
         for cols, end in ((slice(0, half), plus + minus), (slice(half, 2 * half), plus - minus)):
-            part = mult_ref[rows, cols] + weight(OWN) * x_ref[rows, cols]
-            own.append(part)
+            own.append(own_ref[rows, cols])
             seen = mask_ref[:, rows, cols].astype(jnp.float32)
             base.append(
-                part + seen[0] * (obs_ref[0, rows, cols] - x1_ref[rows, cols])
+                own[-1] + seen[0] * (obs_ref[0, rows, cols] - x1_ref[rows, cols])
                 + seen[1] * (obs_ref[1, rows, cols] - end)
             )
         base_plus[rows] = base[0] + base[1]
         base_minus[rows] = base[0] - base[1]
         own_plus, own_minus = own[0] + own[1], own[0] - own[1]
         step_plus[rows] = own_plus - plus
-        second_ref[rows] = jnp.where(weight(FIRST) > 0.0, plus + own_plus * weight(SHARE), minus + own_minus * weight(SHARE))
-        third_ref[rows] = jnp.where(weight(FIRST) > 0.0, minus + own_minus * weight(SHARE), own_minus - minus)
-
-
-def defect(here, x, mult, obs, mask, x1, plus, minus):
-    band, width = x.shape
+        first = weight(FIRST) > 0.0
+        sent_minus = minus + weight(SHARE) * own_minus
+        second_ref[rows] = jnp.where(first, plus + weight(SHARE) * own_plus, sent_minus)
+        third_ref[rows] = jnp.where(first, sent_minus, own_minus - minus)
+
+
+def defect(here, own, obs, mask, x1, plus, minus):
+    band, width = own.shape
     rows = 4 * ROWS
     whole = pl.BlockSpec((rows, width), lambda i: (i, 0))
     pair = pl.BlockSpec((2, rows, width), lambda i: (0, i, 0))
@@ -358,17 +392,35 @@
         defect_kernel,
         grid=(band // rows,),
         out_shape=[jax.ShapeDtypeStruct((band, width // 2), jnp.float32)] * 5,
-        in_specs=[SMEM, SMEM, whole, whole, pair, pair, whole, part, part],
+        in_specs=[SMEM, whole, pair, pair, whole, part, part],
         out_specs=[part] * 5,
         compiler_params=LIMIT,
         cost_estimate=pl.CostEstimate(flops=30 * band * width, bytes_accessed=40 * band * width, transcendentals=0),
         name="defect",
-    )(here, jnp.asarray(WEIGHTS), x, mult, obs, mask, x1, plus, minus)
-
-
-def resid_kernel(bands, first, here_ref, table, base_ref, *refs):
-    weight = weight_of(here_ref, table)
+    )(here, own, obs, mask, x1, plus, minus)
+
+
+def mix_kernel(first, here_ref, one_ref, other_ref, out_ref):
+    weight = weight_of(here_ref)
+    one = one_ref[...] if first is None else weight(first) * one_ref[...]
+    out_ref[...] = one + weight(ONWARD if first is None else SIDE) * other_ref[...]
+
+
+def mix(here, first, one, other):
+    return pl.pallas_call(
+        functools.partial(mix_kernel, first),
+        out_shape=jax.ShapeDtypeStruct(one.shape, jnp.float32),
+        in_specs=[SMEM] + [VMEM] * 2,
+        out_specs=VMEM,
+        compiler_params=LIMIT,
+        cost_estimate=pl.CostEstimate(flops=3 * one.size, bytes_accessed=12 * one.size, transcendentals=0),
+        name="mix",
+    )(here, one, other)
+
+
+def resid_kernel(bands, first, here_ref, base_ref, *refs):
     terms, outs = refs[:-bands], refs[-bands:]
+    weight = weight_of(here_ref)
     columns = outs[0].shape[1]
     for shift in range(bands):
         target = lax.rem(here_ref[0] + shift, bands)
@@ -379,18 +431,18 @@
         outs[shift][...] = value
 
 
-def resid_blocks(here, bands, first, base, terms):
+def resid_blocks(here, bands, first, base, *terms):
     band, half = base.shape
     columns = half // bands
     return pl.pallas_call(
         functools.partial(resid_kernel, bands, first),
         out_shape=[jax.ShapeDtypeStruct((band, columns), jnp.float32)] * bands,
-        in_specs=[SMEM, SMEM] + [VMEM] * (1 + len(terms)),
+        in_specs=[SMEM] + [VMEM] * 4,
         out_specs=[VMEM] * bands,
         compiler_params=LIMIT,
         cost_estimate=pl.CostEstimate(flops=8 * band * half, bytes_accessed=24 * band * half, transcendentals=0),
         name="resid_blocks",
-    )(here, jnp.asarray(WEIGHTS), base, *terms)
+    )(here, base, *terms)
 
 
 def lat_kernel(bands, here_ref, *refs):
@@ -489,41 +541,18 @@
     )(here, *blocks, *matrices, *extra)
 
 
-def mix_kernel(here_ref, table, near_ref, side_ref, step_ref, second_ref, far_ref, cross_ref):
-    weight = weight_of(here_ref, table)
-    for at in range(0, near_ref.shape[0], ROWS):
+def multiplier_kernel(here_ref, own_ref, plus_ref, minus_ref, near_ref, cross_ref, out_ref):
+    weight = weight_of(here_ref)
+    half = own_ref.shape[1] // 2
+    for at in range(0, own_ref.shape[0], ROWS):
         rows = slice(at, at + ROWS)
-        far_ref[rows] = near_ref[rows] + weight(ONWARD) * step_ref[rows]
-        cross_ref[rows] = weight(SECOND) * second_ref[rows] + weight(SIDE) * side_ref[rows]
-
-
-def mix(here, near, side, step_plus, second):
-    shape = jax.ShapeDtypeStruct(near.shape, jnp.float32)
-    return pl.pallas_call(
-        mix_kernel,
-        out_shape=[shape] * 2,
-        in_specs=[SMEM] * 2 + [VMEM] * 4,
-        out_specs=[VMEM] * 2,
-        compiler_params=LIMIT,
-        cost_estimate=pl.CostEstimate(flops=5 * near.size, bytes_accessed=24 * near.size, transcendentals=0),
-        name="mix",
-    )(here, jnp.asarray(WEIGHTS), near, side, step_plus, second)
-
-
-def multiplier_kernel(here_ref, table, x_ref, mult_ref, plus_ref, minus_ref, near_ref, cross_ref, out_ref):
-    weight = weight_of(here_ref, table)
-    half = x_ref.shape[1] // 2
-    known = weight(KNOWN)
-    for at in range(0, x_ref.shape[0], ROWS):
-        rows = slice(at, at + ROWS)
-        plus = plus_ref[rows] + known * (cross_ref[rows] - near_ref[rows])
-        minus = minus_ref[rows]
-        for cols, end in ((slice(0, half), plus + minus), (slice(half, 2 * half), plus - minus)):
-            out_ref[rows, cols] = mult_ref[rows, cols] + weight(OWN) * x_ref[rows, cols] - 0.5 * end
-
-
-def new_multipliers(here, x, mult, plus, minus, near, cross):
-    band, width = x.shape
+        plus, minus = plus_ref[rows] + weight(KNOWN) * (cross_ref[rows] - near_ref[rows]), minus_ref[rows]
+        out_ref[rows, :half] = own_ref[rows, :half] - 0.5 * (plus + minus)
+        out_ref[rows, half:] = own_ref[rows, half:] - 0.5 * (plus - minus)
+
+
+def new_multipliers(here, own, *terms):
+    band, width = own.shape
     rows = 4 * ROWS
     whole = pl.BlockSpec((rows, width), lambda i: (i, 0))
     part = pl.BlockSpec((rows, width // 2), lambda i: (i, 0))
@@ -531,12 +560,12 @@
         multiplier_kernel,
         grid=(band // rows,),
         out_shape=jax.ShapeDtypeStruct((band, width), jnp.float32),
-        in_specs=[SMEM] * 2 + [whole] * 2 + [part] * 4,
+        in_specs=[SMEM, whole] + [part] * 4,
         out_specs=whole,
         compiler_params=LIMIT,
         cost_estimate=pl.CostEstimate(flops=6 * band * width, bytes_accessed=20 * band * width, transcendentals=0),
         name="new_multipliers",
-    )(here, jnp.asarray(WEIGHTS), x, mult, plus, minus, near, cross)
+    )(here, own, *terms)
 
 
 def exchange(blocks):
@@ -548,13 +577,8 @@
     return moved
 
 
-WEIGHTS = np.array([
-    [0.0, 1.0, -1.0, 1.0, 0.5, 1.0, 0.0, 0.0, 0.0, 0.0, 0.0, 0.0, 0.0, 0.0],
-    [0.5, 1 / 2, 1.0, 0.0, 1.0, 0.0, 0.0, 0.0, 0.0, 1.0, 0.0, 0.0, 1.0, 0.5],
-    [0.5, 1 / 3, 1.0, 0.0, 0.0, 1.0, 1 / 3, 0.0, 1.0, 0.0, 0.5, 1.0, 0.0, 0.0],
-    [0.5, 1 / 4, 1.0, 0.0, 0.0, 0.0, 1.0, 1.0, 1 / 3, 0.0, 0.0, 1.0, 1 / 3, 0.0],
-], np.float32)
-OWN, SHARE, SIGN, FIRST, ONWARD, SECOND, SIDE, EVEN, ODD, KNOWN = 0, 1, 2, 3, 4, 5, 6, 7, 10, 13
+def hop(value, pairs):
+    return lax.ppermute(value, "win", pairs)
 
 
 def per_device(
@@ -582,28 +606,27 @@
         lax.ppermute(x[-2:], "lat", [(i, i + 1) for i in range(bands - 1)]),
         lax.ppermute(x[:2], "lat", [(i + 1, i) for i in range(bands - 1)]),
     )
-    x1, plus, minus, near, side = forecast(here, bands, (speed, drift, kappa), x, mult, edges)
-    near = lax.ppermute(near, "win", [(0, 1), (1, 0), (2, 3)])
-    side = lax.ppermute(side, "win", [(0, 2), (1, 3)])
+    x, own, x1, plus, minus, near, side = forecast(here, bands, (speed, drift, kappa), x, mult, edges)
+    near = hop(near, [(0, 1), (1, 0), (2, 3)])
+    side = hop(side, [(0, 2), (1, 3)])
     base_plus, base_minus, step_plus, second, third = defect(
-        here, x, mult, observations[0, :, 0], obs_mask[0], x1, plus, minus
+        here, own, observations[0, :, 0], obs_mask[0], x1, plus, minus
     )
-    lat_matrices, step_plus, second = lax.optimization_barrier((build(lat_spectrum), step_plus, second))
-    far, cross = mix(here, near, side, step_plus, second)
-    far = lax.ppermute(far, "win", [(0, 2), (1, 3)])
-    cross = lax.ppermute(cross, "win", [(0, 1), (2, 3), (3, 2)])
-    even = list(resid_blocks(here, bands, EVEN, base_plus, (near, far, cross)))
-    lon_matrices, third, even[0] = lax.optimization_barrier((build(lon_spectrum), third, even[0]))
-    third = lax.ppermute(third, "win", [(0, 1), (1, 3)])
-    odd = resid_blocks(here, bands, ODD, base_minus, (side, cross, third))
-    plus = lax.ppermute(plus, "win", [(1, 2), (2, 3)])
-    minus = lax.ppermute(minus, "win", [(0, 1), (1, 2), (2, 3)])
+    far = hop(mix(here, None, near, step_plus), [(0, 2), (1, 3)])
+    cross = hop(mix(here, SECOND, second, side), [(0, 1), (2, 3), (3, 2)])
+    third = hop(third, [(0, 1), (1, 3)])
+    plus = hop(plus, [(1, 2), (2, 3)])
+    minus = hop(minus, [(0, 1), (1, 2), (2, 3)])
+    lat_matrices = build(lat_spectrum)
+    lon_matrices = build(lon_spectrum)
+    even = resid_blocks(here, bands, EVEN, base_plus, near, far, cross)
+    odd = resid_blocks(here, bands, ODD, base_minus, side, cross, third)
     even, odd = exchange(even), exchange(odd)
-    even = exchange(lat_apply(here, even, lat_matrices))
-    odd = exchange(lat_apply(here, odd, lat_matrices))
+    even = lat_apply(here, even, lat_matrices)
+    even, odd = exchange(even), exchange(lat_apply(here, odd, lat_matrices))
     even = lon_apply(here, even, lon_matrices[:2])
     field = lon_apply(here, odd, lon_matrices[2:], (even, x))
-    lam = new_multipliers(here, x, mult, plus, minus, near, cross)
+    lam = new_multipliers(here, own, plus, minus, near, cross)
     return (field[None, None], lam[None, None])
 
 

time: 126 us -> 133 us (1.056)
  starting transfers between devices: 49.5 us -> 58.1 us
  local copies, waits for them, and re-layouts: 4.14 us -> 0.99 us
  Pallas kernels: 25.5 us -> 27 us
    ppermute x7, starting transfers between devices: 16.4 us -> 23 us  [hop(): return lax.ppermute(value, 'win', pairs)]
    unnamed x44 -> x32, local copies, waits for them, and re-layouts: 3.25 us -> 0.1 us
    ppermute x28, starting transfers between devices: 28.8 us -> 30.7 us  [exchange(): moved.append(lax.ppermute(blocks[shift], 'lat', route))]
    pallas_call x2 -> x3, Pallas kernels: 3.69 us -> 5.38 us  [the longest x1 4.18 us: forecast(): pl.pallas_call(forecast_kernel, out_shape=[whole] * 2 + shapes, in_specs=...]
  transfers between devices with their start and end apart: 37 -> 37, of which waited for: 12 -> 12; matrix products, arithmetic and copies ran while one was open for 0% -> 0% of each run, Pallas kernels for 16% -> 17%
where the time goes in v1:
time: 133 us; the launch traced here: 132 us
  starting transfers between devices  58.1 us (44%)
  waiting for transfers between devices  42.6 us (32%)
  Pallas kernels  27 us (20%)
  between operations  3.06 us (2%)
    ppermute x28, starting transfers between devices, exchange(): moved.append(lax.ppermute(blocks[shift], 'lat', route))  30.7 us
    ppermute x7, waiting for transfers between devices, hop(): return lax.ppermute(value, 'win', pairs)  29.3 us
    ppermute x7, starting transfers between devices, hop(): return lax.ppermute(value, 'win', pairs)  23 us
    ppermute x28, waiting for transfers between devices, exchange(): moved.append(lax.ppermute(blocks[shift], 'lat', route))  13.4 us
    pallas_call x2, Pallas kernels, build(): pl.pallas_call(functools.partial(build_kernel, count), out_shape=[shape]...  7.2 us
    pallas_call x2, Pallas kernels, lon_apply(): pl.pallas_call(functools.partial(lon_odd_kernel if extra else lon_even_ke...  4.36 us
    pallas_call x1, Pallas kernels, forecast(): pl.pallas_call(forecast_kernel, out_shape=[whole] * 2 + shapes, in_specs=...  4.18 us
    ppermute x1, starting transfers between devices, per_device_hops(): lax.ppermute(x[-2:], 'lat', [(i, i + 1) for i in range(bands - 1)])  3.03 us
  transfers between devices with their start and end apart: 37, of which 12 were waited for; matrix products, arithmetic and copies ran while one was open for 0% of the time, Pallas kernels for 17%

profile of v1, /device:TPU:0, one launch (start us, length us, event | category | flops | bytes accessed | tf_op | source)
XLA Modules:
  0.0 131.9 jit_solution(11064367973021777359)
XLA Ops:
  0.6 0.9 slice_bitcast_fusion
  1.5 1.3 collective-permute-start.1
  2.8 3.0 %collective-permute-start = (f32[2,2048]{1,0:T(2,128)S(1)}, f32[2,2048]{1,0:T(2,128)S(1)}, u32[]{:S(2)}, u32[]{:S(2)}) collective-permute-start(f32[2,2048]{1,0:T(2,128)S(1)} %get-tuple-element.117), channel_id=1, source_target_pairs={{0,1},{1,2},{2,3},{3,4},{4,5},{5,6},{6,7},{8,9},{9,10},{10,11},{11... | collective-permute-start | bytes 49160 | tf_op jit(solution)/shard_map/ppermute | solution.py:606
  5.9 0.1 pad_add_fusion.here_ref
  7.9 4.2 %forecast.1 = (f32[128,2048]{1,0:T(8,128)S(1)}, f32[128,2048]{1,0:T(8,128)S(1)}, f32[128,2048]{1,0:T(8,128)S(1)}, f32[128,1024]{1,0:T(8,128)S(1)}, f32[128,1024]...) custom-call(s32[2]{0:T(128)S(1)} %pad_add_fusion.here_ref, f32[1]{0:T(128)S(6)} %copy.33.speed, ...), custom_call_target="tpu_custom_call" | custom-call | flops 10485760 | bytes 5242880 | tf_op jit(solution)/shard_map/forecast/pallas_call | solution.py:331
  12.1 1.8 %edges.1 = (f32[128,2048]{1,0:T(8,128)S(1)}, f32[128,1024]{1,0:T(8,128)S(1)}, f32[128,1024]{1,0:T(8,128)S(1)}, f32[128,1024]{1,0:T(8,128)S(1)}, f32[128,1024]{1,0:T(8,128)S(1)}) custom-call(s32[2]{0:T(128)S(1)} %pad_add_fusion.here_ref, f32[1]{0:T(128)S(6)} %copy.33.speed, ...), custom_call_target="tpu_custom_call", output_to_operand_aliasing={{0}: (8, {}), {1}: (9, {}), {2}: (10, {}), {3}: (11, {}), {... | custom-call | flops 2048000 | bytes 819200 | tf_op jit(solution)/shard_map/edges/pallas_call | solution.py:342
  13.9 4.9 %collective-permute-start.19 = (f32[128,1024]{1,0:T(8,128)S(1)}, f32[128,1024]{1,0:T(8,128)S(1)}, u32[]{:S(2)}, u32[]{:S(2)}) collective-permute-start(f32[128,1024]{1,0:T(8,128)S(1)} %get-tuple-element.96), channel_id=1, source_target_pairs={{0,8},{8,0},{16,24},{1,9},{9,1},{17,25},{2,10},{10,2},{18,26},{3,1... | collective-permute-start | bytes 1572872 | tf_op jit(solution)/shard_map/ppermute | solution.py:581
  18.8 3.5 %collective-permute-start.2 = (f32[128,1024]{1,0:T(8,128)S(1)}, f32[128,1024]{1,0:T(8,128)S(1)}, u32[]{:S(2)}, u32[]{:S(2)}) collective-permute-start(f32[128,1024]{1,0:T(8,128)S(1)} %get-tuple-element.70), channel_id=1, source_target_pairs={{0,16},{8,24},{1,17},{9,25},{2,18},{10,26},{3,19},{11,27},{4,20},{... | collective-permute-start | bytes 1572872 | tf_op jit(solution)/shard_map/ppermute | solution.py:581
  22.3 1.5 %defect.1 = (f32[128,1024]{1,0:T(8,128)S(1)}, f32[128,1024]{1,0:T(8,128)S(1)}, f32[128,1024]{1,0:T(8,128)S(1)}, f32[128,1024]{1,0:T(8,128)S(1)}, f32[128,1024]{1,0:T(8,128)S(1)}) custom-call(s32[2]{0:T(128)S(1)} %pad_add_fusion.here_ref, f32[128,2048]{1,0:T(8,128)S(1)} %get-tuple-element.59.own_ref, f32[2,128,2048]{2,1,0:T(8,128)S(1)} %bitcast.12, ...), custom_call_target="tpu_custom_call" | custom-call | flops 7864320 | bytes 10485760 | tf_op jit(solution)/shard_map/defect/pallas_call | solution.py:391
  23.8 7.0 %collective-permute-done.19.one_ref.refs_0_.near_ref = f32[128,1024]{1,0:T(8,128)S(1)} collective-permute-done((f32[128,1024]{1,0:T(8,128)S(1)}, f32[128,1024]{1,0:T(8,128)S(1)}, u32[]{:S(2)}, u32[]{:S(2)}) %collective-permute-start.19) | collective-permute-done | bytes 524320 | tf_op jit(solution)/shard_map/ppermute | solution.py:581
  30.9 0.6 mix.3
  31.5 3.5 %collective-permute-start.20 = (f32[128,1024]{1,0:T(8,128)S(1)}, f32[128,1024]{1,0:T(8,128)S(1)}, u32[]{:S(2)}, u32[]{:S(2)}) collective-permute-start(f32[128,1024]{1,0:T(8,128)S(1)} %mix.3), channel_id=1, source_target_pairs={{0,16},{8,24},{1,17},{9,25},{2,18},{10,26},{3,19},{11,27},{4,20},{... | collective-permute-start | bytes 1572872 | tf_op jit(solution)/shard_map/ppermute | solution.py:581
  34.9 0.6 mix.2
  35.5 4.4 %collective-permute-start.3 = (f32[128,1024]{1,0:T(8,128)S(1)}, f32[128,1024]{1,0:T(8,128)S(1)}, u32[]{:S(2)}, u32[]{:S(2)}) collective-permute-start(f32[128,1024]{1,0:T(8,128)S(1)} %mix.2), channel_id=1, source_target_pairs={{0,8},{16,24},{24,16},{1,9},{17,25},{25,17},{2,10},{18,26},{26,18}... | collective-permute-start | bytes 1572872 | tf_op jit(solution)/shard_map/ppermute | solution.py:581
  40.0 0.7 collective-permute-start.35
  40.7 4.2 %collective-permute-start.4 = (f32[128,1024]{1,0:T(8,128)S(1)}, f32[128,1024]{1,0:T(8,128)S(1)}, u32[]{:S(2)}, u32[]{:S(2)}) collective-permute-start(f32[128,1024]{1,0:T(8,128)S(1)} %get-tuple-element.72), channel_id=1, source_target_pairs={{0,8},{8,24},{1,9},{9,25},{2,10},{10,26},{3,11},{11,27},{4,12},{12... | collective-permute-start | bytes 1572872 | tf_op jit(solution)/shard_map/ppermute | solution.py:581
  44.9 1.9 %collective-permute-start.36 = (f32[128,1024]{1,0:T(8,128)S(1)}, f32[128,1024]{1,0:T(8,128)S(1)}, u32[]{:S(2)}, u32[]{:S(2)}) collective-permute-start(f32[128,1024]{1,0:T(8,128)S(1)} %get-tuple-element.68.minus_ref), channel_id=1, source_target_pairs={{0,8},{8,16},{16,24},{1,9},{9,17},{17,25},{2,10},{10,18},{18,26},{... | collective-permute-start | bytes 1572872 | tf_op jit(solution)/shard_map/ppermute | solution.py:581
  46.8 22.2 %collective-permute-done.20.refs_1_ = f32[128,1024]{1,0:T(8,128)S(1)} collective-permute-done((f32[128,1024]{1,0:T(8,128)S(1)}, f32[128,1024]{1,0:T(8,128)S(1)}, u32[]{:S(2)}, u32[]{:S(2)}) %collective-permute-start.20) | collective-permute-done | bytes 524320 | tf_op jit(solution)/shard_map/ppermute | solution.py:581
  69.1 0.0 copy-start.13
  69.1 0.0 copy-start.15
  69.1 0.8 resid_blocks.3
  69.9 0.1 collective-permute-start.21
  70.0 1.6 %collective-permute-start.22 = (f32[128,128]{1,0:T(8,128)S(1)}, f32[128,128]{1,0:T(8,128)S(1)}, u32[]{:S(2)}, u32[]{:S(2)}) collective-permute-start(f32[128,128]{1,0:T(8,128)S(1)} %get-tuple-element.100), channel_id=1, source_target_pairs={{0,2},{1,3},{2,4},{3,5},{4,6},{5,7},{6,0},{7,1},{8,10},{9,11},{10,... | collective-permute-start | bytes 196616 | tf_op jit(solution)/shard_map/ppermute | solution.py:576
  71.6 1.2 collective-permute-start.23
  72.9 2.5 %collective-permute-start.24 = (f32[128,128]{1,0:T(8,128)S(1)}, f32[128,128]{1,0:T(8,128)S(1)}, u32[]{:S(2)}, u32[]{:S(2)}) collective-permute-start(f32[128,128]{1,0:T(8,128)S(1)} %get-tuple-element.102), channel_id=1, source_target_pairs={{0,4},{1,5},{2,6},{3,7},{4,0},{5,1},{6,2},{7,3},{8,12},{9,13},{10,... | collective-permute-start | bytes 196616 | tf_op jit(solution)/shard_map/ppermute | solution.py:576
  75.4 0.1 collective-permute-done.21.refs_1_
  75.5 0.8 collective-permute-done.22.refs_2_
  76.4 1.6 %collective-permute-start.26 = (f32[128,128]{1,0:T(8,128)S(1)}, f32[128,128]{1,0:T(8,128)S(1)}, u32[]{:S(2)}, u32[]{:S(2)}) collective-permute-start(f32[128,128]{1,0:T(8,128)S(1)} %get-tuple-element.104), channel_id=1, source_target_pairs={{0,6},{1,7},{2,0},{3,1},{4,2},{5,3},{6,4},{7,5},{8,14},{9,15},{10,... | collective-permute-start | bytes 196616 | tf_op jit(solution)/shard_map/ppermute | solution.py:576
  78.0 0.8 resid_blocks.2
  78.8 2.9 %collective-permute-done.23.refs_3_ = f32[128,128]{1,0:T(8,128)S(1)} collective-permute-done((f32[128,128]{1,0:T(8,128)S(1)}, f32[128,128]{1,0:T(8,128)S(1)}, u32[]{:S(2)}, u32[]{:S(2)}) %collective-permute-start.23) | collective-permute-done | bytes 65568 | tf_op jit(solution)/shard_map/ppermute | solution.py:576
  81.7 0.2 collective-permute-done.24.refs_4_
  81.9 1.0 collective-permute-start.5
  82.9 2.1 %collective-permute-start.6 = (f32[128,128]{1,0:T(8,128)S(1)}, f32[128,128]{1,0:T(8,128)S(1)}, u32[]{:S(2)}, u32[]{:S(2)}) collective-permute-start(f32[128,128]{1,0:T(8,128)S(1)} %get-tuple-element.75), channel_id=1, source_target_pairs={{0,2},{1,3},{2,4},{3,5},{4,6},{5,7},{6,0},{7,1},{8,10},{9,11},{10,... | collective-permute-start | bytes 196616 | tf_op jit(solution)/shard_map/ppermute | solution.py:576
  85.1 1.7 %collective-permute-start.7 = (f32[128,128]{1,0:T(8,128)S(1)}, f32[128,128]{1,0:T(8,128)S(1)}, u32[]{:S(2)}, u32[]{:S(2)}) collective-permute-start(f32[128,128]{1,0:T(8,128)S(1)} %get-tuple-element.76), channel_id=1, source_target_pairs={{0,3},{1,4},{2,5},{3,6},{4,7},{5,0},{6,1},{7,2},{8,11},{9,12},{10,... | collective-permute-start | bytes 196616 | tf_op jit(solution)/shard_map/ppermute | solution.py:576
  86.8 0.4 collective-permute-start.8
  87.3 0.6 collective-permute-done.5.refs_1_
  87.9 1.4 %collective-permute-start.9 = (f32[128,128]{1,0:T(8,128)S(1)}, f32[128,128]{1,0:T(8,128)S(1)}, u32[]{:S(2)}, u32[]{:S(2)}) collective-permute-start(f32[128,128]{1,0:T(8,128)S(1)} %get-tuple-element.78), channel_id=1, source_target_pairs={{0,5},{1,6},{2,7},{3,0},{4,1},{5,2},{6,3},{7,4},{8,13},{9,14},{10,... | collective-permute-start | bytes 196616 | tf_op jit(solution)/shard_map/ppermute | solution.py:576
  89.3 0.5 collective-permute-done.6.refs_2_
  89.8 1.8 %collective-permute-start.10 = (f32[128,128]{1,0:T(8,128)S(1)}, f32[128,128]{1,0:T(8,128)S(1)}, u32[]{:S(2)}, u32[]{:S(2)}) collective-permute-start(f32[128,128]{1,0:T(8,128)S(1)} %get-tuple-element.79), channel_id=1, source_target_pairs={{0,6},{1,7},{2,0},{3,1},{4,2},{5,3},{6,4},{7,5},{8,14},{9,15},{10,... | collective-permute-start | bytes 196616 | tf_op jit(solution)/shard_map/ppermute | solution.py:576
  91.6 2.7 %collective-permute-done.7.refs_3_ = f32[128,128]{1,0:T(8,128)S(1)} collective-permute-done((f32[128,128]{1,0:T(8,128)S(1)}, f32[128,128]{1,0:T(8,128)S(1)}, u32[]{:S(2)}, u32[]{:S(2)}) %collective-permute-start.7) | collective-permute-done | bytes 65568 | tf_op jit(solution)/shard_map/ppermute | solution.py:576
  94.3 2.4 %shard_map.212 = (bf16[512,512]{1,0:T(8,128)(2,1)S(1)}, bf16[512,512]{1,0:T(8,128)(2,1)S(1)}, bf16[512,512]{1,0:T(8,128)(2,1)S(1)}, bf16[512,512]{1,0:T(8,128)(2,1)S(1)}) custom-call(f32[1,1024]{1,0:T(1,128)S(1)} %copy-done.12, f32[8,256]{1,0:T(8,128)S(1)} %copy-done.11, f32[128,256]{1,0:T(8,128)S(1)} %copy-done.2, f32[8,128]{1,0:T(8,128)S(1)} %copy-done.15, ...), custom_call_target="tpu_custom_call" | custom-call | flops 4194304 | bytes 2097152 | tf_op jit(solution)/shard_map/pallas_call | solution.py:110
  96.7 0.0 copy-start.3
  96.7 0.0 copy-start.4
  96.7 0.0 copy-start.7
  96.8 1.5 %lat_apply.3 = (f32[128,128]{1,0:T(8,128)S(1)}, f32[128,128]{1,0:T(8,128)S(1)}, f32[128,128]{1,0:T(8,128)S(1)}, f32[128,128]{1,0:T(8,128)S(1)}, f32[128,128]{1,0...) custom-call(s32[2]{0:T(128)S(1)} %pad_add_fusion.here_ref, ...), custom_call_target="tpu_custom_call" | custom-call | flops 402653184 | bytes 2097152 | tf_op jit(solution)/shard_map/lat_apply/pallas_call | solution.py:478
  98.2 0.5 collective-permute-start.28
  98.8 2.2 %collective-permute-start.30 = (f32[128,128]{1,0:T(8,128)S(1)}, f32[128,128]{1,0:T(8,128)S(1)}, u32[]{:S(2)}, u32[]{:S(2)}) collective-permute-start(f32[128,128]{1,0:T(8,128)S(1)} %get-tuple-element.109), channel_id=1, source_target_pairs={{0,3},{1,4},{2,5},{3,6},{4,7},{5,0},{6,1},{7,2},{8,11},{9,12},{10,... | collective-permute-start | bytes 196616 | tf_op jit(solution)/shard_map/ppermute | solution.py:576
  101.0 1.6 %collective-permute-start.31 = (f32[128,128]{1,0:T(8,128)S(1)}, f32[128,128]{1,0:T(8,128)S(1)}, u32[]{:S(2)}, u32[]{:S(2)}) collective-permute-start(f32[128,128]{1,0:T(8,128)S(1)} %get-tuple-element.110), channel_id=1, source_target_pairs={{0,4},{1,5},{2,6},{3,7},{4,0},{5,1},{6,2},{7,3},{8,12},{9,13},{10,... | collective-permute-start | bytes 196616 | tf_op jit(solution)/shard_map/ppermute | solution.py:576
  102.6 1.4 %lat_apply.2 = (f32[128,128]{1,0:T(8,128)S(1)}, f32[128,128]{1,0:T(8,128)S(1)}, f32[128,128]{1,0:T(8,128)S(1)}, f32[128,128]{1,0:T(8,128)S(1)}, f32[128,128]{1,0...) custom-call(s32[2]{0:T(128)S(1)} %pad_add_fusion.here_ref, ...), custom_call_target="tpu_custom_call" | custom-call | flops 402653184 | bytes 2097152 | tf_op jit(solution)/shard_map/lat_apply/pallas_call | solution.py:478
  104.0 0.9 collective-permute-start.32
  104.9 1.9 %collective-permute-start.33 = (f32[128,128]{1,0:T(8,128)S(1)}, f32[128,128]{1,0:T(8,128)S(1)}, u32[]{:S(2)}, u32[]{:S(2)}) collective-permute-start(f32[128,128]{1,0:T(8,128)S(1)} %get-tuple-element.112), channel_id=1, source_target_pairs={{0,6},{1,7},{2,0},{3,1},{4,2},{5,3},{6,4},{7,5},{8,14},{9,15},{10,... | collective-permute-start | bytes 196616 | tf_op jit(solution)/shard_map/ppermute | solution.py:576
  106.8 0.3 collective-permute-start.34
  107.1 3.0 %collective-permute-done.30.refs_3_ = f32[128,128]{1,0:T(8,128)S(1)} collective-permute-done((f32[128,128]{1,0:T(8,128)S(1)}, f32[128,128]{1,0:T(8,128)S(1)}, u32[]{:S(2)}, u32[]{:S(2)}) %collective-permute-start.30) | collective-permute-done | bytes 65568 | tf_op jit(solution)/shard_map/ppermute | solution.py:576
  110.1 0.2 collective-permute-done.31.refs_4_
  110.4 4.8 %shard_map.213 = (bf16[1024,1024]{1,0:T(8,128)(2,1)S(1)}, bf16[1024,1024]{1,0:T(8,128)(2,1)S(1)}, bf16[1024,1024]{1,0:T(8,128)(2,1)S(1)}, bf16[1024,1024]{1,0:T(8,128)(2,1)S(1)}) custom-call(f32[1,2048]{1,0:T(1,128)S(1)} %copy-done.6, f32[16,256]{1,0:T(8,128)S(1)} %copy-done.5, f32[128,256]{1,0:T(8,128)S(1)} %copy-done.3, f32[16,128]{1,0:T(8,128)S(1)} %copy-done.9, ...), custom_call_target="tpu_custom_call" | custom-call | flops 16777216 | bytes 8388608 | tf_op jit(solution)/shard_map/pallas_call | solution.py:110
  115.2 2.2 %new_multipliers.1 = f32[128,2048]{1,0:T(8,128)} custom-call(s32[2]{0:T(128)S(1)} %pad_add_fusion.here_ref, f32[128,2048]{1,0:T(8,128)S(1)} %get-tuple-element.59.own_ref, f32[128,1024]{1,0:T(8,128)S(1)} %collective-permute-done.35.plus_ref, f32[128,1024]{1,0:T(8,128)S(1)} %collective-permute-done.36.minus_ref, ...), custom_call_target="tpu_custom_call" | custom-call | flops 1572864 | bytes 5242880 | tf_op jit(solution)/shard_map/new_multipliers/pallas_call | solution.py:559
  117.4 0.7 collective-permute-start.14
  118.1 4.0 %collective-permute-start.15 = (f32[128,128]{1,0:T(8,128)S(1)}, f32[128,128]{1,0:T(8,128)S(1)}, u32[]{:S(2)}, u32[]{:S(2)}) collective-permute-start(f32[128,128]{1,0:T(8,128)S(1)} %get-tuple-element.89), channel_id=1, source_target_pairs={{0,4},{1,5},{2,6},{3,7},{4,0},{5,1},{6,2},{7,3},{8,12},{9,13},{10,... | collective-permute-start | bytes 196616 | tf_op jit(solution)/shard_map/ppermute | solution.py:576
  122.1 1.7 %collective-permute-start.16 = (f32[128,128]{1,0:T(8,128)S(1)}, f32[128,128]{1,0:T(8,128)S(1)}, u32[]{:S(2)}, u32[]{:S(2)}) collective-permute-start(f32[128,128]{1,0:T(8,128)S(1)} %get-tuple-element.90), channel_id=1, source_target_pairs={{0,5},{1,6},{2,7},{3,0},{4,1},{5,2},{6,3},{7,4},{8,13},{9,14},{10,... | collective-permute-start | bytes 196616 | tf_op jit(solution)/shard_map/ppermute | solution.py:576
  123.9 0.4 collective-permute-start.17
  124.3 0.8 collective-permute-start.18
  125.1 1.7 %lon_apply.2.refs_10_ = f32[128,1024]{1,0:T(8,128)S(1)} custom-call(s32[2]{0:T(128)S(1)} %pad_add_fusion.here_ref, f32[128,128]{1,0:T(8,128)S(1)} %get-tuple-element.106.refs_0_, f32[128,128]{1,0:T(8,128)S(1)} %collective-permute-done.28.refs_1_, f32[128,128]{1,0:T(8,128)S(1)} %collective-permute-done.29.refs_2_, ...), custom_call_target="tpu_custom_call" | custom-call | flops 805306368 | bytes 4194304 | tf_op jit(solution)/shard_map/lon_apply/pallas_call | solution.py:530
  126.8 2.3 %collective-permute-done.17.refs_6_ = f32[128,128]{1,0:T(8,128)S(1)} collective-permute-done((f32[128,128]{1,0:T(8,128)S(1)}, f32[128,128]{1,0:T(8,128)S(1)}, u32[]{:S(2)}, u32[]{:S(2)}) %collective-permute-start.17) | collective-permute-done | bytes 65568 | tf_op jit(solution)/shard_map/ppermute | solution.py:576
  129.2 2.7 %lon_apply.3 = f32[128,2048]{1,0:T(8,128)} custom-call(s32[2]{0:T(128)S(1)} %pad_add_fusion.here_ref, f32[128,128]{1,0:T(8,128)S(1)} %get-tuple-element.85.refs_0_, f32[128,128]{1,0:T(8,128)S(1)} %collective-permute-done.12.refs_1_, f32[128,128]{1,0:T(8,128)S(1)} %collective-permute-done.13.refs_2_, f32[128,128]{1,0:T(8,128)S(1)} %collective-permute-done.14.refs_3_, ...), custom_call_target="tpu_custom_call" | custom-call | flops 805306368 | bytes 4194304 | tf_op jit(solution)/shard_map/lon_apply/pallas_call | solution.py:530
  (58 shorter events, 0.2 us)
Async XLA Ops:
  1.5 10.6 %collective-permute-start.1 = (f32[2,2048]{1,0:T(2,128)S(1)}, f32[2,2048]{1,0:T(2,128)S(1)}, u32[]{:S(2)}, u32[]{:S(2)}) collective-permute-start(f32[2,2048]{1,0:T(2,128)S(1)} %get-tuple-element.116), channel_id=1, source_target_pairs={{1,0},{2,1},{3,2},{4,3},{5,4},{6,5},{7,6},{9,8},{10,9},{11,10},{12... | collective-permute-start | bytes 49160 | tf_op jit(solution)/shard_map/ppermute | solution.py:607
  2.8 9.3 %collective-permute-start = (f32[2,2048]{1,0:T(2,128)S(1)}, f32[2,2048]{1,0:T(2,128)S(1)}, u32[]{:S(2)}, u32[]{:S(2)}) collective-permute-start(f32[2,2048]{1,0:T(2,128)S(1)} %get-tuple-element.117), channel_id=1, source_target_pairs={{0,1},{1,2},{2,3},{3,4},{4,5},{5,6},{6,7},{8,9},{9,10},{10,11},{11... | collective-permute-start | bytes 49160 | tf_op jit(solution)/shard_map/ppermute | solution.py:606
  12.1 10.2 %copy-start = (f32[1,2,1,128,2048]{4,3,2,1,0:T(8,128)S(1)}, f32[1,2,1,128,2048]{4,3,2,1,0:T(8,128)}, u32[]{:S(2)}) copy-start(f32[1,2,1,128,2048]{4,3,2,1,0:T(8,128)} %param.23) | copy-start | bytes 6291460
  12.1 10.2 %copy-start.1 = (s32[1,2,128,2048]{3,2,1,0:T(8,128)S(1)}, s32[1,2,128,2048]{3,2,1,0:T(8,128)}, u32[]{:S(2)}) copy-start(s32[1,2,128,2048]{3,2,1,0:T(8,128)} %param.24) | copy-start | bytes 6291460
  13.9 16.9 %collective-permute-start.19 = (f32[128,1024]{1,0:T(8,128)S(1)}, f32[128,1024]{1,0:T(8,128)S(1)}, u32[]{:S(2)}, u32[]{:S(2)}) collective-permute-start(f32[128,1024]{1,0:T(8,128)S(1)} %get-tuple-element.96), channel_id=1, source_target_pairs={{0,8},{8,0},{16,24},{1,9},{9,1},{17,25},{2,10},{10,2},{18,26},{3,1... | collective-permute-start | bytes 1572872 | tf_op jit(solution)/shard_map/ppermute | solution.py:581
  18.8 16.1 %collective-permute-start.2 = (f32[128,1024]{1,0:T(8,128)S(1)}, f32[128,1024]{1,0:T(8,128)S(1)}, u32[]{:S(2)}, u32[]{:S(2)}) collective-permute-start(f32[128,1024]{1,0:T(8,128)S(1)} %get-tuple-element.70), channel_id=1, source_target_pairs={{0,16},{8,24},{1,17},{9,25},{2,18},{10,26},{3,19},{11,27},{4,20},{... | collective-permute-start | bytes 1572872 | tf_op jit(solution)/shard_map/ppermute | solution.py:581
  31.5 37.6 %collective-permute-start.20 = (f32[128,1024]{1,0:T(8,128)S(1)}, f32[128,1024]{1,0:T(8,128)S(1)}, u32[]{:S(2)}, u32[]{:S(2)}) collective-permute-start(f32[128,1024]{1,0:T(8,128)S(1)} %mix.3), channel_id=1, source_target_pairs={{0,16},{8,24},{1,17},{9,25},{2,18},{10,26},{3,19},{11,27},{4,20},{... | collective-permute-start | bytes 1572872 | tf_op jit(solution)/shard_map/ppermute | solution.py:581
  35.5 33.5 %collective-permute-start.3 = (f32[128,1024]{1,0:T(8,128)S(1)}, f32[128,1024]{1,0:T(8,128)S(1)}, u32[]{:S(2)}, u32[]{:S(2)}) collective-permute-start(f32[128,1024]{1,0:T(8,128)S(1)} %mix.2), channel_id=1, source_target_pairs={{0,8},{16,24},{24,16},{1,9},{17,25},{25,17},{2,10},{18,26},{26,18}... | collective-permute-start | bytes 1572872 | tf_op jit(solution)/shard_map/ppermute | solution.py:581
  40.0 31.7 %collective-permute-start.35 = (f32[128,1024]{1,0:T(8,128)S(1)}, f32[128,1024]{1,0:T(8,128)S(1)}, u32[]{:S(2)}, u32[]{:S(2)}) collective-permute-start(f32[128,1024]{1,0:T(8,128)S(1)} %get-tuple-element.67.plus_ref), channel_id=1, source_target_pairs={{8,16},{16,24},{9,17},{17,25},{10,18},{18,26},{11,19},{19,27},{12,... | collective-permute-start | bytes 1572872 | tf_op jit(solution)/shard_map/ppermute | solution.py:581
  40.7 32.2 %collective-permute-start.4 = (f32[128,1024]{1,0:T(8,128)S(1)}, f32[128,1024]{1,0:T(8,128)S(1)}, u32[]{:S(2)}, u32[]{:S(2)}) collective-permute-start(f32[128,1024]{1,0:T(8,128)S(1)} %get-tuple-element.72), channel_id=1, source_target_pairs={{0,8},{8,24},{1,9},{9,25},{2,10},{10,26},{3,11},{11,27},{4,12},{12... | collective-permute-start | bytes 1572872 | tf_op jit(solution)/shard_map/ppermute | solution.py:581
  44.9 59.2 %collective-permute-start.36 = (f32[128,1024]{1,0:T(8,128)S(1)}, f32[128,1024]{1,0:T(8,128)S(1)}, u32[]{:S(2)}, u32[]{:S(2)}) collective-permute-start(f32[128,1024]{1,0:T(8,128)S(1)} %get-tuple-element.68.minus_ref), channel_id=1, source_target_pairs={{0,8},{8,16},{16,24},{1,9},{9,17},{17,25},{2,10},{10,18},{18,26},{... | collective-permute-start | bytes 1572872 | tf_op jit(solution)/shard_map/ppermute | solution.py:581
  69.0 25.2 %copy-start.2 = (f32[128,256]{1,0:T(8,128)S(1)}, f32[128,256]{1,0:T(8,128)}, u32[]{:S(2)}) copy-start(f32[128,256]{1,0:T(8,128)} %constant.33.clone.middle_ref) | copy-start | bytes 393220
  69.0 25.2 %copy-start.10 = (f32[8,256]{1,0:T(8,128)S(1)}, f32[8,256]{1,0:T(8,128)}, u32[]{:S(2)}) copy-start(f32[8,256]{1,0:T(8,128)} %constant.35.clone.twist_ref) | copy-start | bytes 24580
  69.0 25.2 %copy-start.11 = (f32[8,256]{1,0:T(8,128)S(1)}, f32[8,256]{1,0:T(8,128)}, u32[]{:S(2)}) copy-start(f32[8,256]{1,0:T(8,128)} %constant.32.clone.inner_ref) | copy-start | bytes 24580
  69.0 25.2 %copy-start.12 = (f32[1,1024]{1,0:T(1,128)S(1)}, f32[1,1024]{1,0:T(1,128)}, u32[]{:S(2)}) copy-start(f32[1,1024]{1,0:T(1,128)} %d_ref.2) | copy-start | bytes 12292
  69.1 25.2 %copy-start.13 = (f32[8,8]{1,0:T(8,128)S(1)}, f32[8,8]{1,0:T(8,128)}, u32[]{:S(2)}) copy-start(f32[8,8]{1,0:T(8,128)} %constant.37.clone.sin_ref) | copy-start | bytes 772
  69.1 25.2 %copy-start.14 = (f32[8,8]{1,0:T(8,128)S(1)}, f32[8,8]{1,0:T(8,128)}, u32[]{:S(2)}) copy-start(f32[8,8]{1,0:T(8,128)} %constant.36.clone.cos_ref) | copy-start | bytes 772
  69.1 25.2 %copy-start.15 = (f32[8,128]{1,0:T(8,128)S(1)}, f32[8,128]{1,0:T(8,128)}, u32[]{:S(2)}) copy-start(f32[8,128]{1,0:T(8,128)} %constant.34.clone.member_ref) | copy-start | bytes 12292
  69.9 5.6 %collective-permute-start.21 = (f32[128,128]{1,0:T(8,128)S(1)}, f32[128,128]{1,0:T(8,128)S(1)}, u32[]{:S(2)}, u32[]{:S(2)}) collective-permute-start(f32[128,128]{1,0:T(8,128)S(1)} %get-tuple-element.99), channel_id=1, source_target_pairs={{0,1},{1,2},{2,3},{3,4},{4,5},{5,6},{6,7},{7,0},{8,9},{9,10},{10,1... | collective-permute-start | bytes 196616 | tf_op jit(solution)/shard_map/ppermute | solution.py:576
  70.0 6.4 %collective-permute-start.22 = (f32[128,128]{1,0:T(8,128)S(1)}, f32[128,128]{1,0:T(8,128)S(1)}, u32[]{:S(2)}, u32[]{:S(2)}) collective-permute-start(f32[128,128]{1,0:T(8,128)S(1)} %get-tuple-element.100), channel_id=1, source_target_pairs={{0,2},{1,3},{2,4},{3,5},{4,6},{5,7},{6,0},{7,1},{8,10},{9,11},{10,... | collective-permute-start | bytes 196616 | tf_op jit(solution)/shard_map/ppermute | solution.py:576
  71.6 10.1 %collective-permute-start.23 = (f32[128,128]{1,0:T(8,128)S(1)}, f32[128,128]{1,0:T(8,128)S(1)}, u32[]{:S(2)}, u32[]{:S(2)}) collective-permute-start(f32[128,128]{1,0:T(8,128)S(1)} %get-tuple-element.101), channel_id=1, source_target_pairs={{0,3},{1,4},{2,5},{3,6},{4,7},{5,0},{6,1},{7,2},{8,11},{9,12},{10,... | collective-permute-start | bytes 196616 | tf_op jit(solution)/shard_map/ppermute | solution.py:576
  72.9 9.0 %collective-permute-start.24 = (f32[128,128]{1,0:T(8,128)S(1)}, f32[128,128]{1,0:T(8,128)S(1)}, u32[]{:S(2)}, u32[]{:S(2)}) collective-permute-start(f32[128,128]{1,0:T(8,128)S(1)} %get-tuple-element.102), channel_id=1, source_target_pairs={{0,4},{1,5},{2,6},{3,7},{4,0},{5,1},{6,2},{7,3},{8,12},{9,13},{10,... | collective-permute-start | bytes 196616 | tf_op jit(solution)/shard_map/ppermute | solution.py:576
  75.5 7.4 %collective-permute-start.25 = (f32[128,128]{1,0:T(8,128)S(1)}, f32[128,128]{1,0:T(8,128)S(1)}, u32[]{:S(2)}, u32[]{:S(2)}) collective-permute-start(f32[128,128]{1,0:T(8,128)S(1)} %get-tuple-element.103), channel_id=1, source_target_pairs={{0,5},{1,6},{2,7},{3,0},{4,1},{5,2},{6,3},{7,4},{8,13},{9,14},{10,... | collective-permute-start | bytes 196616 | tf_op jit(solution)/shard_map/ppermute | solution.py:576
  76.4 8.7 %collective-permute-start.26 = (f32[128,128]{1,0:T(8,128)S(1)}, f32[128,128]{1,0:T(8,128)S(1)}, u32[]{:S(2)}, u32[]{:S(2)}) collective-permute-start(f32[128,128]{1,0:T(8,128)S(1)} %get-tuple-element.104), channel_id=1, source_target_pairs={{0,6},{1,7},{2,0},{3,1},{4,2},{5,3},{6,4},{7,5},{8,14},{9,15},{10,... | collective-permute-start | bytes 196616 | tf_op jit(solution)/shard_map/ppermute | solution.py:576
  81.7 5.1 %collective-permute-start.27 = (f32[128,128]{1,0:T(8,128)S(1)}, f32[128,128]{1,0:T(8,128)S(1)}, u32[]{:S(2)}, u32[]{:S(2)}) collective-permute-start(f32[128,128]{1,0:T(8,128)S(1)} %get-tuple-element.105), channel_id=1, source_target_pairs={{0,7},{1,0},{2,1},{3,2},{4,3},{5,4},{6,5},{7,6},{8,15},{9,8},{10,9... | collective-permute-start | bytes 196616 | tf_op jit(solution)/shard_map/ppermute | solution.py:576
  81.9 6.0 %collective-permute-start.5 = (f32[128,128]{1,0:T(8,128)S(1)}, f32[128,128]{1,0:T(8,128)S(1)}, u32[]{:S(2)}, u32[]{:S(2)}) collective-permute-start(f32[128,128]{1,0:T(8,128)S(1)} %get-tuple-element.74), channel_id=1, source_target_pairs={{0,1},{1,2},{2,3},{3,4},{4,5},{5,6},{6,7},{7,0},{8,9},{9,10},{10,1... | collective-permute-start | bytes 196616 | tf_op jit(solution)/shard_map/ppermute | solution.py:576
  82.9 6.8 %collective-permute-start.6 = (f32[128,128]{1,0:T(8,128)S(1)}, f32[128,128]{1,0:T(8,128)S(1)}, u32[]{:S(2)}, u32[]{:S(2)}) collective-permute-start(f32[128,128]{1,0:T(8,128)S(1)} %get-tuple-element.75), channel_id=1, source_target_pairs={{0,2},{1,3},{2,4},{3,5},{4,6},{5,7},{6,0},{7,1},{8,10},{9,11},{10,... | collective-permute-start | bytes 196616 | tf_op jit(solution)/shard_map/ppermute | solution.py:576
  85.1 9.2 %collective-permute-start.7 = (f32[128,128]{1,0:T(8,128)S(1)}, f32[128,128]{1,0:T(8,128)S(1)}, u32[]{:S(2)}, u32[]{:S(2)}) collective-permute-start(f32[128,128]{1,0:T(8,128)S(1)} %get-tuple-element.76), channel_id=1, source_target_pairs={{0,3},{1,4},{2,5},{3,6},{4,7},{5,0},{6,1},{7,2},{8,11},{9,12},{10,... | collective-permute-start | bytes 196616 | tf_op jit(solution)/shard_map/ppermute | solution.py:576
  86.8 11.4 %collective-permute-start.8 = (f32[128,128]{1,0:T(8,128)S(1)}, f32[128,128]{1,0:T(8,128)S(1)}, u32[]{:S(2)}, u32[]{:S(2)}) collective-permute-start(f32[128,128]{1,0:T(8,128)S(1)} %get-tuple-element.77), channel_id=1, source_target_pairs={{0,4},{1,5},{2,6},{3,7},{4,0},{5,1},{6,2},{7,3},{8,12},{9,13},{10,... | collective-permute-start | bytes 196616 | tf_op jit(solution)/shard_map/ppermute | solution.py:576
  87.9 10.9 %collective-permute-start.9 = (f32[128,128]{1,0:T(8,128)S(1)}, f32[128,128]{1,0:T(8,128)S(1)}, u32[]{:S(2)}, u32[]{:S(2)}) collective-permute-start(f32[128,128]{1,0:T(8,128)S(1)} %get-tuple-element.78), channel_id=1, source_target_pairs={{0,5},{1,6},{2,7},{3,0},{4,1},{5,2},{6,3},{7,4},{8,13},{9,14},{10,... | collective-permute-start | bytes 196616 | tf_op jit(solution)/shard_map/ppermute | solution.py:576
  89.8 9.0 %collective-permute-start.10 = (f32[128,128]{1,0:T(8,128)S(1)}, f32[128,128]{1,0:T(8,128)S(1)}, u32[]{:S(2)}, u32[]{:S(2)}) collective-permute-start(f32[128,128]{1,0:T(8,128)S(1)} %get-tuple-element.79), channel_id=1, source_target_pairs={{0,6},{1,7},{2,0},{3,1},{4,2},{5,3},{6,4},{7,5},{8,14},{9,15},{10,... | collective-permute-start | bytes 196616 | tf_op jit(solution)/shard_map/ppermute | solution.py:576
  94.2 6.7 %collective-permute-start.11 = (f32[128,128]{1,0:T(8,128)S(1)}, f32[128,128]{1,0:T(8,128)S(1)}, u32[]{:S(2)}, u32[]{:S(2)}) collective-permute-start(f32[128,128]{1,0:T(8,128)S(1)} %get-tuple-element.80), channel_id=1, source_target_pairs={{0,7},{1,0},{2,1},{3,2},{4,3},{5,4},{6,5},{7,6},{8,15},{9,8},{10,9... | collective-permute-start | bytes 196616 | tf_op jit(solution)/shard_map/ppermute | solution.py:576
  96.7 13.6 %copy-start.3 = (f32[128,256]{1,0:T(8,128)S(1)}, f32[128,256]{1,0:T(8,128)}, u32[]{:S(2)}) copy-start(f32[128,256]{1,0:T(8,128)} %constant.39.clone.middle_ref) | copy-start | bytes 393220
  96.7 13.6 %copy-start.4 = (f32[16,256]{1,0:T(8,128)S(1)}, f32[16,256]{1,0:T(8,128)}, u32[]{:S(2)}) copy-start(f32[16,256]{1,0:T(8,128)} %constant.41.clone.twist_ref) | copy-start | bytes 49156
  96.7 13.6 %copy-start.5 = (f32[16,256]{1,0:T(8,128)S(1)}, f32[16,256]{1,0:T(8,128)}, u32[]{:S(2)}) copy-start(f32[16,256]{1,0:T(8,128)} %constant.38.clone.inner_ref) | copy-start | bytes 49156
  96.7 13.6 %copy-start.6 = (f32[1,2048]{1,0:T(1,128)S(1)}, f32[1,2048]{1,0:T(1,128)}, u32[]{:S(2)}) copy-start(f32[1,2048]{1,0:T(1,128)} %d_ref.3) | copy-start | bytes 24580
  96.7 13.6 %copy-start.7 = (f32[16,16]{1,0:T(8,128)S(1)}, f32[16,16]{1,0:T(8,128)}, u32[]{:S(2)}) copy-start(f32[16,16]{1,0:T(8,128)} %constant.43.clone.sin_ref) | copy-start | bytes 3076
  96.7 13.6 %copy-start.8 = (f32[16,16]{1,0:T(8,128)S(1)}, f32[16,16]{1,0:T(8,128)}, u32[]{:S(2)}) copy-start(f32[16,16]{1,0:T(8,128)} %constant.42.clone.cos_ref) | copy-start | bytes 3076
  96.8 13.6 %copy-start.9 = (f32[16,128]{1,0:T(8,128)S(1)}, f32[16,128]{1,0:T(8,128)}, u32[]{:S(2)}) copy-start(f32[16,128]{1,0:T(8,128)} %constant.40.clone.member_ref) | copy-start | bytes 24580
  98.2 6.7 %collective-permute-start.28 = (f32[128,128]{1,0:T(8,128)S(1)}, f32[128,128]{1,0:T(8,128)S(1)}, u32[]{:S(2)}, u32[]{:S(2)}) collective-permute-start(f32[128,128]{1,0:T(8,128)S(1)} %get-tuple-element.107), channel_id=1, source_target_pairs={{0,1},{1,2},{2,3},{3,4},{4,5},{5,6},{6,7},{7,0},{8,9},{9,10},{10,1... | collective-permute-start | bytes 196616 | tf_op jit(solution)/shard_map/ppermute | solution.py:576
  98.8 8.0 %collective-permute-start.29 = (f32[128,128]{1,0:T(8,128)S(1)}, f32[128,128]{1,0:T(8,128)S(1)}, u32[]{:S(2)}, u32[]{:S(2)}) collective-permute-start(f32[128,128]{1,0:T(8,128)S(1)} %get-tuple-element.108), channel_id=1, source_target_pairs={{0,2},{1,3},{2,4},{3,5},{4,6},{5,7},{6,0},{7,1},{8,10},{9,11},{10,... | collective-permute-start | bytes 196616 | tf_op jit(solution)/shard_map/ppermute | solution.py:576
  98.8 11.3 %collective-permute-start.30 = (f32[128,128]{1,0:T(8,128)S(1)}, f32[128,128]{1,0:T(8,128)S(1)}, u32[]{:S(2)}, u32[]{:S(2)}) collective-permute-start(f32[128,128]{1,0:T(8,128)S(1)} %get-tuple-element.109), channel_id=1, source_target_pairs={{0,3},{1,4},{2,5},{3,6},{4,7},{5,0},{6,1},{7,2},{8,11},{9,12},{10,... | collective-permute-start | bytes 196616 | tf_op jit(solution)/shard_map/ppermute | solution.py:576
  101.0 9.3 %collective-permute-start.31 = (f32[128,128]{1,0:T(8,128)S(1)}, f32[128,128]{1,0:T(8,128)S(1)}, u32[]{:S(2)}, u32[]{:S(2)}) collective-permute-start(f32[128,128]{1,0:T(8,128)S(1)} %get-tuple-element.110), channel_id=1, source_target_pairs={{0,4},{1,5},{2,6},{3,7},{4,0},{5,1},{6,2},{7,3},{8,12},{9,13},{10,... | collective-permute-start | bytes 196616 | tf_op jit(solution)/shard_map/ppermute | solution.py:576
  104.0 13.3 %collective-permute-start.32 = (f32[128,128]{1,0:T(8,128)S(1)}, f32[128,128]{1,0:T(8,128)S(1)}, u32[]{:S(2)}, u32[]{:S(2)}) collective-permute-start(f32[128,128]{1,0:T(8,128)S(1)} %get-tuple-element.111), channel_id=1, source_target_pairs={{0,5},{1,6},{2,7},{3,0},{4,1},{5,2},{6,3},{7,4},{8,13},{9,14},{10,... | collective-permute-start | bytes 196616 | tf_op jit(solution)/shard_map/ppermute | solution.py:576
  104.9 13.1 %collective-permute-start.33 = (f32[128,128]{1,0:T(8,128)S(1)}, f32[128,128]{1,0:T(8,128)S(1)}, u32[]{:S(2)}, u32[]{:S(2)}) collective-permute-start(f32[128,128]{1,0:T(8,128)S(1)} %get-tuple-element.112), channel_id=1, source_target_pairs={{0,6},{1,7},{2,0},{3,1},{4,2},{5,3},{6,4},{7,5},{8,14},{9,15},{10,... | collective-permute-start | bytes 196616 | tf_op jit(solution)/shard_map/ppermute | solution.py:576
  106.8 15.3 %collective-permute-start.34 = (f32[128,128]{1,0:T(8,128)S(1)}, f32[128,128]{1,0:T(8,128)S(1)}, u32[]{:S(2)}, u32[]{:S(2)}) collective-permute-start(f32[128,128]{1,0:T(8,128)S(1)} %get-tuple-element.113), channel_id=1, source_target_pairs={{0,7},{1,0},{2,1},{3,2},{4,3},{5,4},{6,5},{7,6},{8,15},{9,8},{10,9... | collective-permute-start | bytes 196616 | tf_op jit(solution)/shard_map/ppermute | solution.py:576
  110.1 13.8 %collective-permute-start.12 = (f32[128,128]{1,0:T(8,128)S(1)}, f32[128,128]{1,0:T(8,128)S(1)}, u32[]{:S(2)}, u32[]{:S(2)}) collective-permute-start(f32[128,128]{1,0:T(8,128)S(1)} %get-tuple-element.86), channel_id=1, source_target_pairs={{0,1},{1,2},{2,3},{3,4},{4,5},{5,6},{6,7},{7,0},{8,9},{9,10},{10,1... | collective-permute-start | bytes 196616 | tf_op jit(solution)/shard_map/ppermute | solution.py:576
  110.3 14.0 %collective-permute-start.13 = (f32[128,128]{1,0:T(8,128)S(1)}, f32[128,128]{1,0:T(8,128)S(1)}, u32[]{:S(2)}, u32[]{:S(2)}) collective-permute-start(f32[128,128]{1,0:T(8,128)S(1)} %get-tuple-element.87), channel_id=1, source_target_pairs={{0,2},{1,3},{2,4},{3,5},{4,6},{5,7},{6,0},{7,1},{8,10},{9,11},{10,... | collective-permute-start | bytes 196616 | tf_op jit(solution)/shard_map/ppermute | solution.py:576
  117.4 9.4 %collective-permute-start.14 = (f32[128,128]{1,0:T(8,128)S(1)}, f32[128,128]{1,0:T(8,128)S(1)}, u32[]{:S(2)}, u32[]{:S(2)}) collective-permute-start(f32[128,128]{1,0:T(8,128)S(1)} %get-tuple-element.88), channel_id=1, source_target_pairs={{0,3},{1,4},{2,5},{3,6},{4,7},{5,0},{6,1},{7,2},{8,11},{9,12},{10,... | collective-permute-start | bytes 196616 | tf_op jit(solution)/shard_map/ppermute | solution.py:576
  118.1 8.7 %collective-permute-start.15 = (f32[128,128]{1,0:T(8,128)S(1)}, f32[128,128]{1,0:T(8,128)S(1)}, u32[]{:S(2)}, u32[]{:S(2)}) collective-permute-start(f32[128,128]{1,0:T(8,128)S(1)} %get-tuple-element.89), channel_id=1, source_target_pairs={{0,4},{1,5},{2,6},{3,7},{4,0},{5,1},{6,2},{7,3},{8,12},{9,13},{10,... | collective-permute-start | bytes 196616 | tf_op jit(solution)/shard_map/ppermute | solution.py:576
  122.1 4.7 %collective-permute-start.16 = (f32[128,128]{1,0:T(8,128)S(1)}, f32[128,128]{1,0:T(8,128)S(1)}, u32[]{:S(2)}, u32[]{:S(2)}) collective-permute-start(f32[128,128]{1,0:T(8,128)S(1)} %get-tuple-element.90), channel_id=1, source_target_pairs={{0,5},{1,6},{2,7},{3,0},{4,1},{5,2},{6,3},{7,4},{8,13},{9,14},{10,... | collective-permute-start | bytes 196616 | tf_op jit(solution)/shard_map/ppermute | solution.py:576
  123.9 5.3 %collective-permute-start.17 = (f32[128,128]{1,0:T(8,128)S(1)}, f32[128,128]{1,0:T(8,128)S(1)}, u32[]{:S(2)}, u32[]{:S(2)}) collective-permute-start(f32[128,128]{1,0:T(8,128)S(1)} %get-tuple-element.91), channel_id=1, source_target_pairs={{0,6},{1,7},{2,0},{3,1},{4,2},{5,3},{6,4},{7,5},{8,14},{9,15},{10,... | collective-permute-start | bytes 196616 | tf_op jit(solution)/shard_map/ppermute | solution.py:576
  124.3 4.9 %collective-permute-start.18 = (f32[128,128]{1,0:T(8,128)S(1)}, f32[128,128]{1,0:T(8,128)S(1)}, u32[]{:S(2)}, u32[]{:S(2)}) collective-permute-start(f32[128,128]{1,0:T(8,128)S(1)} %get-tuple-element.92), channel_id=1, source_target_pairs={{0,7},{1,0},{2,1},{3,2},{4,3},{5,4},{6,5},{7,6},{8,15},{9,8},{10,9... | collective-permute-start | bytes 196616 | tf_op jit(solution)/shard_map/ppermute | solution.py:576

commit v2 on v1

--- a/solution.py
+++ b/solution.py
@@ -62,37 +62,37 @@
     gc, gs = g[:, :LANES], g[:, LANES:]
     c = mm(cos_ref[...], gc) - mm(sin_ref[...], gs)
     s = mm(sin_ref[...], gc) + mm(cos_ref[...], gs)
-    rows = lax.broadcasted_iota(jnp.int32, (LANES, LANES), 0)
-    cols = lax.broadcasted_iota(jnp.int32, (LANES, LANES), 1)
-    flip = jnp.where(rows + cols == LANES - 1, 1.0, 0.0)
+    upside_down = ROWS - 1 - lax.broadcasted_iota(jnp.int32, (ROWS, LANES), 0)
+    ahead = (lax.broadcasted_iota(jnp.int32, (LANES, LANES), 1)
+             - lax.broadcasted_iota(jnp.int32, (LANES, LANES), 0))
     for part in range(2):
         wrap = 1.0 if part == 0 else -1.0
         hi_ref, lo_ref = (even_hi, even_lo) if part == 0 else (odd_hi, odd_lo)
 
-        def row(table, at):
-            sign = 1.0
-            if at < 0 or at >= blocks:
-                sign, at = wrap, at % blocks
+        def sheared(table, at, shift):
             at += part * blocks
-            return sign * table[at:at + 1]
-
+            return pltpu.roll(jnp.broadcast_to(table[at:at + 1], (LANES, LANES)), shift, 1, stride=1, stride_axis=0)
+
+        before = wrap * sheared(c, blocks - 1, 0)
         for b in range(blocks):
-            window = jnp.concatenate([row(c, b - 1), row(c, b)], axis=1)
-            window = jnp.broadcast_to(window, (LANES, 2 * LANES))
-            toep[b] = pltpu.roll(window, 0, 1, stride=1, stride_axis=0)[:, LANES:]
-            window = jnp.concatenate([row(s, b), row(s, b + 1)], axis=1)
-            window = jnp.broadcast_to(window, (LANES, 2 * LANES))
-            window = pltpu.roll(window, LANES + 1, 1, stride=1, stride_axis=0)[:, :LANES]
-            hank[b] = mm(flip, window)
+            now = sheared(c, b, 0)
+            block = jnp.where(ahead >= 0, now, before)
+            toep[b] = block
+            toep[b + blocks] = wrap * block
+            before = now
+        first = now = sheared(s, 0, 1)
+        for b in range(blocks):
+            after = sheared(s, b + 1, 1) if b + 1 < blocks else wrap * first
+            block = jnp.where(ahead <= 0, now, after)
+            for at in range(0, LANES, ROWS):
+                rows = jnp.take_along_axis(block[at:at + ROWS], upside_down, axis=0)
+                hank[b, LANES - ROWS - at:LANES - at] = rows
+                hank[b + blocks, LANES - ROWS - at:LANES - at] = wrap * rows
+            now = after
 
         def body(i, _):
             for j in range(blocks):
-                t = toep[lax.rem(j - i + blocks, blocks)]
-                h = hank[lax.rem(i + j, blocks)]
-                if part == 1:
-                    t = t * jnp.where(j < i, -1.0, 1.0)
-                    h = h * jnp.where(i + j >= blocks, -1.0, 1.0)
-                a = t + h
+                a = toep[jnp.where(j < i, j - i + 2 * blocks, j - i)] + hank[i + j]
                 hi = a.astype(jnp.bfloat16)
                 at = (pl.ds(pl.multiple_of(i * LANES, LANES), LANES), pl.ds(j * LANES, LANES))
                 hi_ref[at] = hi
@@ -110,7 +110,7 @@
     return pl.pallas_call(
         functools.partial(build_kernel, count),
         out_shape=[shape] * 4, in_specs=[VMEM] * 7, out_specs=[VMEM] * 4,
-        scratch_shapes=[pltpu.VMEM((half // LANES, LANES, LANES), jnp.float32)] * 2,
+        scratch_shapes=[pltpu.VMEM((2 * half // LANES, LANES, LANES), jnp.float32)] * 2,
         compiler_params=LIMIT,
         cost_estimate=pl.CostEstimate(flops=2 * half * half * 8, bytes_accessed=8 * half * half, transcendentals=0),
     )(spectrum, *tables)
@@ -242,18 +242,19 @@
     return pick
 
 
-def windowed(weight, own, ended):
+def windowed(sign, share, own, ended):
     half = own.shape[1] // 2
-    values = (ended, weight(SIGN) * ended + weight(SHARE) * own)
+    values = (ended, sign * ended + share * own)
     return [part for value in values for part in
             (value[:, :half] + value[:, half:], value[:, :half] - value[:, half:])]
 
 
-def forecast_kernel(here_ref, speed, drift, kappa, x_hbm, mult_hbm, x_ref, own_ref, x1_ref, *refs):
+def forecast_kernel(here_ref, model, x_hbm, mult_hbm, x_ref, own_ref, x1_ref, *refs):
     outs, (mult_ref, sems) = refs[:4], refs[4:]
     band = x_ref.shape[0]
     chunk = band // 4
-    weight, scal = weight_of(here_ref), (speed[0], drift[0], kappa[0])
+    weight, scal = weight_of(here_ref), (model[0], model[1], model[2])
+    sign, share = weight(SIGN), weight(SHARE)
 
     def step(source, at, count):
         return stencil(scal, source[at:at + count], source[at + 1:at + count + 1], source[at - 1:at + count - 1])
@@ -274,22 +275,24 @@
             x1_ref[stepped:stepped + ROWS] = step(x_ref, stepped, ROWS)
             stepped += ROWS
     x1_ref[stepped:stepped + 1] = step(x_ref, stepped, 1)
+    kept = weight(OWN)
     for part in range(4):
         copies[4 + part].wait()
         for at in range(part * chunk, (part + 1) * chunk, ROWS):
             rows = slice(at, at + ROWS)
-            own = mult_ref[rows] + weight(OWN) * x_ref[rows]
+            own = mult_ref[rows] + kept * x_ref[rows]
             own_ref[rows] = own
             if 0 < at < band - ROWS:
-                for out, value in zip(outs, windowed(weight, own, 0.5 * step(x1_ref, at, ROWS))):
+                for out, value in zip(outs, windowed(sign, share, own, 0.5 * step(x1_ref, at, ROWS))):
                     out[rows] = value
 
 
-def edge_kernel(bands, here_ref, speed, drift, kappa, x_ref, own_ref, low_ref, high_ref, *refs):
+def edge_kernel(bands, here_ref, model, x_ref, own_ref, low_ref, high_ref, *refs):
     outs, (ext, mid, whole, parts, sems) = refs[5:10], refs[10:]
     band = x_ref.shape[0]
     edge = low_ref.shape[0]
-    weight, scal = weight_of(here_ref), (speed[0], drift[0], kappa[0])
+    weight, scal = weight_of(here_ref), (model[0], model[1], model[2])
+    sign, share = weight(SIGN), weight(SHARE)
     copies = []
     for end in range(2):
         at = 0 if end == 0 else band - ROWS
@@ -314,7 +317,7 @@
         mid[end, ROWS:2 * ROWS] = step(ext, ROWS, ROWS)
         rows = slice(at, at + ROWS)
         whole[end] = mid[end, ROWS:2 * ROWS]
-        for number, part in enumerate(windowed(weight, own_ref[rows], 0.5 * step(mid, ROWS, ROWS))):
+        for number, part in enumerate(windowed(sign, share, own_ref[rows], 0.5 * step(mid, ROWS, ROWS))):
             parts[end, number] = part
         sources = [whole.at[end]] + [parts.at[end, number] for number in range(4)]
         for number, (source, out) in enumerate(zip(sources, outs)):
@@ -324,27 +327,27 @@
         copy.wait()
 
 
-def forecast(here, bands, scal, x, mult, exchange_edges):
+def forecast(here, bands, model, x, mult, exchange_edges):
     band, width = x.shape
     whole = jax.ShapeDtypeStruct((band, width), jnp.float32)
     shapes = [whole] + [jax.ShapeDtypeStruct((band, width // 2), jnp.float32)] * 4
     x, own, *inner = pl.pallas_call(
         forecast_kernel,
         out_shape=[whole] * 2 + shapes,
-        in_specs=[SMEM] * 4 + [HBM] * 2,
+        in_specs=[SMEM] * 2 + [HBM] * 2,
         out_specs=[VMEM] * 7,
         scratch_shapes=[pltpu.VMEM((band, width), jnp.float32), pltpu.SemaphoreType.DMA((2, 4))],
         compiler_params=LIMIT,
         cost_estimate=pl.CostEstimate(flops=40 * band * width, bytes_accessed=20 * band * width, transcendentals=0),
         name="forecast",
-    )(here, *scal, pltpu.with_memory_space_constraint(x, pltpu.HBM), pltpu.with_memory_space_constraint(mult, pltpu.HBM))
+    )(here, model, pltpu.with_memory_space_constraint(x, pltpu.HBM), pltpu.with_memory_space_constraint(mult, pltpu.HBM))
     low, high = exchange_edges
     outs = pl.pallas_call(
         functools.partial(edge_kernel, bands),
         out_shape=shapes,
-        in_specs=[SMEM] * 4 + [VMEM] * 4 + [ANY] * 5,
+        in_specs=[SMEM] * 2 + [VMEM] * 4 + [ANY] * 5,
         out_specs=[ANY] * 5,
-        input_output_aliases={8 + number: number for number in range(5)},
+        input_output_aliases={6 + number: number for number in range(5)},
         scratch_shapes=[pltpu.VMEM((2, 4 * ROWS, width), jnp.float32)] * 2 + [
             pltpu.VMEM((2, ROWS, width), jnp.float32),
             pltpu.VMEM((2, 4, ROWS, width // 2), jnp.float32),
@@ -353,7 +356,7 @@
         compiler_params=LIMIT,
         cost_estimate=pl.CostEstimate(flops=1000 * width, bytes_accessed=400 * width, transcendentals=0),
         name="edges",
-    )(here, *scal, x, own, low, high, *inner)
+    )(here, model, x, own, low, high, *inner)
     return x, own, *outs
 
 
@@ -361,6 +364,7 @@
                   base_plus, base_minus, step_plus, second_ref, third_ref):
     half = own_ref.shape[1] // 2
     weight = weight_of(here_ref)
+    first, share = weight(FIRST) > 0.0, weight(SHARE)
     for at in range(0, own_ref.shape[0], ROWS):
         rows = slice(at, at + ROWS)
         plus, minus = plus_ref[rows], minus_ref[rows]
@@ -376,9 +380,8 @@
         base_minus[rows] = base[0] - base[1]
         own_plus, own_minus = own[0] + own[1], own[0] - own[1]
         step_plus[rows] = own_plus - plus
-        first = weight(FIRST) > 0.0
-        sent_minus = minus + weight(SHARE) * own_minus
-        second_ref[rows] = jnp.where(first, plus + weight(SHARE) * own_plus, sent_minus)
+        sent_minus = minus + share * own_minus
+        second_ref[rows] = jnp.where(first, plus + share * own_plus, sent_minus)
         third_ref[rows] = jnp.where(first, sent_minus, own_minus - minus)
 
 
@@ -420,14 +423,14 @@
 
 def resid_kernel(bands, first, here_ref, base_ref, *refs):
     terms, outs = refs[:-bands], refs[-bands:]
-    weight = weight_of(here_ref)
+    weights = [weight_of(here_ref)(first + number) for number in range(len(terms))]
     columns = outs[0].shape[1]
     for shift in range(bands):
         target = lax.rem(here_ref[0] + shift, bands)
         at = pl.ds(pl.multiple_of(target * columns, columns), columns)
         value = base_ref[:, at]
-        for number, term in enumerate(terms):
-            value = value - weight(first + number) * term[:, at]
+        for weight, term in zip(weights, terms):
+            value = value - weight * term[:, at]
         outs[shift][...] = value
 
 
@@ -515,24 +518,37 @@
 
 
 def lon_odd_kernel(bands, here_ref, *refs):
-    blocks, (hi, lo, even, field, out, gathered) = refs[:bands], refs[bands:]
+    blocks, (hi, lo, even, field, out, gathered, result, sems) = refs[:bands], refs[bands:]
     gather_rows(here_ref[0], bands, blocks, gathered)
     half = hi.shape[0]
-    odd = lon_product(blocks[0].shape[0], hi, lo, gathered)
-    out[:, :half] = field[:, :half] + 0.5 * (even[...] + odd)
-    out[:, half:] = field[:, half:] + 0.5 * (even[...] - odd)
+    band, parts = blocks[0].shape[0], sems.shape[0]
+    chunk = half // parts
+    copies = []
+    for part in range(parts):
+        cols = slice(part * chunk, (part + 1) * chunk)
+        odd = lon_product(band, hi.at[:, cols], lo.at[:, cols], gathered)
+        for side, value in enumerate((even[:, cols] + odd, even[:, cols] - odd)):
+            at = slice(side * half + part * chunk, side * half + (part + 1) * chunk)
+            result[:, at] = field[:, at] + 0.5 * value
+            copies.append(pltpu.make_async_copy(result.at[:, at], out.at[:, at], sems.at[part, side]))
+            copies[-1].start()
+    for copy in copies:
+        copy.wait()
 
 
 def lon_apply(here, blocks, matrices, extra=()):
     bands = len(blocks)
     band, _ = blocks[0].shape
     half = matrices[0].shape[0]
+    scratch = [pltpu.VMEM((2 * band, half), jnp.bfloat16)]
+    if extra:
+        scratch += [pltpu.VMEM((band, 2 * half), jnp.float32), pltpu.SemaphoreType.DMA((4, 2))]
     return pl.pallas_call(
         functools.partial(lon_odd_kernel if extra else lon_even_kernel, bands),
         out_shape=jax.ShapeDtypeStruct((band, 2 * half if extra else half), jnp.float32),
         in_specs=[SMEM] + [VMEM] * (bands + 2 + len(extra)),
-        out_specs=VMEM,
-        scratch_shapes=[pltpu.VMEM((2 * band, half), jnp.bfloat16)],
+        out_specs=ANY if extra else VMEM,
+        scratch_shapes=scratch,
         compiler_params=LIMIT,
         cost_estimate=pl.CostEstimate(
             flops=6 * band * half * half, bytes_accessed=4 * half * half, transcendentals=0
@@ -541,27 +557,32 @@
     )(here, *blocks, *matrices, *extra)
 
 
-def multiplier_kernel(here_ref, own_ref, plus_ref, minus_ref, near_ref, cross_ref, out_ref):
-    weight = weight_of(here_ref)
-    half = own_ref.shape[1] // 2
-    for at in range(0, own_ref.shape[0], ROWS):
+def multiplier_kernel(here_ref, own_ref, plus_ref, minus_ref, near_ref, direct_ref, out_ref, result, sems):
+    known = weight_of(here_ref)(KNOWN)
+    band, half = plus_ref.shape
+    chunk = band // sems.shape[0]
+    copies = []
+    for at in range(0, band, ROWS):
         rows = slice(at, at + ROWS)
-        plus, minus = plus_ref[rows] + weight(KNOWN) * (cross_ref[rows] - near_ref[rows]), minus_ref[rows]
-        out_ref[rows, :half] = own_ref[rows, :half] - 0.5 * (plus + minus)
-        out_ref[rows, half:] = own_ref[rows, half:] - 0.5 * (plus - minus)
+        plus, minus = plus_ref[rows] + known * (direct_ref[rows] - near_ref[rows]), minus_ref[rows]
+        result[rows, :half] = own_ref[rows, :half] - 0.5 * (plus + minus)
+        result[rows, half:] = own_ref[rows, half:] - 0.5 * (plus - minus)
+        if (at + ROWS) % chunk == 0:
+            part = slice(at + ROWS - chunk, at + ROWS)
+            copies.append(pltpu.make_async_copy(result.at[part], out_ref.at[part], sems.at[at // chunk]))
+            copies[-1].start()
+    for copy in copies:
+        copy.wait()
 
 
 def new_multipliers(here, own, *terms):
     band, width = own.shape
-    rows = 4 * ROWS
-    whole = pl.BlockSpec((rows, width), lambda i: (i, 0))
-    part = pl.BlockSpec((rows, width // 2), lambda i: (i, 0))
     return pl.pallas_call(
         multiplier_kernel,
-        grid=(band // rows,),
         out_shape=jax.ShapeDtypeStruct((band, width), jnp.float32),
-        in_specs=[SMEM, whole] + [part] * 4,
-        out_specs=whole,
+        in_specs=[SMEM] + [VMEM] * 5,
+        out_specs=ANY,
+        scratch_shapes=[pltpu.VMEM((band, width), jnp.float32), pltpu.SemaphoreType.DMA((4,))],
         compiler_params=LIMIT,
         cost_estimate=pl.CostEstimate(flops=6 * band * width, bytes_accessed=20 * band * width, transcendentals=0),
         name="new_multipliers",
@@ -606,27 +627,28 @@
         lax.ppermute(x[-2:], "lat", [(i, i + 1) for i in range(bands - 1)]),
         lax.ppermute(x[:2], "lat", [(i + 1, i) for i in range(bands - 1)]),
     )
-    x, own, x1, plus, minus, near, side = forecast(here, bands, (speed, drift, kappa), x, mult, edges)
+    x, own, x1, plus, minus, near, side = forecast(here, bands, jnp.concatenate([speed, drift, kappa]), x, mult, edges)
     near = hop(near, [(0, 1), (1, 0), (2, 3)])
     side = hop(side, [(0, 2), (1, 3)])
     base_plus, base_minus, step_plus, second, third = defect(
         here, own, observations[0, :, 0], obs_mask[0], x1, plus, minus
     )
+    direct = hop(second, [(0, 1)])
     far = hop(mix(here, None, near, step_plus), [(0, 2), (1, 3)])
-    cross = hop(mix(here, SECOND, second, side), [(0, 1), (2, 3), (3, 2)])
+    cross = hop(mix(here, SECOND, second, side), [(2, 3), (3, 2)])
     third = hop(third, [(0, 1), (1, 3)])
     plus = hop(plus, [(1, 2), (2, 3)])
     minus = hop(minus, [(0, 1), (1, 2), (2, 3)])
     lat_matrices = build(lat_spectrum)
     lon_matrices = build(lon_spectrum)
-    even = resid_blocks(here, bands, EVEN, base_plus, near, far, cross)
+    even = resid_blocks(here, bands, EVEN, base_plus, near, far, direct)
     odd = resid_blocks(here, bands, ODD, base_minus, side, cross, third)
     even, odd = exchange(even), exchange(odd)
     even = lat_apply(here, even, lat_matrices)
     even, odd = exchange(even), exchange(lat_apply(here, odd, lat_matrices))
     even = lon_apply(here, even, lon_matrices[:2])
     field = lon_apply(here, odd, lon_matrices[2:], (even, x))
-    lam = new_multipliers(here, own, plus, minus, near, cross)
+    lam = new_multipliers(here, own, plus, minus, near, direct)
     return (field[None, None], lam[None, None])
 
 

time: 133 us -> 135 us (1.015)
  waiting for transfers between devices: 42.6 us -> 48.5 us
  Pallas kernels: 27 us -> 24.5 us
  starting transfers between devices: 58.1 us -> 56.4 us
    ppermute x28, waiting for transfers between devices: 13.4 us -> 17.5 us  [exchange(): moved.append(lax.ppermute(blocks[shift], 'lat', route))]
    ppermute x28, starting transfers between devices: 30.7 us -> 27.7 us  [exchange(): moved.append(lax.ppermute(blocks[shift], 'lat', route))]
    pallas_call x2, Pallas kernels: 7.2 us -> 5.38 us  [build(): pl.pallas_call(functools.partial(build_kernel, count), out_shape=[shape]...]
    ppermute x7 -> x8, waiting for transfers between devices: 29.3 us -> 30.9 us  [hop(): return lax.ppermute(value, 'win', pairs)]
    ppermute x7 -> x8, starting transfers between devices: 23 us -> 24.4 us  [hop(): return lax.ppermute(value, 'win', pairs)]
  transfers between devices with their start and end apart: 37 -> 38, of which waited for: 12 -> 14; matrix products, arithmetic and copies ran while one was open for 0% -> 0% of each run, Pallas kernels for 17% -> 15%
where the time goes in v2:
time: 135 us; the launch traced here: 134 us
  starting transfers between devices  56.4 us (42%)
  waiting for transfers between devices  48.5 us (36%)
  Pallas kernels  24.5 us (18%)
  between operations  3.05 us (2%)
    ppermute x8, waiting for transfers between devices, hop(): return lax.ppermute(value, 'win', pairs)  30.9 us
    ppermute x28, starting transfers between devices, exchange(): moved.append(lax.ppermute(blocks[shift], 'lat', route))  27.7 us
    ppermute x8, starting transfers between devices, hop(): return lax.ppermute(value, 'win', pairs)  24.4 us
    ppermute x28, waiting for transfers between devices, exchange(): moved.append(lax.ppermute(blocks[shift], 'lat', route))  17.5 us
    pallas_call x2, Pallas kernels, build(): pl.pallas_call(functools.partial(build_kernel, count), out_shape=[shape]...  5.38 us
    pallas_call x2, Pallas kernels, lon_apply(): pl.pallas_call(functools.partial(lon_odd_kernel if extra else lon_even_ke...  4.27 us
    pallas_call x1, Pallas kernels, forecast(): pl.pallas_call(forecast_kernel, out_shape=[whole] * 2 + shapes, in_specs=...  4.18 us
    ppermute x1, starting transfers between devices, per_device_hops(): lax.ppermute(x[-2:], 'lat', [(i, i + 1) for i in range(bands - 1)])  3.03 us
  transfers between devices with their start and end apart: 38, of which 14 were waited for; matrix products, arithmetic and copies ran while one was open for 0% of the time, Pallas kernels for 15%

profile of v2, /device:TPU:0, one launch (start us, length us, event | category | flops | bytes accessed | tf_op | source)
XLA Modules:
  0.0 133.6 jit_solution(6181062534086031625)
XLA Ops:
  0.6 0.9 slice_bitcast_fusion
  1.5 1.3 collective-permute-start.1
  2.8 3.0 %collective-permute-start = (f32[2,2048]{1,0:T(2,128)S(1)}, f32[2,2048]{1,0:T(2,128)S(1)}, u32[]{:S(2)}, u32[]{:S(2)}) collective-permute-start(f32[2,2048]{1,0:T(2,128)S(1)} %get-tuple-element.117), channel_id=1, source_target_pairs={{0,1},{1,2},{2,3},{3,4},{4,5},{5,6},{6,7},{8,9},{9,10},{10,11},{11... | collective-permute-start | bytes 49160 | tf_op jit(solution)/shard_map/ppermute | solution.py:627
  7.8 0.1 pad_add_fusion.here_ref
  7.9 0.1 pad_maximum_fusion.model
  8.0 4.2 %forecast.1 = (f32[128,2048]{1,0:T(8,128)S(1)}, f32[128,2048]{1,0:T(8,128)S(1)}, f32[128,2048]{1,0:T(8,128)S(1)}, f32[128,1024]{1,0:T(8,128)S(1)}, f32[128,1024]...) custom-call(s32[2]{0:T(128)S(1)} %pad_add_fusion.here_ref, f32[3]{0:T(128)S(1)} %pad_maximum_fusion.model, ...), custom_call_target="tpu_custom_call" | custom-call | flops 10485760 | bytes 5242880 | tf_op jit(solution)/shard_map/forecast/pallas_call | solution.py:334
  12.2 1.8 %edges.1 = (f32[128,2048]{1,0:T(8,128)S(1)}, f32[128,1024]{1,0:T(8,128)S(1)}, f32[128,1024]{1,0:T(8,128)S(1)}, f32[128,1024]{1,0:T(8,128)S(1)}, f32[128,1024]{1,0:T(8,128)S(1)}) custom-call(s32[2]{0:T(128)S(1)} %pad_add_fusion.here_ref, f32[3]{0:T(128)S(1)} %pad_maximum_fusion.model, ...), custom_call_target="tpu_custom_call", output_to_operand_aliasing={{0}: (6, {}), {1}: (7, {}), {2}: (8, {}), {3}: (9, {}), {4}... | custom-call | flops 2048000 | bytes 819200 | tf_op jit(solution)/shard_map/edges/pallas_call | solution.py:345
  14.0 4.9 %collective-permute-start.2 = (f32[128,1024]{1,0:T(8,128)S(1)}, f32[128,1024]{1,0:T(8,128)S(1)}, u32[]{:S(2)}, u32[]{:S(2)}) collective-permute-start(f32[128,1024]{1,0:T(8,128)S(1)} %get-tuple-element.70), channel_id=1, source_target_pairs={{0,16},{8,24},{1,17},{9,25},{2,18},{10,26},{3,19},{11,27},{4,20},{... | collective-permute-start | bytes 1572872 | tf_op jit(solution)/shard_map/ppermute | solution.py:602
  18.9 3.4 %collective-permute-start.19 = (f32[128,1024]{1,0:T(8,128)S(1)}, f32[128,1024]{1,0:T(8,128)S(1)}, u32[]{:S(2)}, u32[]{:S(2)}) collective-permute-start(f32[128,1024]{1,0:T(8,128)S(1)} %get-tuple-element.96), channel_id=1, source_target_pairs={{0,8},{8,0},{16,24},{1,9},{9,1},{17,25},{2,10},{10,2},{18,26},{3,1... | collective-permute-start | bytes 1572872 | tf_op jit(solution)/shard_map/ppermute | solution.py:602
  22.3 1.6 %defect.1 = (f32[128,1024]{1,0:T(8,128)S(1)}, f32[128,1024]{1,0:T(8,128)S(1)}, f32[128,1024]{1,0:T(8,128)S(1)}, f32[128,1024]{1,0:T(8,128)S(1)}, f32[128,1024]{1,0:T(8,128)S(1)}) custom-call(s32[2]{0:T(128)S(1)} %pad_add_fusion.here_ref, f32[128,2048]{1,0:T(8,128)S(1)} %get-tuple-element.59.own_ref, f32[2,128,2048]{2,1,0:T(8,128)S(1)} %bitcast.12, ...), custom_call_target="tpu_custom_call" | custom-call | flops 7864320 | bytes 10485760 | tf_op jit(solution)/shard_map/defect/pallas_call | solution.py:394
  23.9 2.5 %collective-permute-start.4 = (f32[128,1024]{1,0:T(8,128)S(1)}, f32[128,1024]{1,0:T(8,128)S(1)}, u32[]{:S(2)}, u32[]{:S(2)}) collective-permute-start(f32[128,1024]{1,0:T(8,128)S(1)} %get-tuple-element.72), channel_id=1, source_target_pairs={{0,8},{8,24},{1,9},{9,25},{2,10},{10,26},{3,11},{11,27},{4,12},{12... | collective-permute-start | bytes 1572872 | tf_op jit(solution)/shard_map/ppermute | solution.py:602
  26.4 4.5 %collective-permute-done.2.other_ref.refs_0_ = f32[128,1024]{1,0:T(8,128)S(1)} collective-permute-done((f32[128,1024]{1,0:T(8,128)S(1)}, f32[128,1024]{1,0:T(8,128)S(1)}, u32[]{:S(2)}, u32[]{:S(2)}) %collective-permute-start.2) | collective-permute-done | bytes 524320 | tf_op jit(solution)/shard_map/ppermute | solution.py:602
  30.9 0.6 mix.2
  31.6 0.7 collective-permute-start.3
  32.3 3.4 %collective-permute-start.21 = (f32[128,1024]{1,0:T(8,128)S(1)}, f32[128,1024]{1,0:T(8,128)S(1)}, u32[]{:S(2)}, u32[]{:S(2)}) collective-permute-start(f32[128,1024]{1,0:T(8,128)S(1)} %get-tuple-element.71.one_ref), channel_id=1, source_target_pairs={{0,8},{1,9},{2,10},{3,11},{4,12},{5,13},{6,14},{7,15}} | collective-permute-start | bytes 1572872 | tf_op jit(solution)/shard_map/ppermute | solution.py:602
  35.7 0.6 mix.3
  36.3 4.4 %collective-permute-start.20 = (f32[128,1024]{1,0:T(8,128)S(1)}, f32[128,1024]{1,0:T(8,128)S(1)}, u32[]{:S(2)}, u32[]{:S(2)}) collective-permute-start(f32[128,1024]{1,0:T(8,128)S(1)} %mix.3), channel_id=1, source_target_pairs={{0,16},{8,24},{1,17},{9,25},{2,18},{10,26},{3,19},{11,27},{4,20},{... | collective-permute-start | bytes 1572872 | tf_op jit(solution)/shard_map/ppermute | solution.py:602
  40.7 0.7 collective-permute-start.36
  41.4 4.4 %collective-permute-done.4.refs_2_ = f32[128,1024]{1,0:T(8,128)S(1)} collective-permute-done((f32[128,1024]{1,0:T(8,128)S(1)}, f32[128,1024]{1,0:T(8,128)S(1)}, u32[]{:S(2)}, u32[]{:S(2)}) %collective-permute-start.4) | collective-permute-done | bytes 524320 | tf_op jit(solution)/shard_map/ppermute | solution.py:602
  45.8 4.4 %collective-permute-start.37 = (f32[128,1024]{1,0:T(8,128)S(1)}, f32[128,1024]{1,0:T(8,128)S(1)}, u32[]{:S(2)}, u32[]{:S(2)}) collective-permute-start(f32[128,1024]{1,0:T(8,128)S(1)} %get-tuple-element.68.minus_ref), channel_id=1, source_target_pairs={{0,8},{8,16},{16,24},{1,9},{9,17},{17,25},{2,10},{10,18},{18,26},{... | collective-permute-start | bytes 1572872 | tf_op jit(solution)/shard_map/ppermute | solution.py:602
  50.4 0.8 resid_blocks.2
  51.2 0.1 collective-permute-start.5
  51.3 5.8 %collective-permute-done.21.refs_2_.direct_ref = f32[128,1024]{1,0:T(8,128)S(1)} collective-permute-done((f32[128,1024]{1,0:T(8,128)S(1)}, f32[128,1024]{1,0:T(8,128)S(1)}, u32[]{:S(2)}, u32[]{:S(2)}) %collective-permute-start.21) | collective-permute-done | bytes 524320 | tf_op jit(solution)/shard_map/ppermute | solution.py:602
  57.1 1.6 %collective-permute-start.6 = (f32[128,128]{1,0:T(8,128)S(1)}, f32[128,128]{1,0:T(8,128)S(1)}, u32[]{:S(2)}, u32[]{:S(2)}) collective-permute-start(f32[128,128]{1,0:T(8,128)S(1)} %get-tuple-element.75), channel_id=1, source_target_pairs={{0,2},{1,3},{2,4},{3,5},{4,6},{5,7},{6,0},{7,1},{8,10},{9,11},{10,... | collective-permute-start | bytes 196616 | tf_op jit(solution)/shard_map/ppermute | solution.py:597
  58.7 16.1 %collective-permute-done.20.refs_1_ = f32[128,1024]{1,0:T(8,128)S(1)} collective-permute-done((f32[128,1024]{1,0:T(8,128)S(1)}, f32[128,1024]{1,0:T(8,128)S(1)}, u32[]{:S(2)}, u32[]{:S(2)}) %collective-permute-start.20) | collective-permute-done | bytes 524320 | tf_op jit(solution)/shard_map/ppermute | solution.py:602
  74.8 0.6 collective-permute-start.7
  75.4 2.0 %collective-permute-start.8 = (f32[128,128]{1,0:T(8,128)S(1)}, f32[128,128]{1,0:T(8,128)S(1)}, u32[]{:S(2)}, u32[]{:S(2)}) collective-permute-start(f32[128,128]{1,0:T(8,128)S(1)} %get-tuple-element.77), channel_id=1, source_target_pairs={{0,4},{1,5},{2,6},{3,7},{4,0},{5,1},{6,2},{7,3},{8,12},{9,13},{10,... | collective-permute-start | bytes 196616 | tf_op jit(solution)/shard_map/ppermute | solution.py:597
  77.4 2.4 %collective-permute-start.9 = (f32[128,128]{1,0:T(8,128)S(1)}, f32[128,128]{1,0:T(8,128)S(1)}, u32[]{:S(2)}, u32[]{:S(2)}) collective-permute-start(f32[128,128]{1,0:T(8,128)S(1)} %get-tuple-element.78), channel_id=1, source_target_pairs={{0,5},{1,6},{2,7},{3,0},{4,1},{5,2},{6,3},{7,4},{8,13},{9,14},{10,... | collective-permute-start | bytes 196616 | tf_op jit(solution)/shard_map/ppermute | solution.py:597
  79.7 0.8 resid_blocks.3
  80.6 1.7 %collective-permute-done.7.refs_3_ = f32[128,128]{1,0:T(8,128)S(1)} collective-permute-done((f32[128,128]{1,0:T(8,128)S(1)}, f32[128,128]{1,0:T(8,128)S(1)}, u32[]{:S(2)}, u32[]{:S(2)}) %collective-permute-start.7) | collective-permute-done | bytes 65568 | tf_op jit(solution)/shard_map/ppermute | solution.py:597
  82.3 2.0 %collective-permute-done.8.refs_4_ = f32[128,128]{1,0:T(8,128)S(1)} collective-permute-done((f32[128,128]{1,0:T(8,128)S(1)}, f32[128,128]{1,0:T(8,128)S(1)}, u32[]{:S(2)}, u32[]{:S(2)}) %collective-permute-start.8) | collective-permute-done | bytes 65568 | tf_op jit(solution)/shard_map/ppermute | solution.py:597
  84.3 3.8 %collective-permute-start.11 = (f32[128,128]{1,0:T(8,128)S(1)}, f32[128,128]{1,0:T(8,128)S(1)}, u32[]{:S(2)}, u32[]{:S(2)}) collective-permute-start(f32[128,128]{1,0:T(8,128)S(1)} %get-tuple-element.80), channel_id=1, source_target_pairs={{0,7},{1,0},{2,1},{3,2},{4,3},{5,4},{6,5},{7,6},{8,15},{9,8},{10,9... | collective-permute-start | bytes 196616 | tf_op jit(solution)/shard_map/ppermute | solution.py:597
  88.0 0.1 collective-permute-start.23
  88.1 1.8 %collective-permute-done.11.refs_7_ = f32[128,128]{1,0:T(8,128)S(1)} collective-permute-done((f32[128,128]{1,0:T(8,128)S(1)}, f32[128,128]{1,0:T(8,128)S(1)}, u32[]{:S(2)}, u32[]{:S(2)}) %collective-permute-start.11) | collective-permute-done | bytes 65568 | tf_op jit(solution)/shard_map/ppermute | solution.py:597
  89.9 3.6 %collective-permute-done.22.refs_1_ = f32[128,128]{1,0:T(8,128)S(1)} collective-permute-done((f32[128,128]{1,0:T(8,128)S(1)}, f32[128,128]{1,0:T(8,128)S(1)}, u32[]{:S(2)}, u32[]{:S(2)}) %collective-permute-start.22) | collective-permute-done | bytes 65568 | tf_op jit(solution)/shard_map/ppermute | solution.py:597
  93.6 0.5 collective-permute-start.25
  94.1 0.9 collective-permute-done.23.refs_2_
  95.0 4.9 %collective-permute-done.24.refs_3_ = f32[128,128]{1,0:T(8,128)S(1)} collective-permute-done((f32[128,128]{1,0:T(8,128)S(1)}, f32[128,128]{1,0:T(8,128)S(1)}, u32[]{:S(2)}, u32[]{:S(2)}) %collective-permute-start.24) | collective-permute-done | bytes 65568 | tf_op jit(solution)/shard_map/ppermute | solution.py:597
  99.9 0.2 collective-permute-done.25.refs_4_
  100.0 0.2 collective-permute-start.28
  100.3 1.6 %shard_map.212 = (bf16[512,512]{1,0:T(8,128)(2,1)S(1)}, bf16[512,512]{1,0:T(8,128)(2,1)S(1)}, bf16[512,512]{1,0:T(8,128)(2,1)S(1)}, bf16[512,512]{1,0:T(8,128)(2,1)S(1)}) custom-call(f32[1,1024]{1,0:T(1,128)S(1)} %copy-done.12, f32[8,256]{1,0:T(8,128)S(1)} %copy-done.11, f32[128,256]{1,0:T(8,128)S(1)} %copy-done.2, f32[8,128]{1,0:T(8,128)S(1)} %copy-done.15, ...), custom_call_target="tpu_custom_call" | custom-call | flops 4194304 | bytes 2097152 | tf_op jit(solution)/shard_map/pallas_call | solution.py:110
  102.0 1.5 %lat_apply.2 = (f32[128,128]{1,0:T(8,128)S(1)}, f32[128,128]{1,0:T(8,128)S(1)}, f32[128,128]{1,0:T(8,128)S(1)}, f32[128,128]{1,0:T(8,128)S(1)}, f32[128,128]{1,0...) custom-call(s32[2]{0:T(128)S(1)} %pad_add_fusion.here_ref, ...), custom_call_target="tpu_custom_call" | custom-call | flops 402653184 | bytes 2097152 | tf_op jit(solution)/shard_map/lat_apply/pallas_call | solution.py:481
  103.5 0.9 collective-permute-start.12
  104.4 1.7 %collective-permute-start.13 = (f32[128,128]{1,0:T(8,128)S(1)}, f32[128,128]{1,0:T(8,128)S(1)}, u32[]{:S(2)}, u32[]{:S(2)}) collective-permute-start(f32[128,128]{1,0:T(8,128)S(1)} %get-tuple-element.87), channel_id=1, source_target_pairs={{0,2},{1,3},{2,4},{3,5},{4,6},{5,7},{6,0},{7,1},{8,10},{9,11},{10,... | collective-permute-start | bytes 196616 | tf_op jit(solution)/shard_map/ppermute | solution.py:597
  106.1 1.4 %lat_apply.3 = (f32[128,128]{1,0:T(8,128)S(1)}, f32[128,128]{1,0:T(8,128)S(1)}, f32[128,128]{1,0:T(8,128)S(1)}, f32[128,128]{1,0:T(8,128)S(1)}, f32[128,128]{1,0...) custom-call(s32[2]{0:T(128)S(1)} %pad_add_fusion.here_ref, ...), custom_call_target="tpu_custom_call" | custom-call | flops 402653184 | bytes 2097152 | tf_op jit(solution)/shard_map/lat_apply/pallas_call | solution.py:481
  107.5 0.1 collective-permute-start.29
  107.7 0.1 collective-permute-start.30
  107.7 2.6 %collective-permute-start.31 = (f32[128,128]{1,0:T(8,128)S(1)}, f32[128,128]{1,0:T(8,128)S(1)}, u32[]{:S(2)}, u32[]{:S(2)}) collective-permute-start(f32[128,128]{1,0:T(8,128)S(1)} %get-tuple-element.109), channel_id=1, source_target_pairs={{0,3},{1,4},{2,5},{3,6},{4,7},{5,0},{6,1},{7,2},{8,11},{9,12},{10,... | collective-permute-start | bytes 196616 | tf_op jit(solution)/shard_map/ppermute | solution.py:597
  110.3 1.5 %collective-permute-start.32 = (f32[128,128]{1,0:T(8,128)S(1)}, f32[128,128]{1,0:T(8,128)S(1)}, u32[]{:S(2)}, u32[]{:S(2)}) collective-permute-start(f32[128,128]{1,0:T(8,128)S(1)} %get-tuple-element.110), channel_id=1, source_target_pairs={{0,4},{1,5},{2,6},{3,7},{4,0},{5,1},{6,2},{7,3},{8,12},{9,13},{10,... | collective-permute-start | bytes 196616 | tf_op jit(solution)/shard_map/ppermute | solution.py:597
  111.8 2.3 %collective-permute-start.33 = (f32[128,128]{1,0:T(8,128)S(1)}, f32[128,128]{1,0:T(8,128)S(1)}, u32[]{:S(2)}, u32[]{:S(2)}) collective-permute-start(f32[128,128]{1,0:T(8,128)S(1)} %get-tuple-element.111), channel_id=1, source_target_pairs={{0,5},{1,6},{2,7},{3,0},{4,1},{5,2},{6,3},{7,4},{8,13},{9,14},{10,... | collective-permute-start | bytes 196616 | tf_op jit(solution)/shard_map/ppermute | solution.py:597
  114.1 0.5 collective-permute-start.34
  114.6 0.8 collective-permute-start.35
  115.4 3.7 %shard_map.213 = (bf16[1024,1024]{1,0:T(8,128)(2,1)S(1)}, bf16[1024,1024]{1,0:T(8,128)(2,1)S(1)}, bf16[1024,1024]{1,0:T(8,128)(2,1)S(1)}, bf16[1024,1024]{1,0:T(8,128)(2,1)S(1)}) custom-call(f32[1,2048]{1,0:T(1,128)S(1)} %copy-done.6, f32[16,256]{1,0:T(8,128)S(1)} %copy-done.5, f32[128,256]{1,0:T(8,128)S(1)} %copy-done.3, f32[16,128]{1,0:T(8,128)S(1)} %copy-done.9, ...), custom_call_target="tpu_custom_call" | custom-call | flops 16777216 | bytes 8388608 | tf_op jit(solution)/shard_map/pallas_call | solution.py:110
  119.2 1.6 %new_multipliers.1 = f32[128,2048]{1,0:T(8,128)} custom-call(s32[2]{0:T(128)S(1)} %pad_add_fusion.here_ref, f32[128,2048]{1,0:T(8,128)S(1)} %get-tuple-element.59.own_ref, f32[128,1024]{1,0:T(8,128)S(1)} %collective-permute-done.36.plus_ref, f32[128,1024]{1,0:T(8,128)S(1)} %collective-permute-done.37.minus_ref, ...), custom_call_target="tpu_custom_call" | custom-call | flops 1572864 | bytes 5242880 | tf_op jit(solution)/shard_map/new_multipliers/pallas_call | solution.py:580
  120.8 1.0 collective-permute-start.14
  121.7 1.1 collective-permute-start.15
  122.8 2.3 %collective-permute-start.16 = (f32[128,128]{1,0:T(8,128)S(1)}, f32[128,128]{1,0:T(8,128)S(1)}, u32[]{:S(2)}, u32[]{:S(2)}) collective-permute-start(f32[128,128]{1,0:T(8,128)S(1)} %get-tuple-element.90), channel_id=1, source_target_pairs={{0,5},{1,6},{2,7},{3,0},{4,1},{5,2},{6,3},{7,4},{8,13},{9,14},{10,... | collective-permute-start | bytes 196616 | tf_op jit(solution)/shard_map/ppermute | solution.py:597
  125.1 1.3 collective-permute-start.17
  126.4 0.5 collective-permute-start.18
  126.9 1.7 %lon_apply.2.refs_10_ = f32[128,1024]{1,0:T(8,128)S(1)} custom-call(s32[2]{0:T(128)S(1)} %pad_add_fusion.here_ref, f32[128,128]{1,0:T(8,128)S(1)} %get-tuple-element.106.refs_0_, f32[128,128]{1,0:T(8,128)S(1)} %collective-permute-done.29.refs_1_, f32[128,128]{1,0:T(8,128)S(1)} %collective-permute-done.30.refs_2_, ...), custom_call_target="tpu_custom_call" | custom-call | flops 805306368 | bytes 4194304 | tf_op jit(solution)/shard_map/lon_apply/pallas_call | solution.py:546
  128.6 0.1 collective-permute-done.14.refs_3_
  128.7 1.4 %collective-permute-done.15.refs_4_ = f32[128,128]{1,0:T(8,128)S(1)} collective-permute-done((f32[128,128]{1,0:T(8,128)S(1)}, f32[128,128]{1,0:T(8,128)S(1)}, u32[]{:S(2)}, u32[]{:S(2)}) %collective-permute-start.15) | collective-permute-done | bytes 65568 | tf_op jit(solution)/shard_map/ppermute | solution.py:597
  130.1 0.9 collective-permute-done.17.refs_6_
  131.0 2.6 %lon_apply.3 = f32[128,2048]{1,0:T(8,128)} custom-call(s32[2]{0:T(128)S(1)} %pad_add_fusion.here_ref, f32[128,128]{1,0:T(8,128)S(1)} %get-tuple-element.85.refs_0_, f32[128,128]{1,0:T(8,128)S(1)} %collective-permute-done.12.refs_1_, f32[128,128]{1,0:T(8,128)S(1)} %collective-permute-done.13.refs_2_, f32[128,128]{1,0:T(8,128)S(1)} %collective-permute-done.14.refs_3_, ...), custom_call_target="tpu_custom_call" | custom-call | flops 805306368 | bytes 4194304 | tf_op jit(solution)/shard_map/lon_apply/pallas_call | solution.py:546
  (61 shorter events, 0.2 us)
Async XLA Ops:
  1.5 10.6 %collective-permute-start.1 = (f32[2,2048]{1,0:T(2,128)S(1)}, f32[2,2048]{1,0:T(2,128)S(1)}, u32[]{:S(2)}, u32[]{:S(2)}) collective-permute-start(f32[2,2048]{1,0:T(2,128)S(1)} %get-tuple-element.116), channel_id=1, source_target_pairs={{1,0},{2,1},{3,2},{4,3},{5,4},{6,5},{7,6},{9,8},{10,9},{11,10},{12... | collective-permute-start | bytes 49160 | tf_op jit(solution)/shard_map/ppermute | solution.py:628
  2.8 9.3 %collective-permute-start = (f32[2,2048]{1,0:T(2,128)S(1)}, f32[2,2048]{1,0:T(2,128)S(1)}, u32[]{:S(2)}, u32[]{:S(2)}) collective-permute-start(f32[2,2048]{1,0:T(2,128)S(1)} %get-tuple-element.117), channel_id=1, source_target_pairs={{0,1},{1,2},{2,3},{3,4},{4,5},{5,6},{6,7},{8,9},{9,10},{10,11},{11... | collective-permute-start | bytes 49160 | tf_op jit(solution)/shard_map/ppermute | solution.py:627
  12.2 10.2 %copy-start = (f32[1,2,1,128,2048]{4,3,2,1,0:T(8,128)S(1)}, f32[1,2,1,128,2048]{4,3,2,1,0:T(8,128)}, u32[]{:S(2)}) copy-start(f32[1,2,1,128,2048]{4,3,2,1,0:T(8,128)} %param.23) | copy-start | bytes 6291460
  12.2 10.2 %copy-start.1 = (s32[1,2,128,2048]{3,2,1,0:T(8,128)S(1)}, s32[1,2,128,2048]{3,2,1,0:T(8,128)}, u32[]{:S(2)}) copy-start(s32[1,2,128,2048]{3,2,1,0:T(8,128)} %param.24) | copy-start | bytes 6291460
  14.0 17.0 %collective-permute-start.2 = (f32[128,1024]{1,0:T(8,128)S(1)}, f32[128,1024]{1,0:T(8,128)S(1)}, u32[]{:S(2)}, u32[]{:S(2)}) collective-permute-start(f32[128,1024]{1,0:T(8,128)S(1)} %get-tuple-element.70), channel_id=1, source_target_pairs={{0,16},{8,24},{1,17},{9,25},{2,18},{10,26},{3,19},{11,27},{4,20},{... | collective-permute-start | bytes 1572872 | tf_op jit(solution)/shard_map/ppermute | solution.py:602
  18.9 16.8 %collective-permute-start.19 = (f32[128,1024]{1,0:T(8,128)S(1)}, f32[128,1024]{1,0:T(8,128)S(1)}, u32[]{:S(2)}, u32[]{:S(2)}) collective-permute-start(f32[128,1024]{1,0:T(8,128)S(1)} %get-tuple-element.96), channel_id=1, source_target_pairs={{0,8},{8,0},{16,24},{1,9},{9,1},{17,25},{2,10},{10,2},{18,26},{3,1... | collective-permute-start | bytes 1572872 | tf_op jit(solution)/shard_map/ppermute | solution.py:602
  23.9 21.9 %collective-permute-start.4 = (f32[128,1024]{1,0:T(8,128)S(1)}, f32[128,1024]{1,0:T(8,128)S(1)}, u32[]{:S(2)}, u32[]{:S(2)}) collective-permute-start(f32[128,1024]{1,0:T(8,128)S(1)} %get-tuple-element.72), channel_id=1, source_target_pairs={{0,8},{8,24},{1,9},{9,25},{2,10},{10,26},{3,11},{11,27},{4,12},{12... | collective-permute-start | bytes 1572872 | tf_op jit(solution)/shard_map/ppermute | solution.py:602
  31.6 18.7 %collective-permute-start.3 = (f32[128,1024]{1,0:T(8,128)S(1)}, f32[128,1024]{1,0:T(8,128)S(1)}, u32[]{:S(2)}, u32[]{:S(2)}) collective-permute-start(f32[128,1024]{1,0:T(8,128)S(1)} %mix.2), channel_id=1, source_target_pairs={{16,24},{24,16},{17,25},{25,17},{18,26},{26,18},{19,27},{27,19},{2... | collective-permute-start | bytes 1572872 | tf_op jit(solution)/shard_map/ppermute | solution.py:602
  32.3 24.8 %collective-permute-start.21 = (f32[128,1024]{1,0:T(8,128)S(1)}, f32[128,1024]{1,0:T(8,128)S(1)}, u32[]{:S(2)}, u32[]{:S(2)}) collective-permute-start(f32[128,1024]{1,0:T(8,128)S(1)} %get-tuple-element.71.one_ref), channel_id=1, source_target_pairs={{0,8},{1,9},{2,10},{3,11},{4,12},{5,13},{6,14},{7,15}} | collective-permute-start | bytes 1572872 | tf_op jit(solution)/shard_map/ppermute | solution.py:602
  36.3 38.5 %collective-permute-start.20 = (f32[128,1024]{1,0:T(8,128)S(1)}, f32[128,1024]{1,0:T(8,128)S(1)}, u32[]{:S(2)}, u32[]{:S(2)}) collective-permute-start(f32[128,1024]{1,0:T(8,128)S(1)} %mix.3), channel_id=1, source_target_pairs={{0,16},{8,24},{1,17},{9,25},{2,18},{10,26},{3,19},{11,27},{4,20},{... | collective-permute-start | bytes 1572872 | tf_op jit(solution)/shard_map/ppermute | solution.py:602
  40.7 67.0 %collective-permute-start.36 = (f32[128,1024]{1,0:T(8,128)S(1)}, f32[128,1024]{1,0:T(8,128)S(1)}, u32[]{:S(2)}, u32[]{:S(2)}) collective-permute-start(f32[128,1024]{1,0:T(8,128)S(1)} %get-tuple-element.67.plus_ref), channel_id=1, source_target_pairs={{8,16},{16,24},{9,17},{17,25},{10,18},{18,26},{11,19},{19,27},{12,... | collective-permute-start | bytes 1572872 | tf_op jit(solution)/shard_map/ppermute | solution.py:602
  45.8 61.9 %collective-permute-start.37 = (f32[128,1024]{1,0:T(8,128)S(1)}, f32[128,1024]{1,0:T(8,128)S(1)}, u32[]{:S(2)}, u32[]{:S(2)}) collective-permute-start(f32[128,1024]{1,0:T(8,128)S(1)} %get-tuple-element.68.minus_ref), channel_id=1, source_target_pairs={{0,8},{8,16},{16,24},{1,9},{9,17},{17,25},{2,10},{10,18},{18,26},{... | collective-permute-start | bytes 1572872 | tf_op jit(solution)/shard_map/ppermute | solution.py:602
  50.3 50.0 %copy-start.2 = (f32[128,256]{1,0:T(8,128)S(1)}, f32[128,256]{1,0:T(8,128)}, u32[]{:S(2)}) copy-start(f32[128,256]{1,0:T(8,128)} %constant.33.clone.middle_ref) | copy-start | bytes 393220
  50.3 50.0 %copy-start.10 = (f32[8,256]{1,0:T(8,128)S(1)}, f32[8,256]{1,0:T(8,128)}, u32[]{:S(2)}) copy-start(f32[8,256]{1,0:T(8,128)} %constant.35.clone.twist_ref) | copy-start | bytes 24580
  50.3 50.0 %copy-start.11 = (f32[8,256]{1,0:T(8,128)S(1)}, f32[8,256]{1,0:T(8,128)}, u32[]{:S(2)}) copy-start(f32[8,256]{1,0:T(8,128)} %constant.32.clone.inner_ref) | copy-start | bytes 24580
  50.3 50.0 %copy-start.12 = (f32[1,1024]{1,0:T(1,128)S(1)}, f32[1,1024]{1,0:T(1,128)}, u32[]{:S(2)}) copy-start(f32[1,1024]{1,0:T(1,128)} %d_ref.2) | copy-start | bytes 12292
  50.3 49.9 %copy-start.13 = (f32[8,8]{1,0:T(8,128)S(1)}, f32[8,8]{1,0:T(8,128)}, u32[]{:S(2)}) copy-start(f32[8,8]{1,0:T(8,128)} %constant.37.clone.sin_ref) | copy-start | bytes 772
  50.3 49.9 %copy-start.14 = (f32[8,8]{1,0:T(8,128)S(1)}, f32[8,8]{1,0:T(8,128)}, u32[]{:S(2)}) copy-start(f32[8,8]{1,0:T(8,128)} %constant.36.clone.cos_ref) | copy-start | bytes 772
  50.3 49.9 %copy-start.15 = (f32[8,128]{1,0:T(8,128)S(1)}, f32[8,128]{1,0:T(8,128)}, u32[]{:S(2)}) copy-start(f32[8,128]{1,0:T(8,128)} %constant.34.clone.member_ref) | copy-start | bytes 12292
  51.2 24.2 %collective-permute-start.5 = (f32[128,128]{1,0:T(8,128)S(1)}, f32[128,128]{1,0:T(8,128)S(1)}, u32[]{:S(2)}, u32[]{:S(2)}) collective-permute-start(f32[128,128]{1,0:T(8,128)S(1)} %get-tuple-element.74), channel_id=1, source_target_pairs={{0,1},{1,2},{2,3},{3,4},{4,5},{5,6},{6,7},{7,0},{8,9},{9,10},{10,1... | collective-permute-start | bytes 196616 | tf_op jit(solution)/shard_map/ppermute | solution.py:597
  57.1 20.3 %collective-permute-start.6 = (f32[128,128]{1,0:T(8,128)S(1)}, f32[128,128]{1,0:T(8,128)S(1)}, u32[]{:S(2)}, u32[]{:S(2)}) collective-permute-start(f32[128,128]{1,0:T(8,128)S(1)} %get-tuple-element.75), channel_id=1, source_target_pairs={{0,2},{1,3},{2,4},{3,5},{4,6},{5,7},{6,0},{7,1},{8,10},{9,11},{10,... | collective-permute-start | bytes 196616 | tf_op jit(solution)/shard_map/ppermute | solution.py:597
  74.8 7.5 %collective-permute-start.7 = (f32[128,128]{1,0:T(8,128)S(1)}, f32[128,128]{1,0:T(8,128)S(1)}, u32[]{:S(2)}, u32[]{:S(2)}) collective-permute-start(f32[128,128]{1,0:T(8,128)S(1)} %get-tuple-element.76), channel_id=1, source_target_pairs={{0,3},{1,4},{2,5},{3,6},{4,7},{5,0},{6,1},{7,2},{8,11},{9,12},{10,... | collective-permute-start | bytes 196616 | tf_op jit(solution)/shard_map/ppermute | solution.py:597
  75.4 8.9 %collective-permute-start.8 = (f32[128,128]{1,0:T(8,128)S(1)}, f32[128,128]{1,0:T(8,128)S(1)}, u32[]{:S(2)}, u32[]{:S(2)}) collective-permute-start(f32[128,128]{1,0:T(8,128)S(1)} %get-tuple-element.77), channel_id=1, source_target_pairs={{0,4},{1,5},{2,6},{3,7},{4,0},{5,1},{6,2},{7,3},{8,12},{9,13},{10,... | collective-permute-start | bytes 196616 | tf_op jit(solution)/shard_map/ppermute | solution.py:597
  77.4 10.7 %collective-permute-start.9 = (f32[128,128]{1,0:T(8,128)S(1)}, f32[128,128]{1,0:T(8,128)S(1)}, u32[]{:S(2)}, u32[]{:S(2)}) collective-permute-start(f32[128,128]{1,0:T(8,128)S(1)} %get-tuple-element.78), channel_id=1, source_target_pairs={{0,5},{1,6},{2,7},{3,0},{4,1},{5,2},{6,3},{7,4},{8,13},{9,14},{10,... | collective-permute-start | bytes 196616 | tf_op jit(solution)/shard_map/ppermute | solution.py:597
  82.2 5.8 %collective-permute-start.10 = (f32[128,128]{1,0:T(8,128)S(1)}, f32[128,128]{1,0:T(8,128)S(1)}, u32[]{:S(2)}, u32[]{:S(2)}) collective-permute-start(f32[128,128]{1,0:T(8,128)S(1)} %get-tuple-element.79), channel_id=1, source_target_pairs={{0,6},{1,7},{2,0},{3,1},{4,2},{5,3},{6,4},{7,5},{8,14},{9,15},{10,... | collective-permute-start | bytes 196616 | tf_op jit(solution)/shard_map/ppermute | solution.py:597
  84.3 5.7 %collective-permute-start.11 = (f32[128,128]{1,0:T(8,128)S(1)}, f32[128,128]{1,0:T(8,128)S(1)}, u32[]{:S(2)}, u32[]{:S(2)}) collective-permute-start(f32[128,128]{1,0:T(8,128)S(1)} %get-tuple-element.80), channel_id=1, source_target_pairs={{0,7},{1,0},{2,1},{3,2},{4,3},{5,4},{6,5},{7,6},{8,15},{9,8},{10,9... | collective-permute-start | bytes 196616 | tf_op jit(solution)/shard_map/ppermute | solution.py:597
  88.0 5.6 %collective-permute-start.22 = (f32[128,128]{1,0:T(8,128)S(1)}, f32[128,128]{1,0:T(8,128)S(1)}, u32[]{:S(2)}, u32[]{:S(2)}) collective-permute-start(f32[128,128]{1,0:T(8,128)S(1)} %get-tuple-element.99), channel_id=1, source_target_pairs={{0,1},{1,2},{2,3},{3,4},{4,5},{5,6},{6,7},{7,0},{8,9},{9,10},{10,1... | collective-permute-start | bytes 196616 | tf_op jit(solution)/shard_map/ppermute | solution.py:597
  88.0 6.9 %collective-permute-start.23 = (f32[128,128]{1,0:T(8,128)S(1)}, f32[128,128]{1,0:T(8,128)S(1)}, u32[]{:S(2)}, u32[]{:S(2)}) collective-permute-start(f32[128,128]{1,0:T(8,128)S(1)} %get-tuple-element.100), channel_id=1, source_target_pairs={{0,2},{1,3},{2,4},{3,5},{4,6},{5,7},{6,0},{7,1},{8,10},{9,11},{10,... | collective-permute-start | bytes 196616 | tf_op jit(solution)/shard_map/ppermute | solution.py:597
  89.9 9.9 %collective-permute-start.24 = (f32[128,128]{1,0:T(8,128)S(1)}, f32[128,128]{1,0:T(8,128)S(1)}, u32[]{:S(2)}, u32[]{:S(2)}) collective-permute-start(f32[128,128]{1,0:T(8,128)S(1)} %get-tuple-element.101), channel_id=1, source_target_pairs={{0,3},{1,4},{2,5},{3,6},{4,7},{5,0},{6,1},{7,2},{8,11},{9,12},{10,... | collective-permute-start | bytes 196616 | tf_op jit(solution)/shard_map/ppermute | solution.py:597
  93.6 6.5 %collective-permute-start.25 = (f32[128,128]{1,0:T(8,128)S(1)}, f32[128,128]{1,0:T(8,128)S(1)}, u32[]{:S(2)}, u32[]{:S(2)}) collective-permute-start(f32[128,128]{1,0:T(8,128)S(1)} %get-tuple-element.102), channel_id=1, source_target_pairs={{0,4},{1,5},{2,6},{3,7},{4,0},{5,1},{6,2},{7,3},{8,12},{9,13},{10,... | collective-permute-start | bytes 196616 | tf_op jit(solution)/shard_map/ppermute | solution.py:597
  95.0 8.5 %collective-permute-start.26 = (f32[128,128]{1,0:T(8,128)S(1)}, f32[128,128]{1,0:T(8,128)S(1)}, u32[]{:S(2)}, u32[]{:S(2)}) collective-permute-start(f32[128,128]{1,0:T(8,128)S(1)} %get-tuple-element.103), channel_id=1, source_target_pairs={{0,5},{1,6},{2,7},{3,0},{4,1},{5,2},{6,3},{7,4},{8,13},{9,14},{10,... | collective-permute-start | bytes 196616 | tf_op jit(solution)/shard_map/ppermute | solution.py:597
  99.9 4.5 %collective-permute-start.27 = (f32[128,128]{1,0:T(8,128)S(1)}, f32[128,128]{1,0:T(8,128)S(1)}, u32[]{:S(2)}, u32[]{:S(2)}) collective-permute-start(f32[128,128]{1,0:T(8,128)S(1)} %get-tuple-element.104), channel_id=1, source_target_pairs={{0,6},{1,7},{2,0},{3,1},{4,2},{5,3},{6,4},{7,5},{8,14},{9,15},{10,... | collective-permute-start | bytes 196616 | tf_op jit(solution)/shard_map/ppermute | solution.py:597
  100.0 6.0 %collective-permute-start.28 = (f32[128,128]{1,0:T(8,128)S(1)}, f32[128,128]{1,0:T(8,128)S(1)}, u32[]{:S(2)}, u32[]{:S(2)}) collective-permute-start(f32[128,128]{1,0:T(8,128)S(1)} %get-tuple-element.105), channel_id=1, source_target_pairs={{0,7},{1,0},{2,1},{3,2},{4,3},{5,4},{6,5},{7,6},{8,15},{9,8},{10,9... | collective-permute-start | bytes 196616 | tf_op jit(solution)/shard_map/ppermute | solution.py:597
  101.9 13.5 %copy-start.3 = (f32[128,256]{1,0:T(8,128)S(1)}, f32[128,256]{1,0:T(8,128)}, u32[]{:S(2)}) copy-start(f32[128,256]{1,0:T(8,128)} %constant.39.clone.middle_ref) | copy-start | bytes 393220
  101.9 13.4 %copy-start.4 = (f32[16,256]{1,0:T(8,128)S(1)}, f32[16,256]{1,0:T(8,128)}, u32[]{:S(2)}) copy-start(f32[16,256]{1,0:T(8,128)} %constant.41.clone.twist_ref) | copy-start | bytes 49156
  102.0 13.4 %copy-start.5 = (f32[16,256]{1,0:T(8,128)S(1)}, f32[16,256]{1,0:T(8,128)}, u32[]{:S(2)}) copy-start(f32[16,256]{1,0:T(8,128)} %constant.38.clone.inner_ref) | copy-start | bytes 49156
  102.0 13.4 %copy-start.6 = (f32[1,2048]{1,0:T(1,128)S(1)}, f32[1,2048]{1,0:T(1,128)}, u32[]{:S(2)}) copy-start(f32[1,2048]{1,0:T(1,128)} %d_ref.3) | copy-start | bytes 24580
  102.0 13.4 %copy-start.7 = (f32[16,16]{1,0:T(8,128)S(1)}, f32[16,16]{1,0:T(8,128)}, u32[]{:S(2)}) copy-start(f32[16,16]{1,0:T(8,128)} %constant.43.clone.sin_ref) | copy-start | bytes 3076
  102.0 13.4 %copy-start.8 = (f32[16,16]{1,0:T(8,128)S(1)}, f32[16,16]{1,0:T(8,128)}, u32[]{:S(2)}) copy-start(f32[16,16]{1,0:T(8,128)} %constant.42.clone.cos_ref) | copy-start | bytes 3076
  102.0 13.4 %copy-start.9 = (f32[16,128]{1,0:T(8,128)S(1)}, f32[16,128]{1,0:T(8,128)}, u32[]{:S(2)}) copy-start(f32[16,128]{1,0:T(8,128)} %constant.40.clone.member_ref) | copy-start | bytes 24580
  103.5 6.8 %collective-permute-start.12 = (f32[128,128]{1,0:T(8,128)S(1)}, f32[128,128]{1,0:T(8,128)S(1)}, u32[]{:S(2)}, u32[]{:S(2)}) collective-permute-start(f32[128,128]{1,0:T(8,128)S(1)} %get-tuple-element.86), channel_id=1, source_target_pairs={{0,1},{1,2},{2,3},{3,4},{4,5},{5,6},{6,7},{7,0},{8,9},{9,10},{10,1... | collective-permute-start | bytes 196616 | tf_op jit(solution)/shard_map/ppermute | solution.py:597
  104.4 7.4 %collective-permute-start.13 = (f32[128,128]{1,0:T(8,128)S(1)}, f32[128,128]{1,0:T(8,128)S(1)}, u32[]{:S(2)}, u32[]{:S(2)}) collective-permute-start(f32[128,128]{1,0:T(8,128)S(1)} %get-tuple-element.87), channel_id=1, source_target_pairs={{0,2},{1,3},{2,4},{3,5},{4,6},{5,7},{6,0},{7,1},{8,10},{9,11},{10,... | collective-permute-start | bytes 196616 | tf_op jit(solution)/shard_map/ppermute | solution.py:597
  107.5 6.6 %collective-permute-start.29 = (f32[128,128]{1,0:T(8,128)S(1)}, f32[128,128]{1,0:T(8,128)S(1)}, u32[]{:S(2)}, u32[]{:S(2)}) collective-permute-start(f32[128,128]{1,0:T(8,128)S(1)} %get-tuple-element.107), channel_id=1, source_target_pairs={{0,1},{1,2},{2,3},{3,4},{4,5},{5,6},{6,7},{7,0},{8,9},{9,10},{10,1... | collective-permute-start | bytes 196616 | tf_op jit(solution)/shard_map/ppermute | solution.py:597
  107.7 6.9 %collective-permute-start.30 = (f32[128,128]{1,0:T(8,128)S(1)}, f32[128,128]{1,0:T(8,128)S(1)}, u32[]{:S(2)}, u32[]{:S(2)}) collective-permute-start(f32[128,128]{1,0:T(8,128)S(1)} %get-tuple-element.108), channel_id=1, source_target_pairs={{0,2},{1,3},{2,4},{3,5},{4,6},{5,7},{6,0},{7,1},{8,10},{9,11},{10,... | collective-permute-start | bytes 196616 | tf_op jit(solution)/shard_map/ppermute | solution.py:597
  107.7 13.1 %collective-permute-start.31 = (f32[128,128]{1,0:T(8,128)S(1)}, f32[128,128]{1,0:T(8,128)S(1)}, u32[]{:S(2)}, u32[]{:S(2)}) collective-permute-start(f32[128,128]{1,0:T(8,128)S(1)} %get-tuple-element.109), channel_id=1, source_target_pairs={{0,3},{1,4},{2,5},{3,6},{4,7},{5,0},{6,1},{7,2},{8,11},{9,12},{10,... | collective-permute-start | bytes 196616 | tf_op jit(solution)/shard_map/ppermute | solution.py:597
  110.3 11.4 %collective-permute-start.32 = (f32[128,128]{1,0:T(8,128)S(1)}, f32[128,128]{1,0:T(8,128)S(1)}, u32[]{:S(2)}, u32[]{:S(2)}) collective-permute-start(f32[128,128]{1,0:T(8,128)S(1)} %get-tuple-element.110), channel_id=1, source_target_pairs={{0,4},{1,5},{2,6},{3,7},{4,0},{5,1},{6,2},{7,3},{8,12},{9,13},{10,... | collective-permute-start | bytes 196616 | tf_op jit(solution)/shard_map/ppermute | solution.py:597
  111.8 11.0 %collective-permute-start.33 = (f32[128,128]{1,0:T(8,128)S(1)}, f32[128,128]{1,0:T(8,128)S(1)}, u32[]{:S(2)}, u32[]{:S(2)}) collective-permute-start(f32[128,128]{1,0:T(8,128)S(1)} %get-tuple-element.111), channel_id=1, source_target_pairs={{0,5},{1,6},{2,7},{3,0},{4,1},{5,2},{6,3},{7,4},{8,13},{9,14},{10,... | collective-permute-start | bytes 196616 | tf_op jit(solution)/shard_map/ppermute | solution.py:597
  114.1 11.0 %collective-permute-start.34 = (f32[128,128]{1,0:T(8,128)S(1)}, f32[128,128]{1,0:T(8,128)S(1)}, u32[]{:S(2)}, u32[]{:S(2)}) collective-permute-start(f32[128,128]{1,0:T(8,128)S(1)} %get-tuple-element.112), channel_id=1, source_target_pairs={{0,6},{1,7},{2,0},{3,1},{4,2},{5,3},{6,4},{7,5},{8,14},{9,15},{10,... | collective-permute-start | bytes 196616 | tf_op jit(solution)/shard_map/ppermute | solution.py:597
  114.6 11.8 %collective-permute-start.35 = (f32[128,128]{1,0:T(8,128)S(1)}, f32[128,128]{1,0:T(8,128)S(1)}, u32[]{:S(2)}, u32[]{:S(2)}) collective-permute-start(f32[128,128]{1,0:T(8,128)S(1)} %get-tuple-element.113), channel_id=1, source_target_pairs={{0,7},{1,0},{2,1},{3,2},{4,3},{5,4},{6,5},{7,6},{8,15},{9,8},{10,9... | collective-permute-start | bytes 196616 | tf_op jit(solution)/shard_map/ppermute | solution.py:597
  120.8 8.0 %collective-permute-start.14 = (f32[128,128]{1,0:T(8,128)S(1)}, f32[128,128]{1,0:T(8,128)S(1)}, u32[]{:S(2)}, u32[]{:S(2)}) collective-permute-start(f32[128,128]{1,0:T(8,128)S(1)} %get-tuple-element.88), channel_id=1, source_target_pairs={{0,3},{1,4},{2,5},{3,6},{4,7},{5,0},{6,1},{7,2},{8,11},{9,12},{10,... | collective-permute-start | bytes 196616 | tf_op jit(solution)/shard_map/ppermute | solution.py:597
  121.7 8.4 %collective-permute-start.15 = (f32[128,128]{1,0:T(8,128)S(1)}, f32[128,128]{1,0:T(8,128)S(1)}, u32[]{:S(2)}, u32[]{:S(2)}) collective-permute-start(f32[128,128]{1,0:T(8,128)S(1)} %get-tuple-element.89), channel_id=1, source_target_pairs={{0,4},{1,5},{2,6},{3,7},{4,0},{5,1},{6,2},{7,3},{8,12},{9,13},{10,... | collective-permute-start | bytes 196616 | tf_op jit(solution)/shard_map/ppermute | solution.py:597
  122.8 7.3 %collective-permute-start.16 = (f32[128,128]{1,0:T(8,128)S(1)}, f32[128,128]{1,0:T(8,128)S(1)}, u32[]{:S(2)}, u32[]{:S(2)}) collective-permute-start(f32[128,128]{1,0:T(8,128)S(1)} %get-tuple-element.90), channel_id=1, source_target_pairs={{0,5},{1,6},{2,7},{3,0},{4,1},{5,2},{6,3},{7,4},{8,13},{9,14},{10,... | collective-permute-start | bytes 196616 | tf_op jit(solution)/shard_map/ppermute | solution.py:597
  125.1 5.8 %collective-permute-start.17 = (f32[128,128]{1,0:T(8,128)S(1)}, f32[128,128]{1,0:T(8,128)S(1)}, u32[]{:S(2)}, u32[]{:S(2)}) collective-permute-start(f32[128,128]{1,0:T(8,128)S(1)} %get-tuple-element.91), channel_id=1, source_target_pairs={{0,6},{1,7},{2,0},{3,1},{4,2},{5,3},{6,4},{7,5},{8,14},{9,15},{10,... | collective-permute-start | bytes 196616 | tf_op jit(solution)/shard_map/ppermute | solution.py:597
  126.4 4.6 %collective-permute-start.18 = (f32[128,128]{1,0:T(8,128)S(1)}, f32[128,128]{1,0:T(8,128)S(1)}, u32[]{:S(2)}, u32[]{:S(2)}) collective-permute-start(f32[128,128]{1,0:T(8,128)S(1)} %get-tuple-element.92), channel_id=1, source_target_pairs={{0,7},{1,0},{2,1},{3,2},{4,3},{5,4},{6,5},{7,6},{8,15},{9,8},{10,9... | collective-permute-start | bytes 196616 | tf_op jit(solution)/shard_map/ppermute | solution.py:597

commit v3 on v2

--- a/solution.py
+++ b/solution.py
@@ -249,115 +249,62 @@
             (value[:, :half] + value[:, half:], value[:, :half] - value[:, half:])]
 
 
-def forecast_kernel(here_ref, model, x_hbm, mult_hbm, x_ref, own_ref, x1_ref, *refs):
-    outs, (mult_ref, sems) = refs[:4], refs[4:]
+def forecast_kernel(bands, here_ref, model, inside_ref, outside_ref, x_hbm, mult_hbm, x_ref, own_ref, x1_ref, *refs):
+    outs, (ext, mid, mult_ref, sems) = refs[:4], refs[4:]
     band = x_ref.shape[0]
+    edge = inside_ref.shape[0] // 2
     chunk = band // 4
     weight, scal = weight_of(here_ref), (model[0], model[1], model[2])
-    sign, share = weight(SIGN), weight(SHARE)
+    sign, share, kept = weight(SIGN), weight(SHARE), weight(OWN)
+    copies = []
+    for number, (source, target, start) in enumerate(((x_hbm, ext, ROWS), (mult_hbm, mult_ref, 0))):
+        for part in range(4):
+            to = slice(start + part * chunk, start + (part + 1) * chunk)
+            copies.append(pltpu.make_async_copy(
+                source.at[part * chunk:(part + 1) * chunk], target.at[to], sems.at[number, part]
+            ))
+            copies[-1].start()
 
     def step(source, at, count):
         return stencil(scal, source[at:at + count], source[at + 1:at + count + 1], source[at - 1:at + count - 1])
 
-    copies = []
-    for number, (source, target) in enumerate(((x_hbm, x_ref), (mult_hbm, mult_ref))):
-        for part in range(4):
-            rows = slice(part * chunk, (part + 1) * chunk)
-            copies.append(pltpu.make_async_copy(source.at[rows], target.at[rows], sems.at[number, part]))
-            copies[-1].start()
-    ready, stepped = 0, ROWS
+    second_of_pair = lax.rem(here_ref[0], 2) == 1
+    ext[ROWS - edge:ROWS] = jnp.where(second_of_pair, inside_ref[edge:], outside_ref[edge:])
+    ext[ROWS + band:ROWS + band + edge] = jnp.where(second_of_pair, outside_ref[:edge], inside_ref[:edge])
+    stepped = ROWS
     for part in range(4):
         copies[part].wait()
-        ready += chunk
         if part == 0:
-            x1_ref[ROWS - 1:ROWS] = step(x_ref, ROWS - 1, 1)
-        while stepped + ROWS < ready:
-            x1_ref[stepped:stepped + ROWS] = step(x_ref, stepped, ROWS)
+            mid[ROWS - 1:ROWS] = step(ext, ROWS - 1, 1) * jnp.where(here_ref[0] > 0, 1.0, 0.0)
+        while stepped + ROWS < ROWS + (part + 1) * chunk or (part == 3 and stepped < ROWS + band):
+            mid[stepped:stepped + ROWS] = step(ext, stepped, ROWS)
             stepped += ROWS
-    x1_ref[stepped:stepped + 1] = step(x_ref, stepped, 1)
-    kept = weight(OWN)
+    mid[ROWS + band:ROWS + band + 1] = step(ext, ROWS + band, 1) * jnp.where(here_ref[0] < bands - 1, 1.0, 0.0)
     for part in range(4):
         copies[4 + part].wait()
         for at in range(part * chunk, (part + 1) * chunk, ROWS):
-            rows = slice(at, at + ROWS)
-            own = mult_ref[rows] + kept * x_ref[rows]
-            own_ref[rows] = own
-            if 0 < at < band - ROWS:
-                for out, value in zip(outs, windowed(sign, share, own, 0.5 * step(x1_ref, at, ROWS))):
-                    out[rows] = value
-
-
-def edge_kernel(bands, here_ref, model, x_ref, own_ref, low_ref, high_ref, *refs):
-    outs, (ext, mid, whole, parts, sems) = refs[5:10], refs[10:]
-    band = x_ref.shape[0]
-    edge = low_ref.shape[0]
-    weight, scal = weight_of(here_ref), (model[0], model[1], model[2])
-    sign, share = weight(SIGN), weight(SHARE)
-    copies = []
-    for end in range(2):
-        at = 0 if end == 0 else band - ROWS
-        if end == 0:
-            ext[end, ROWS - edge:ROWS] = low_ref[...]
-            ext[end, ROWS:3 * ROWS] = x_ref[:2 * ROWS]
-        else:
-            ext[end, :2 * ROWS] = x_ref[band - 2 * ROWS:]
-            ext[end, 2 * ROWS:2 * ROWS + edge] = high_ref[...]
-
-        def step(source, row, count):
-            return stencil(scal, source[end, row:row + count], source[end, row + 1:row + count + 1],
-                           source[end, row - 1:row + count - 1])
-
-        before, after = step(ext, ROWS - 1, 1), step(ext, 2 * ROWS, 1)
-        if end == 0:
-            before = before * jnp.where(here_ref[0] > 0, 1.0, 0.0)
-        else:
-            after = after * jnp.where(here_ref[0] < bands - 1, 1.0, 0.0)
-        mid[end, ROWS - 1:ROWS] = before
-        mid[end, 2 * ROWS:2 * ROWS + 1] = after
-        mid[end, ROWS:2 * ROWS] = step(ext, ROWS, ROWS)
-        rows = slice(at, at + ROWS)
-        whole[end] = mid[end, ROWS:2 * ROWS]
-        for number, part in enumerate(windowed(sign, share, own_ref[rows], 0.5 * step(mid, ROWS, ROWS))):
-            parts[end, number] = part
-        sources = [whole.at[end]] + [parts.at[end, number] for number in range(4)]
-        for number, (source, out) in enumerate(zip(sources, outs)):
-            copies.append(pltpu.make_async_copy(source, out.at[rows], sems.at[end, number]))
-            copies[-1].start()
-    for copy in copies:
-        copy.wait()
-
-
-def forecast(here, bands, model, x, mult, exchange_edges):
+            rows, shifted = slice(at, at + ROWS), slice(at + ROWS, at + 2 * ROWS)
+            field = ext[shifted]
+            own = mult_ref[rows] + kept * field
+            x_ref[rows], own_ref[rows], x1_ref[rows] = field, own, mid[shifted]
+            for out, value in zip(outs, windowed(sign, share, own, 0.5 * step(mid, at + ROWS, ROWS))):
+                out[rows] = value
+
+
+def forecast(here, bands, model, x, mult, rims):
     band, width = x.shape
     whole = jax.ShapeDtypeStruct((band, width), jnp.float32)
-    shapes = [whole] + [jax.ShapeDtypeStruct((band, width // 2), jnp.float32)] * 4
-    x, own, *inner = pl.pallas_call(
-        forecast_kernel,
-        out_shape=[whole] * 2 + shapes,
-        in_specs=[SMEM] * 2 + [HBM] * 2,
+    tall = pltpu.VMEM((band + 2 * ROWS, width), jnp.float32)
+    return pl.pallas_call(
+        functools.partial(forecast_kernel, bands),
+        out_shape=[whole] * 3 + [jax.ShapeDtypeStruct((band, width // 2), jnp.float32)] * 4,
+        in_specs=[SMEM] * 2 + [VMEM] * 2 + [HBM] * 2,
         out_specs=[VMEM] * 7,
-        scratch_shapes=[pltpu.VMEM((band, width), jnp.float32), pltpu.SemaphoreType.DMA((2, 4))],
+        scratch_shapes=[tall, tall, pltpu.VMEM((band, width), jnp.float32), pltpu.SemaphoreType.DMA((2, 4))],
         compiler_params=LIMIT,
         cost_estimate=pl.CostEstimate(flops=40 * band * width, bytes_accessed=20 * band * width, transcendentals=0),
         name="forecast",
-    )(here, model, pltpu.with_memory_space_constraint(x, pltpu.HBM), pltpu.with_memory_space_constraint(mult, pltpu.HBM))
-    low, high = exchange_edges
-    outs = pl.pallas_call(
-        functools.partial(edge_kernel, bands),
-        out_shape=shapes,
-        in_specs=[SMEM] * 2 + [VMEM] * 4 + [ANY] * 5,
-        out_specs=[ANY] * 5,
-        input_output_aliases={6 + number: number for number in range(5)},
-        scratch_shapes=[pltpu.VMEM((2, 4 * ROWS, width), jnp.float32)] * 2 + [
-            pltpu.VMEM((2, ROWS, width), jnp.float32),
-            pltpu.VMEM((2, 4, ROWS, width // 2), jnp.float32),
-            pltpu.SemaphoreType.DMA((2, 5)),
-        ],
-        compiler_params=LIMIT,
-        cost_estimate=pl.CostEstimate(flops=1000 * width, bytes_accessed=400 * width, transcendentals=0),
-        name="edges",
-    )(here, model, x, own, low, high, *inner)
-    return x, own, *outs
+    )(here, model, *rims, *[pltpu.with_memory_space_constraint(value, pltpu.HBM) for value in (x, mult)])
 
 
 def defect_kernel(here_ref, own_ref, obs_ref, mask_ref, x1_ref, plus_ref, minus_ref,
@@ -426,7 +373,7 @@
     weights = [weight_of(here_ref)(first + number) for number in range(len(terms))]
     columns = outs[0].shape[1]
     for shift in range(bands):
-        target = lax.rem(here_ref[0] + shift, bands)
+        target = jnp.bitwise_xor(here_ref[0], shift)
         at = pl.ds(pl.multiple_of(target * columns, columns), columns)
         value = base_ref[:, at]
         for weight, term in zip(weights, terms):
@@ -455,7 +402,7 @@
     pairs = bands // 2
     band, columns = blocks[0].shape
     for shift in range(pairs):
-        source = lax.rem(here - shift + bands, bands)
+        source = jnp.bitwise_xor(here, shift)
         rows = pl.ds(pl.multiple_of(lax.rem(source, pairs) * band, band), band)
         first, other = blocks[shift][...], blocks[shift + pairs][...]
         sign = jnp.where(source < pairs, 1.0, -1.0)
@@ -468,7 +415,7 @@
         both = dot(hi[...], gathered[part])
         mixed[part] = both[:, :columns] + both[:, columns:] + dot(lo[...], gathered[part, :, :columns])
     for shift in range(bands):
-        target = lax.rem(here + shift, bands)
+        target = jnp.bitwise_xor(here, shift)
         rows = pl.ds(pl.multiple_of(lax.rem(target, pairs) * band, band), band)
         sign = jnp.where(target < pairs, 1.0, -1.0)
         outs[shift][...] = mixed[0, rows] + sign * mixed[1, rows]
@@ -498,7 +445,7 @@
 def gather_rows(here, bands, blocks, gathered):
     band, columns = blocks[0].shape
     for shift in range(bands):
-        source = lax.rem(here - shift + bands, bands)
+        source = jnp.bitwise_xor(here, shift)
         at = pl.ds(pl.multiple_of(source * columns, columns), columns)
         hi, lo = split(blocks[shift][...])
         gathered[:band, at] = hi
@@ -591,10 +538,10 @@
 
 def exchange(blocks):
     bands = len(blocks)
-    moved = [blocks[0]]
-    for shift in range(1, bands):
-        route = [(source, (source + shift) % bands) for source in range(bands)]
-        moved.append(lax.ppermute(blocks[shift], "lat", route))
+    moved = list(blocks)
+    for shift in [*range(bands // 2, bands), *range(2, bands // 2), 1]:
+        route = [(source, source ^ shift) for source in range(bands)]
+        moved[shift] = lax.ppermute(blocks[shift], "lat", route)
     return moved
 
 
@@ -608,7 +555,7 @@
     bands, windows = lax.axis_size("lat"), lax.axis_size("win")
     band, nlon = state.shape[2:]
     columns = nlon // 2 // bands
-    if windows != 4 or state.shape[1] != 1 or bands % 2 or band % LANES or columns % LANES:
+    if windows != 4 or state.shape[1] != 1 or bands & (bands - 1) or band % LANES or columns % LANES:
         return per_device_any(
             state, multipliers, observations, obs_mask, speed, drift, kappa, lat_spectrum, lon_spectrum
         )
@@ -623,9 +570,10 @@
     bands = lax.axis_size("lat")
     here = jnp.stack([lax.axis_index("lat"), lax.axis_index("win")]).astype(jnp.int32)
     x, mult = state[0, 0], multipliers[0, 0]
+    rims = jnp.concatenate([x[:2], x[-2:]])
     edges = (
-        lax.ppermute(x[-2:], "lat", [(i, i + 1) for i in range(bands - 1)]),
-        lax.ppermute(x[:2], "lat", [(i + 1, i) for i in range(bands - 1)]),
+        lax.ppermute(rims, "lat", [(i, i ^ 1) for i in range(bands)]),
+        lax.ppermute(rims, "lat", [pair for i in range(1, bands - 1, 2) for pair in ((i, i + 1), (i + 1, i))]),
     )
     x, own, x1, plus, minus, near, side = forecast(here, bands, jnp.concatenate([speed, drift, kappa]), x, mult, edges)
     near = hop(near, [(0, 1), (1, 0), (2, 3)])

time: 135 us -> 134 us (level)
  waiting for transfers between devices: 48.5 us -> 38 us
  starting transfers between devices: 56.4 us -> 65 us
  local copies, waits for them, and re-layouts: 1 us -> 2.72 us
  Pallas kernels: 24.5 us -> 23 us
    ppermute x30, starting transfers between devices: 32 us -> 40.9 us  [the longest x28 35.8 us: exchange(): moved[shift] = lax.ppermute(blocks[shift], 'lat', route)]
    ppermute x30, waiting for transfers between devices: 17.5 us -> 11.9 us  [the longest x28 11.9 us: exchange(): moved[shift] = lax.ppermute(blocks[shift], 'lat', route)]
    ppermute x8, waiting for transfers between devices: 30.9 us -> 26.1 us  [hop(): return lax.ppermute(value, 'win', pairs)]
    unnamed x32, local copies, waits for them, and re-layouts: 0.11 us -> 1.69 us
    pallas_call x2 -> x1, Pallas kernels: 5.95 us -> 4.45 us  [forecast(): pl.pallas_call(functools.partial(forecast_kernel, bands), out_shape=[whol...]
  transfers between devices with their start and end apart: 38 -> 38, of which waited for: 14 -> 9; matrix products, arithmetic and copies ran while one was open for 0% -> 0% of each run, Pallas kernels for 15% -> 12%
where the time goes in v3:
time: 134 us; the launch traced here: 132 us
  starting transfers between devices  65 us (49%)
  waiting for transfers between devices  38 us (28%)
  Pallas kernels  23 us (17%)
  between operations  3.22 us (2%)
  local copies, waits for them, and re-layouts  2.72 us (2%)
    ppermute x28, starting transfers between devices, exchange(): moved[shift] = lax.ppermute(blocks[shift], 'lat', route)  35.8 us
    ppermute x8, waiting for transfers between devices, hop(): return lax.ppermute(value, 'win', pairs)  26.1 us
    ppermute x8, starting transfers between devices, hop(): return lax.ppermute(value, 'win', pairs)  24.1 us
    ppermute x28, waiting for transfers between devices, exchange(): moved[shift] = lax.ppermute(blocks[shift], 'lat', route)  11.9 us
    pallas_call x2, Pallas kernels, build(): pl.pallas_call(functools.partial(build_kernel, count), out_shape=[shape]...  5.38 us
    ppermute x1, starting transfers between devices, per_device_hops(): lax.ppermute(rims, 'lat', [(i, i ^ 1) for i in range(bands)])  4.48 us
    pallas_call x1, Pallas kernels, forecast(): pl.pallas_call(functools.partial(forecast_kernel, bands), out_shape=[whol...  4.45 us
    pallas_call x2, Pallas kernels, lon_apply(): pl.pallas_call(functools.partial(lon_odd_kernel if extra else lon_even_ke...  4.27 us
  transfers between devices with their start and end apart: 38, of which 9 were waited for; matrix products, arithmetic and copies ran while one was open for 0% of the time, Pallas kernels for 12%

profile of v3, /device:TPU:0, one launch (start us, length us, event | category | flops | bytes accessed | tf_op | source)
XLA Modules:
  0.0 132.1 jit_solution(12751488705768760070)
XLA Ops:
  0.6 1.0 slice_bitcast_fusion.1
  1.7 0.7 collective-permute-start.1
  2.4 4.5 %collective-permute-start = (f32[4,2048]{1,0:T(4,128)S(1)}, f32[4,2048]{1,0:T(4,128)S(1)}, u32[]{:S(2)}, u32[]{:S(2)}) collective-permute-start(f32[4,2048]{1,0:T(4,128)S(1)} %pad_maximum_fusion), channel_id=1, source_target_pairs={{0,1},{1,0},{2,3},{3,2},{4,5},{5,4},{6,7},{7,6},{8,9},{9,8},{10,11... | collective-permute-start | bytes 98312 | tf_op jit(solution)/shard_map/ppermute | solution.py:575
  8.8 0.1 pad_add_fusion.here_ref
  8.9 0.1 pad_maximum_fusion.1.model
  9.0 4.4 %forecast.1 = (f32[128,2048]{1,0:T(8,128)S(1)}, f32[128,2048]{1,0:T(8,128)S(1)}, f32[128,2048]{1,0:T(8,128)S(1)}, f32[128,1024]{1,0:T(8,128)S(1)}, f32[128,1024]...) custom-call(s32[2]{0:T(128)S(1)} %pad_add_fusion.here_ref, f32[3]{0:T(128)S(1)} %pad_maximum_fusion.1.model, ...), custom_call_target="tpu_custom_call" | custom-call | flops 10485760 | bytes 5242880 | tf_op jit(solution)/shard_map/forecast/pallas_call | solution.py:298
  13.4 3.5 %collective-permute-start.2 = (f32[128,1024]{1,0:T(8,128)S(1)}, f32[128,1024]{1,0:T(8,128)S(1)}, u32[]{:S(2)}, u32[]{:S(2)}) collective-permute-start(f32[128,1024]{1,0:T(8,128)S(1)} %get-tuple-element.59), channel_id=1, source_target_pairs={{0,16},{8,24},{1,17},{9,25},{2,18},{10,26},{3,19},{11,27},{4,20},{... | collective-permute-start | bytes 1572872 | tf_op jit(solution)/shard_map/ppermute | solution.py:549
  16.9 3.4 %collective-permute-start.19 = (f32[128,1024]{1,0:T(8,128)S(1)}, f32[128,1024]{1,0:T(8,128)S(1)}, u32[]{:S(2)}, u32[]{:S(2)}) collective-permute-start(f32[128,1024]{1,0:T(8,128)S(1)} %get-tuple-element.85), channel_id=1, source_target_pairs={{0,8},{8,0},{16,24},{1,9},{9,1},{17,25},{2,10},{10,2},{18,26},{3,1... | collective-permute-start | bytes 1572872 | tf_op jit(solution)/shard_map/ppermute | solution.py:549
  20.3 1.6 %copy-done.1 = s32[1,2,128,2048]{3,2,1,0:T(8,128)S(1)} copy-done((s32[1,2,128,2048]{3,2,1,0:T(8,128)S(1)}, s32[1,2,128,2048]{3,2,1,0:T(8,128)}, u32[]{:S(2)}) %copy-start.1) | copy-done | bytes 2097176
  21.9 1.5 %defect.1 = (f32[128,1024]{1,0:T(8,128)S(1)}, f32[128,1024]{1,0:T(8,128)S(1)}, f32[128,1024]{1,0:T(8,128)S(1)}, f32[128,1024]{1,0:T(8,128)S(1)}, f32[128,1024]{1,0:T(8,128)S(1)}) custom-call(s32[2]{0:T(128)S(1)} %pad_add_fusion.here_ref, f32[128,2048]{1,0:T(8,128)S(1)} %get-tuple-element.54.own_ref, f32[2,128,2048]{2,1,0:T(8,128)S(1)} %bitcast.12, ...), custom_call_target="tpu_custom_call" | custom-call | flops 7864320 | bytes 10485760 | tf_op jit(solution)/shard_map/defect/pallas_call | solution.py:341
  23.4 2.5 %collective-permute-start.4 = (f32[128,1024]{1,0:T(8,128)S(1)}, f32[128,1024]{1,0:T(8,128)S(1)}, u32[]{:S(2)}, u32[]{:S(2)}) collective-permute-start(f32[128,1024]{1,0:T(8,128)S(1)} %get-tuple-element.61), channel_id=1, source_target_pairs={{0,8},{8,24},{1,9},{9,25},{2,10},{10,26},{3,11},{11,27},{4,12},{12... | collective-permute-start | bytes 1572872 | tf_op jit(solution)/shard_map/ppermute | solution.py:549
  25.9 2.3 %collective-permute-done.2.other_ref.refs_0_ = f32[128,1024]{1,0:T(8,128)S(1)} collective-permute-done((f32[128,1024]{1,0:T(8,128)S(1)}, f32[128,1024]{1,0:T(8,128)S(1)}, u32[]{:S(2)}, u32[]{:S(2)}) %collective-permute-start.2) | collective-permute-done | bytes 524320 | tf_op jit(solution)/shard_map/ppermute | solution.py:549
  28.2 0.6 mix.2
  28.8 0.7 collective-permute-start.3
  29.5 4.4 %collective-permute-start.21 = (f32[128,1024]{1,0:T(8,128)S(1)}, f32[128,1024]{1,0:T(8,128)S(1)}, u32[]{:S(2)}, u32[]{:S(2)}) collective-permute-start(f32[128,1024]{1,0:T(8,128)S(1)} %get-tuple-element.60.one_ref), channel_id=1, source_target_pairs={{0,8},{1,9},{2,10},{3,11},{4,12},{5,13},{6,14},{7,15}} | collective-permute-start | bytes 1572872 | tf_op jit(solution)/shard_map/ppermute | solution.py:549
  33.9 0.6 mix.3
  34.5 4.4 %collective-permute-start.20 = (f32[128,1024]{1,0:T(8,128)S(1)}, f32[128,1024]{1,0:T(8,128)S(1)}, u32[]{:S(2)}, u32[]{:S(2)}) collective-permute-start(f32[128,1024]{1,0:T(8,128)S(1)} %mix.3), channel_id=1, source_target_pairs={{0,16},{8,24},{1,17},{9,25},{2,18},{10,26},{3,19},{11,27},{4,20},{... | collective-permute-start | bytes 1572872 | tf_op jit(solution)/shard_map/ppermute | solution.py:549
  38.9 0.7 collective-permute-start.36
  39.6 4.2 %collective-permute-done.4.refs_2_ = f32[128,1024]{1,0:T(8,128)S(1)} collective-permute-done((f32[128,1024]{1,0:T(8,128)S(1)}, f32[128,1024]{1,0:T(8,128)S(1)}, u32[]{:S(2)}, u32[]{:S(2)}) %collective-permute-start.4) | collective-permute-done | bytes 524320 | tf_op jit(solution)/shard_map/ppermute | solution.py:549
  43.8 4.6 %collective-permute-start.37 = (f32[128,1024]{1,0:T(8,128)S(1)}, f32[128,1024]{1,0:T(8,128)S(1)}, u32[]{:S(2)}, u32[]{:S(2)}) collective-permute-start(f32[128,1024]{1,0:T(8,128)S(1)} %get-tuple-element.57.minus_ref), channel_id=1, source_target_pairs={{0,8},{8,16},{16,24},{1,9},{9,17},{17,25},{2,10},{10,18},{18,26},{... | collective-permute-start | bytes 1572872 | tf_op jit(solution)/shard_map/ppermute | solution.py:549
  48.4 0.0 copy-start.2
  48.4 0.0 copy-start.10
  48.4 0.0 copy-start.11
  48.5 0.0 copy-start.13
  48.5 0.8 resid_blocks.2
  49.3 0.1 collective-permute-start.5
  49.4 5.6 %collective-permute-done.21.refs_2_.direct_ref = f32[128,1024]{1,0:T(8,128)S(1)} collective-permute-done((f32[128,1024]{1,0:T(8,128)S(1)}, f32[128,1024]{1,0:T(8,128)S(1)}, u32[]{:S(2)}, u32[]{:S(2)}) %collective-permute-start.21) | collective-permute-done | bytes 524320 | tf_op jit(solution)/shard_map/ppermute | solution.py:549
  55.1 1.6 %collective-permute-start.6 = (f32[128,128]{1,0:T(8,128)S(1)}, f32[128,128]{1,0:T(8,128)S(1)}, u32[]{:S(2)}, u32[]{:S(2)}) collective-permute-start(f32[128,128]{1,0:T(8,128)S(1)} %get-tuple-element.64), channel_id=1, source_target_pairs={{0,2},{1,3},{2,0},{3,1},{4,6},{5,7},{6,4},{7,5},{8,10},{9,11},{10,... | collective-permute-start | bytes 196616 | tf_op jit(solution)/shard_map/ppermute | solution.py:544
  56.6 14.0 %collective-permute-done.20.refs_1_ = f32[128,1024]{1,0:T(8,128)S(1)} collective-permute-done((f32[128,1024]{1,0:T(8,128)S(1)}, f32[128,1024]{1,0:T(8,128)S(1)}, u32[]{:S(2)}, u32[]{:S(2)}) %collective-permute-start.20) | collective-permute-done | bytes 524320 | tf_op jit(solution)/shard_map/ppermute | solution.py:549
  70.6 2.6 %collective-permute-start.8 = (f32[128,128]{1,0:T(8,128)S(1)}, f32[128,128]{1,0:T(8,128)S(1)}, u32[]{:S(2)}, u32[]{:S(2)}) collective-permute-start(f32[128,128]{1,0:T(8,128)S(1)} %get-tuple-element.66), channel_id=1, source_target_pairs={{0,4},{1,5},{2,6},{3,7},{4,0},{5,1},{6,2},{7,3},{8,12},{9,13},{10,... | collective-permute-start | bytes 196616 | tf_op jit(solution)/shard_map/ppermute | solution.py:544
  73.2 1.3 %collective-permute-start.9 = (f32[128,128]{1,0:T(8,128)S(1)}, f32[128,128]{1,0:T(8,128)S(1)}, u32[]{:S(2)}, u32[]{:S(2)}) collective-permute-start(f32[128,128]{1,0:T(8,128)S(1)} %get-tuple-element.67), channel_id=1, source_target_pairs={{0,5},{1,4},{2,7},{3,6},{4,1},{5,0},{6,3},{7,2},{8,13},{9,12},{10,... | collective-permute-start | bytes 196616 | tf_op jit(solution)/shard_map/ppermute | solution.py:544
  74.5 0.8 resid_blocks.3
  75.4 2.5 %collective-permute-start.10 = (f32[128,128]{1,0:T(8,128)S(1)}, f32[128,128]{1,0:T(8,128)S(1)}, u32[]{:S(2)}, u32[]{:S(2)}) collective-permute-start(f32[128,128]{1,0:T(8,128)S(1)} %get-tuple-element.68), channel_id=1, source_target_pairs={{0,6},{1,7},{2,4},{3,5},{4,2},{5,3},{6,0},{7,1},{8,14},{9,15},{10,... | collective-permute-start | bytes 196616 | tf_op jit(solution)/shard_map/ppermute | solution.py:544
  77.9 4.0 %collective-permute-start.11 = (f32[128,128]{1,0:T(8,128)S(1)}, f32[128,128]{1,0:T(8,128)S(1)}, u32[]{:S(2)}, u32[]{:S(2)}) collective-permute-start(f32[128,128]{1,0:T(8,128)S(1)} %get-tuple-element.69), channel_id=1, source_target_pairs={{0,7},{1,6},{2,5},{3,4},{4,3},{5,2},{6,1},{7,0},{8,15},{9,14},{10,... | collective-permute-start | bytes 196616 | tf_op jit(solution)/shard_map/ppermute | solution.py:544
  81.9 0.2 collective-permute-done.9.refs_5_
  82.2 2.5 %collective-permute-start.23 = (f32[128,128]{1,0:T(8,128)S(1)}, f32[128,128]{1,0:T(8,128)S(1)}, u32[]{:S(2)}, u32[]{:S(2)}) collective-permute-start(f32[128,128]{1,0:T(8,128)S(1)} %get-tuple-element.89), channel_id=1, source_target_pairs={{0,2},{1,3},{2,0},{3,1},{4,6},{5,7},{6,4},{7,5},{8,10},{9,11},{10,... | collective-permute-start | bytes 196616 | tf_op jit(solution)/shard_map/ppermute | solution.py:544
  84.7 1.8 %collective-permute-start.24 = (f32[128,128]{1,0:T(8,128)S(1)}, f32[128,128]{1,0:T(8,128)S(1)}, u32[]{:S(2)}, u32[]{:S(2)}) collective-permute-start(f32[128,128]{1,0:T(8,128)S(1)} %get-tuple-element.90), channel_id=1, source_target_pairs={{0,3},{1,2},{2,1},{3,0},{4,7},{5,6},{6,5},{7,4},{8,11},{9,10},{10,... | collective-permute-start | bytes 196616 | tf_op jit(solution)/shard_map/ppermute | solution.py:544
  86.5 1.6 %collective-permute-start.25 = (f32[128,128]{1,0:T(8,128)S(1)}, f32[128,128]{1,0:T(8,128)S(1)}, u32[]{:S(2)}, u32[]{:S(2)}) collective-permute-start(f32[128,128]{1,0:T(8,128)S(1)} %get-tuple-element.91), channel_id=1, source_target_pairs={{0,4},{1,5},{2,6},{3,7},{4,0},{5,1},{6,2},{7,3},{8,12},{9,13},{10,... | collective-permute-start | bytes 196616 | tf_op jit(solution)/shard_map/ppermute | solution.py:544
  88.1 1.2 collective-permute-start.26
  89.3 1.9 %collective-permute-start.27 = (f32[128,128]{1,0:T(8,128)S(1)}, f32[128,128]{1,0:T(8,128)S(1)}, u32[]{:S(2)}, u32[]{:S(2)}) collective-permute-start(f32[128,128]{1,0:T(8,128)S(1)} %get-tuple-element.93), channel_id=1, source_target_pairs={{0,6},{1,7},{2,4},{3,5},{4,2},{5,3},{6,0},{7,1},{8,14},{9,15},{10,... | collective-permute-start | bytes 196616 | tf_op jit(solution)/shard_map/ppermute | solution.py:544
  91.2 4.9 %collective-permute-done.25.refs_4_ = f32[128,128]{1,0:T(8,128)S(1)} collective-permute-done((f32[128,128]{1,0:T(8,128)S(1)}, f32[128,128]{1,0:T(8,128)S(1)}, u32[]{:S(2)}, u32[]{:S(2)}) %collective-permute-start.25) | collective-permute-done | bytes 65568 | tf_op jit(solution)/shard_map/ppermute | solution.py:544
  96.1 1.6 %shard_map.212 = (bf16[512,512]{1,0:T(8,128)(2,1)S(1)}, bf16[512,512]{1,0:T(8,128)(2,1)S(1)}, bf16[512,512]{1,0:T(8,128)(2,1)S(1)}, bf16[512,512]{1,0:T(8,128)(2,1)S(1)}) custom-call(f32[1,1024]{1,0:T(1,128)S(1)} %copy-done.12, f32[8,256]{1,0:T(8,128)S(1)} %copy-done.11, f32[128,256]{1,0:T(8,128)S(1)} %copy-done.2, f32[8,128]{1,0:T(8,128)S(1)} %copy-done.15, ...), custom_call_target="tpu_custom_call" | custom-call | flops 4194304 | bytes 2097152 | tf_op jit(solution)/shard_map/pallas_call | solution.py:110
  97.9 1.5 %lat_apply.2 = (f32[128,128]{1,0:T(8,128)S(1)}, f32[128,128]{1,0:T(8,128)S(1)}, f32[128,128]{1,0:T(8,128)S(1)}, f32[128,128]{1,0:T(8,128)S(1)}, f32[128,128]{1,0...) custom-call(s32[2]{0:T(128)S(1)} %pad_add_fusion.here_ref, ...), custom_call_target="tpu_custom_call" | custom-call | flops 402653184 | bytes 2097152 | tf_op jit(solution)/shard_map/lat_apply/pallas_call | solution.py:428
  99.4 0.1 collective-permute-start.12
  99.4 0.2 collective-permute-start.13
  99.6 2.5 %collective-permute-done.28.refs_7_ = f32[128,128]{1,0:T(8,128)S(1)} collective-permute-done((f32[128,128]{1,0:T(8,128)S(1)}, f32[128,128]{1,0:T(8,128)S(1)}, u32[]{:S(2)}, u32[]{:S(2)}) %collective-permute-start.28) | collective-permute-done | bytes 65568 | tf_op jit(solution)/shard_map/ppermute | solution.py:544
  102.1 1.4 %lat_apply.3 = (f32[128,128]{1,0:T(8,128)S(1)}, f32[128,128]{1,0:T(8,128)S(1)}, f32[128,128]{1,0:T(8,128)S(1)}, f32[128,128]{1,0:T(8,128)S(1)}, f32[128,128]{1,0...) custom-call(s32[2]{0:T(128)S(1)} %pad_add_fusion.here_ref, ...), custom_call_target="tpu_custom_call" | custom-call | flops 402653184 | bytes 2097152 | tf_op jit(solution)/shard_map/lat_apply/pallas_call | solution.py:428
  103.5 0.2 collective-permute-start.29
  103.7 1.7 %collective-permute-start.31 = (f32[128,128]{1,0:T(8,128)S(1)}, f32[128,128]{1,0:T(8,128)S(1)}, u32[]{:S(2)}, u32[]{:S(2)}) collective-permute-start(f32[128,128]{1,0:T(8,128)S(1)} %get-tuple-element.98), channel_id=1, source_target_pairs={{0,3},{1,2},{2,1},{3,0},{4,7},{5,6},{6,5},{7,4},{8,11},{9,10},{10,... | collective-permute-start | bytes 196616 | tf_op jit(solution)/shard_map/ppermute | solution.py:544
  105.5 1.8 %collective-permute-start.32 = (f32[128,128]{1,0:T(8,128)S(1)}, f32[128,128]{1,0:T(8,128)S(1)}, u32[]{:S(2)}, u32[]{:S(2)}) collective-permute-start(f32[128,128]{1,0:T(8,128)S(1)} %get-tuple-element.99), channel_id=1, source_target_pairs={{0,4},{1,5},{2,6},{3,7},{4,0},{5,1},{6,2},{7,3},{8,12},{9,13},{10,... | collective-permute-start | bytes 196616 | tf_op jit(solution)/shard_map/ppermute | solution.py:544
  107.3 0.8 collective-permute-start.33
  108.1 1.3 %collective-permute-start.34 = (f32[128,128]{1,0:T(8,128)S(1)}, f32[128,128]{1,0:T(8,128)S(1)}, u32[]{:S(2)}, u32[]{:S(2)}) collective-permute-start(f32[128,128]{1,0:T(8,128)S(1)} %get-tuple-element.101), channel_id=1, source_target_pairs={{0,6},{1,7},{2,4},{3,5},{4,2},{5,3},{6,0},{7,1},{8,14},{9,15},{10,... | collective-permute-start | bytes 196616 | tf_op jit(solution)/shard_map/ppermute | solution.py:544
  109.5 2.2 %collective-permute-start.35 = (f32[128,128]{1,0:T(8,128)S(1)}, f32[128,128]{1,0:T(8,128)S(1)}, u32[]{:S(2)}, u32[]{:S(2)}) collective-permute-start(f32[128,128]{1,0:T(8,128)S(1)} %get-tuple-element.102), channel_id=1, source_target_pairs={{0,7},{1,6},{2,5},{3,4},{4,3},{5,2},{6,1},{7,0},{8,15},{9,14},{10,... | collective-permute-start | bytes 196616 | tf_op jit(solution)/shard_map/ppermute | solution.py:544
  111.7 3.7 %shard_map.213 = (bf16[1024,1024]{1,0:T(8,128)(2,1)S(1)}, bf16[1024,1024]{1,0:T(8,128)(2,1)S(1)}, bf16[1024,1024]{1,0:T(8,128)(2,1)S(1)}, bf16[1024,1024]{1,0:T(8,128)(2,1)S(1)}) custom-call(f32[1,2048]{1,0:T(1,128)S(1)} %copy-done.6, f32[16,256]{1,0:T(8,128)S(1)} %copy-done.5, f32[128,256]{1,0:T(8,128)S(1)} %copy-done.3, f32[16,128]{1,0:T(8,128)S(1)} %copy-done.9, ...), custom_call_target="tpu_custom_call" | custom-call | flops 16777216 | bytes 8388608 | tf_op jit(solution)/shard_map/pallas_call | solution.py:110
  115.5 1.6 %new_multipliers.1 = f32[128,2048]{1,0:T(8,128)} custom-call(s32[2]{0:T(128)S(1)} %pad_add_fusion.here_ref, f32[128,2048]{1,0:T(8,128)S(1)} %get-tuple-element.54.own_ref, f32[128,1024]{1,0:T(8,128)S(1)} %collective-permute-done.36.plus_ref, f32[128,1024]{1,0:T(8,128)S(1)} %collective-permute-done.37.minus_ref, ...), custom_call_target="tpu_custom_call" | custom-call | flops 1572864 | bytes 5242880 | tf_op jit(solution)/shard_map/new_multipliers/pallas_call | solution.py:527
  117.1 0.1 collective-permute-start.14
  117.2 1.9 %collective-permute-start.15 = (f32[128,128]{1,0:T(8,128)S(1)}, f32[128,128]{1,0:T(8,128)S(1)}, u32[]{:S(2)}, u32[]{:S(2)}) collective-permute-start(f32[128,128]{1,0:T(8,128)S(1)} %get-tuple-element.78), channel_id=1, source_target_pairs={{0,4},{1,5},{2,6},{3,7},{4,0},{5,1},{6,2},{7,3},{8,12},{9,13},{10,... | collective-permute-start | bytes 196616 | tf_op jit(solution)/shard_map/ppermute | solution.py:544
  119.1 0.8 collective-permute-start.16
  119.9 1.7 %collective-permute-start.17 = (f32[128,128]{1,0:T(8,128)S(1)}, f32[128,128]{1,0:T(8,128)S(1)}, u32[]{:S(2)}, u32[]{:S(2)}) collective-permute-start(f32[128,128]{1,0:T(8,128)S(1)} %get-tuple-element.80), channel_id=1, source_target_pairs={{0,6},{1,7},{2,4},{3,5},{4,2},{5,3},{6,0},{7,1},{8,14},{9,15},{10,... | collective-permute-start | bytes 196616 | tf_op jit(solution)/shard_map/ppermute | solution.py:544
  121.6 1.8 %collective-permute-start.18 = (f32[128,128]{1,0:T(8,128)S(1)}, f32[128,128]{1,0:T(8,128)S(1)}, u32[]{:S(2)}, u32[]{:S(2)}) collective-permute-start(f32[128,128]{1,0:T(8,128)S(1)} %get-tuple-element.81), channel_id=1, source_target_pairs={{0,7},{1,6},{2,5},{3,4},{4,3},{5,2},{6,1},{7,0},{8,15},{9,14},{10,... | collective-permute-start | bytes 196616 | tf_op jit(solution)/shard_map/ppermute | solution.py:544
  123.4 1.7 %lon_apply.2.refs_10_ = f32[128,1024]{1,0:T(8,128)S(1)} custom-call(s32[2]{0:T(128)S(1)} %pad_add_fusion.here_ref, f32[128,128]{1,0:T(8,128)S(1)} %get-tuple-element.95.refs_0_, f32[128,128]{1,0:T(8,128)S(1)} %collective-permute-done.29.refs_1_, f32[128,128]{1,0:T(8,128)S(1)} %collective-permute-done.30.refs_2_, ...), custom_call_target="tpu_custom_call" | custom-call | flops 805306368 | bytes 4194304 | tf_op jit(solution)/shard_map/lon_apply/pallas_call | solution.py:493
  125.1 3.3 %collective-permute-done.15.refs_4_ = f32[128,128]{1,0:T(8,128)S(1)} collective-permute-done((f32[128,128]{1,0:T(8,128)S(1)}, f32[128,128]{1,0:T(8,128)S(1)}, u32[]{:S(2)}, u32[]{:S(2)}) %collective-permute-start.15) | collective-permute-done | bytes 65568 | tf_op jit(solution)/shard_map/ppermute | solution.py:544
  128.4 0.9 collective-permute-done.16.refs_5_
  129.3 2.6 %lon_apply.3 = f32[128,2048]{1,0:T(8,128)} custom-call(s32[2]{0:T(128)S(1)} %pad_add_fusion.here_ref, f32[128,128]{1,0:T(8,128)S(1)} %get-tuple-element.74.refs_0_, f32[128,128]{1,0:T(8,128)S(1)} %collective-permute-done.12.refs_1_, f32[128,128]{1,0:T(8,128)S(1)} %collective-permute-done.13.refs_2_, f32[128,128]{1,0:T(8,128)S(1)} %collective-permute-done.14.refs_3_, ...), custom_call_target="tpu_custom_call" | custom-call | flops 805306368 | bytes 4194304 | tf_op jit(solution)/shard_map/lon_apply/pallas_call | solution.py:493
  (61 shorter events, 0.2 us)
Async XLA Ops:
  0.6 19.7 %copy-start = (f32[1,2,1,128,2048]{4,3,2,1,0:T(8,128)S(1)}, f32[1,2,1,128,2048]{4,3,2,1,0:T(8,128)}, u32[]{:S(2)}) copy-start(f32[1,2,1,128,2048]{4,3,2,1,0:T(8,128)} %param.23) | copy-start | bytes 6291460
  1.7 7.2 %collective-permute-start.1 = (f32[4,2048]{1,0:T(4,128)S(1)}, f32[4,2048]{1,0:T(4,128)S(1)}, u32[]{:S(2)}, u32[]{:S(2)}) collective-permute-start(f32[4,2048]{1,0:T(4,128)S(1)} %pad_maximum_fusion), channel_id=1, source_target_pairs={{1,2},{2,1},{3,4},{4,3},{5,6},{6,5},{9,10},{10,9},{11,12},{12,11},... | collective-permute-start | bytes 98312 | tf_op jit(solution)/shard_map/ppermute | solution.py:576
  2.4 6.6 %collective-permute-start = (f32[4,2048]{1,0:T(4,128)S(1)}, f32[4,2048]{1,0:T(4,128)S(1)}, u32[]{:S(2)}, u32[]{:S(2)}) collective-permute-start(f32[4,2048]{1,0:T(4,128)S(1)} %pad_maximum_fusion), channel_id=1, source_target_pairs={{0,1},{1,0},{2,3},{3,2},{4,5},{5,4},{6,7},{7,6},{8,9},{9,8},{10,11... | collective-permute-start | bytes 98312 | tf_op jit(solution)/shard_map/ppermute | solution.py:575
  13.4 14.8 %collective-permute-start.2 = (f32[128,1024]{1,0:T(8,128)S(1)}, f32[128,1024]{1,0:T(8,128)S(1)}, u32[]{:S(2)}, u32[]{:S(2)}) collective-permute-start(f32[128,1024]{1,0:T(8,128)S(1)} %get-tuple-element.59), channel_id=1, source_target_pairs={{0,16},{8,24},{1,17},{9,25},{2,18},{10,26},{3,19},{11,27},{4,20},{... | collective-permute-start | bytes 1572872 | tf_op jit(solution)/shard_map/ppermute | solution.py:549
  16.9 17.0 %collective-permute-start.19 = (f32[128,1024]{1,0:T(8,128)S(1)}, f32[128,1024]{1,0:T(8,128)S(1)}, u32[]{:S(2)}, u32[]{:S(2)}) collective-permute-start(f32[128,1024]{1,0:T(8,128)S(1)} %get-tuple-element.85), channel_id=1, source_target_pairs={{0,8},{8,0},{16,24},{1,9},{9,1},{17,25},{2,10},{10,2},{18,26},{3,1... | collective-permute-start | bytes 1572872 | tf_op jit(solution)/shard_map/ppermute | solution.py:549
  20.3 1.6 %copy-start.1 = (s32[1,2,128,2048]{3,2,1,0:T(8,128)S(1)}, s32[1,2,128,2048]{3,2,1,0:T(8,128)}, u32[]{:S(2)}) copy-start(s32[1,2,128,2048]{3,2,1,0:T(8,128)} %param.24) | copy-start | bytes 6291460
  23.4 20.4 %collective-permute-start.4 = (f32[128,1024]{1,0:T(8,128)S(1)}, f32[128,1024]{1,0:T(8,128)S(1)}, u32[]{:S(2)}, u32[]{:S(2)}) collective-permute-start(f32[128,1024]{1,0:T(8,128)S(1)} %get-tuple-element.61), channel_id=1, source_target_pairs={{0,8},{8,24},{1,9},{9,25},{2,10},{10,26},{3,11},{11,27},{4,12},{12... | collective-permute-start | bytes 1572872 | tf_op jit(solution)/shard_map/ppermute | solution.py:549
  28.8 19.6 %collective-permute-start.3 = (f32[128,1024]{1,0:T(8,128)S(1)}, f32[128,1024]{1,0:T(8,128)S(1)}, u32[]{:S(2)}, u32[]{:S(2)}) collective-permute-start(f32[128,1024]{1,0:T(8,128)S(1)} %mix.2), channel_id=1, source_target_pairs={{16,24},{24,16},{17,25},{25,17},{18,26},{26,18},{19,27},{27,19},{2... | collective-permute-start | bytes 1572872 | tf_op jit(solution)/shard_map/ppermute | solution.py:549
  29.5 25.5 %collective-permute-start.21 = (f32[128,1024]{1,0:T(8,128)S(1)}, f32[128,1024]{1,0:T(8,128)S(1)}, u32[]{:S(2)}, u32[]{:S(2)}) collective-permute-start(f32[128,1024]{1,0:T(8,128)S(1)} %get-tuple-element.60.one_ref), channel_id=1, source_target_pairs={{0,8},{1,9},{2,10},{3,11},{4,12},{5,13},{6,14},{7,15}} | collective-permute-start | bytes 1572872 | tf_op jit(solution)/shard_map/ppermute | solution.py:549
  34.5 36.1 %collective-permute-start.20 = (f32[128,1024]{1,0:T(8,128)S(1)}, f32[128,1024]{1,0:T(8,128)S(1)}, u32[]{:S(2)}, u32[]{:S(2)}) collective-permute-start(f32[128,1024]{1,0:T(8,128)S(1)} %mix.3), channel_id=1, source_target_pairs={{0,16},{8,24},{1,17},{9,25},{2,18},{10,26},{3,19},{11,27},{4,20},{... | collective-permute-start | bytes 1572872 | tf_op jit(solution)/shard_map/ppermute | solution.py:549
  38.9 64.8 %collective-permute-start.36 = (f32[128,1024]{1,0:T(8,128)S(1)}, f32[128,1024]{1,0:T(8,128)S(1)}, u32[]{:S(2)}, u32[]{:S(2)}) collective-permute-start(f32[128,1024]{1,0:T(8,128)S(1)} %get-tuple-element.56.plus_ref), channel_id=1, source_target_pairs={{8,16},{16,24},{9,17},{17,25},{10,18},{18,26},{11,19},{19,27},{12,... | collective-permute-start | bytes 1572872 | tf_op jit(solution)/shard_map/ppermute | solution.py:549
  43.8 59.9 %collective-permute-start.37 = (f32[128,1024]{1,0:T(8,128)S(1)}, f32[128,1024]{1,0:T(8,128)S(1)}, u32[]{:S(2)}, u32[]{:S(2)}) collective-permute-start(f32[128,1024]{1,0:T(8,128)S(1)} %get-tuple-element.57.minus_ref), channel_id=1, source_target_pairs={{0,8},{8,16},{16,24},{1,9},{9,17},{17,25},{2,10},{10,18},{18,26},{... | collective-permute-start | bytes 1572872 | tf_op jit(solution)/shard_map/ppermute | solution.py:549
  48.4 47.7 %copy-start.2 = (f32[128,256]{1,0:T(8,128)S(1)}, f32[128,256]{1,0:T(8,128)}, u32[]{:S(2)}) copy-start(f32[128,256]{1,0:T(8,128)} %constant.33.clone.middle_ref) | copy-start | bytes 393220
  48.4 47.7 %copy-start.10 = (f32[8,256]{1,0:T(8,128)S(1)}, f32[8,256]{1,0:T(8,128)}, u32[]{:S(2)}) copy-start(f32[8,256]{1,0:T(8,128)} %constant.35.clone.twist_ref) | copy-start | bytes 24580
  48.4 47.7 %copy-start.11 = (f32[8,256]{1,0:T(8,128)S(1)}, f32[8,256]{1,0:T(8,128)}, u32[]{:S(2)}) copy-start(f32[8,256]{1,0:T(8,128)} %constant.32.clone.inner_ref) | copy-start | bytes 24580
  48.5 47.6 %copy-start.12 = (f32[1,1024]{1,0:T(1,128)S(1)}, f32[1,1024]{1,0:T(1,128)}, u32[]{:S(2)}) copy-start(f32[1,1024]{1,0:T(1,128)} %d_ref.2) | copy-start | bytes 12292
  48.5 47.6 %copy-start.13 = (f32[8,8]{1,0:T(8,128)S(1)}, f32[8,8]{1,0:T(8,128)}, u32[]{:S(2)}) copy-start(f32[8,8]{1,0:T(8,128)} %constant.37.clone.sin_ref) | copy-start | bytes 772
  48.5 47.6 %copy-start.14 = (f32[8,8]{1,0:T(8,128)S(1)}, f32[8,8]{1,0:T(8,128)}, u32[]{:S(2)}) copy-start(f32[8,8]{1,0:T(8,128)} %constant.36.clone.cos_ref) | copy-start | bytes 772
  48.5 47.6 %copy-start.15 = (f32[8,128]{1,0:T(8,128)S(1)}, f32[8,128]{1,0:T(8,128)}, u32[]{:S(2)}) copy-start(f32[8,128]{1,0:T(8,128)} %constant.34.clone.member_ref) | copy-start | bytes 12292
  49.3 21.3 %collective-permute-start.5 = (f32[128,128]{1,0:T(8,128)S(1)}, f32[128,128]{1,0:T(8,128)S(1)}, u32[]{:S(2)}, u32[]{:S(2)}) collective-permute-start(f32[128,128]{1,0:T(8,128)S(1)} %get-tuple-element.63), channel_id=1, source_target_pairs={{0,1},{1,0},{2,3},{3,2},{4,5},{5,4},{6,7},{7,6},{8,9},{9,8},{10,11... | collective-permute-start | bytes 196616 | tf_op jit(solution)/shard_map/ppermute | solution.py:544
  55.1 18.1 %collective-permute-start.6 = (f32[128,128]{1,0:T(8,128)S(1)}, f32[128,128]{1,0:T(8,128)S(1)}, u32[]{:S(2)}, u32[]{:S(2)}) collective-permute-start(f32[128,128]{1,0:T(8,128)S(1)} %get-tuple-element.64), channel_id=1, source_target_pairs={{0,2},{1,3},{2,0},{3,1},{4,6},{5,7},{6,4},{7,5},{8,10},{9,11},{10,... | collective-permute-start | bytes 196616 | tf_op jit(solution)/shard_map/ppermute | solution.py:544
  70.6 4.8 %collective-permute-start.7 = (f32[128,128]{1,0:T(8,128)S(1)}, f32[128,128]{1,0:T(8,128)S(1)}, u32[]{:S(2)}, u32[]{:S(2)}) collective-permute-start(f32[128,128]{1,0:T(8,128)S(1)} %get-tuple-element.65), channel_id=1, source_target_pairs={{0,3},{1,2},{2,1},{3,0},{4,7},{5,6},{6,5},{7,4},{8,11},{9,10},{10,... | collective-permute-start | bytes 196616 | tf_op jit(solution)/shard_map/ppermute | solution.py:544
  70.6 7.3 %collective-permute-start.8 = (f32[128,128]{1,0:T(8,128)S(1)}, f32[128,128]{1,0:T(8,128)S(1)}, u32[]{:S(2)}, u32[]{:S(2)}) collective-permute-start(f32[128,128]{1,0:T(8,128)S(1)} %get-tuple-element.66), channel_id=1, source_target_pairs={{0,4},{1,5},{2,6},{3,7},{4,0},{5,1},{6,2},{7,3},{8,12},{9,13},{10,... | collective-permute-start | bytes 196616 | tf_op jit(solution)/shard_map/ppermute | solution.py:544
  73.2 9.0 %collective-permute-start.9 = (f32[128,128]{1,0:T(8,128)S(1)}, f32[128,128]{1,0:T(8,128)S(1)}, u32[]{:S(2)}, u32[]{:S(2)}) collective-permute-start(f32[128,128]{1,0:T(8,128)S(1)} %get-tuple-element.67), channel_id=1, source_target_pairs={{0,5},{1,4},{2,7},{3,6},{4,1},{5,0},{6,3},{7,2},{8,13},{9,12},{10,... | collective-permute-start | bytes 196616 | tf_op jit(solution)/shard_map/ppermute | solution.py:544
  75.4 6.8 %collective-permute-start.10 = (f32[128,128]{1,0:T(8,128)S(1)}, f32[128,128]{1,0:T(8,128)S(1)}, u32[]{:S(2)}, u32[]{:S(2)}) collective-permute-start(f32[128,128]{1,0:T(8,128)S(1)} %get-tuple-element.68), channel_id=1, source_target_pairs={{0,6},{1,7},{2,4},{3,5},{4,2},{5,3},{6,0},{7,1},{8,14},{9,15},{10,... | collective-permute-start | bytes 196616 | tf_op jit(solution)/shard_map/ppermute | solution.py:544
  77.9 6.8 %collective-permute-start.11 = (f32[128,128]{1,0:T(8,128)S(1)}, f32[128,128]{1,0:T(8,128)S(1)}, u32[]{:S(2)}, u32[]{:S(2)}) collective-permute-start(f32[128,128]{1,0:T(8,128)S(1)} %get-tuple-element.69), channel_id=1, source_target_pairs={{0,7},{1,6},{2,5},{3,4},{4,3},{5,2},{6,1},{7,0},{8,15},{9,14},{10,... | collective-permute-start | bytes 196616 | tf_op jit(solution)/shard_map/ppermute | solution.py:544
  82.2 4.4 %collective-permute-start.22 = (f32[128,128]{1,0:T(8,128)S(1)}, f32[128,128]{1,0:T(8,128)S(1)}, u32[]{:S(2)}, u32[]{:S(2)}) collective-permute-start(f32[128,128]{1,0:T(8,128)S(1)} %get-tuple-element.88), channel_id=1, source_target_pairs={{0,1},{1,0},{2,3},{3,2},{4,5},{5,4},{6,7},{7,6},{8,9},{9,8},{10,11... | collective-permute-start | bytes 196616 | tf_op jit(solution)/shard_map/ppermute | solution.py:544
  82.2 5.9 %collective-permute-start.23 = (f32[128,128]{1,0:T(8,128)S(1)}, f32[128,128]{1,0:T(8,128)S(1)}, u32[]{:S(2)}, u32[]{:S(2)}) collective-permute-start(f32[128,128]{1,0:T(8,128)S(1)} %get-tuple-element.89), channel_id=1, source_target_pairs={{0,2},{1,3},{2,0},{3,1},{4,6},{5,7},{6,4},{7,5},{8,10},{9,11},{10,... | collective-permute-start | bytes 196616 | tf_op jit(solution)/shard_map/ppermute | solution.py:544
  84.7 4.6 %collective-permute-start.24 = (f32[128,128]{1,0:T(8,128)S(1)}, f32[128,128]{1,0:T(8,128)S(1)}, u32[]{:S(2)}, u32[]{:S(2)}) collective-permute-start(f32[128,128]{1,0:T(8,128)S(1)} %get-tuple-element.90), channel_id=1, source_target_pairs={{0,3},{1,2},{2,1},{3,0},{4,7},{5,6},{6,5},{7,4},{8,11},{9,10},{10,... | collective-permute-start | bytes 196616 | tf_op jit(solution)/shard_map/ppermute | solution.py:544
  86.5 9.6 %collective-permute-start.25 = (f32[128,128]{1,0:T(8,128)S(1)}, f32[128,128]{1,0:T(8,128)S(1)}, u32[]{:S(2)}, u32[]{:S(2)}) collective-permute-start(f32[128,128]{1,0:T(8,128)S(1)} %get-tuple-element.91), channel_id=1, source_target_pairs={{0,4},{1,5},{2,6},{3,7},{4,0},{5,1},{6,2},{7,3},{8,12},{9,13},{10,... | collective-permute-start | bytes 196616 | tf_op jit(solution)/shard_map/ppermute | solution.py:544
  88.1 11.2 %collective-permute-start.26 = (f32[128,128]{1,0:T(8,128)S(1)}, f32[128,128]{1,0:T(8,128)S(1)}, u32[]{:S(2)}, u32[]{:S(2)}) collective-permute-start(f32[128,128]{1,0:T(8,128)S(1)} %get-tuple-element.92), channel_id=1, source_target_pairs={{0,5},{1,4},{2,7},{3,6},{4,1},{5,0},{6,3},{7,2},{8,13},{9,12},{10,... | collective-permute-start | bytes 196616 | tf_op jit(solution)/shard_map/ppermute | solution.py:544
  89.3 10.2 %collective-permute-start.27 = (f32[128,128]{1,0:T(8,128)S(1)}, f32[128,128]{1,0:T(8,128)S(1)}, u32[]{:S(2)}, u32[]{:S(2)}) collective-permute-start(f32[128,128]{1,0:T(8,128)S(1)} %get-tuple-element.93), channel_id=1, source_target_pairs={{0,6},{1,7},{2,4},{3,5},{4,2},{5,3},{6,0},{7,1},{8,14},{9,15},{10,... | collective-permute-start | bytes 196616 | tf_op jit(solution)/shard_map/ppermute | solution.py:544
  96.1 6.0 %collective-permute-start.28 = (f32[128,128]{1,0:T(8,128)S(1)}, f32[128,128]{1,0:T(8,128)S(1)}, u32[]{:S(2)}, u32[]{:S(2)}) collective-permute-start(f32[128,128]{1,0:T(8,128)S(1)} %get-tuple-element.94), channel_id=1, source_target_pairs={{0,7},{1,6},{2,5},{3,4},{4,3},{5,2},{6,1},{7,0},{8,15},{9,14},{10,... | collective-permute-start | bytes 196616 | tf_op jit(solution)/shard_map/ppermute | solution.py:544
  97.8 13.9 %copy-start.3 = (f32[128,256]{1,0:T(8,128)S(1)}, f32[128,256]{1,0:T(8,128)}, u32[]{:S(2)}) copy-start(f32[128,256]{1,0:T(8,128)} %constant.39.clone.middle_ref) | copy-start | bytes 393220
  97.8 13.9 %copy-start.4 = (f32[16,256]{1,0:T(8,128)S(1)}, f32[16,256]{1,0:T(8,128)}, u32[]{:S(2)}) copy-start(f32[16,256]{1,0:T(8,128)} %constant.41.clone.twist_ref) | copy-start | bytes 49156
  97.8 13.9 %copy-start.5 = (f32[16,256]{1,0:T(8,128)S(1)}, f32[16,256]{1,0:T(8,128)}, u32[]{:S(2)}) copy-start(f32[16,256]{1,0:T(8,128)} %constant.38.clone.inner_ref) | copy-start | bytes 49156
  97.8 13.9 %copy-start.6 = (f32[1,2048]{1,0:T(1,128)S(1)}, f32[1,2048]{1,0:T(1,128)}, u32[]{:S(2)}) copy-start(f32[1,2048]{1,0:T(1,128)} %d_ref.3) | copy-start | bytes 24580
  97.8 13.9 %copy-start.7 = (f32[16,16]{1,0:T(8,128)S(1)}, f32[16,16]{1,0:T(8,128)}, u32[]{:S(2)}) copy-start(f32[16,16]{1,0:T(8,128)} %constant.43.clone.sin_ref) | copy-start | bytes 3076
  97.8 13.8 %copy-start.8 = (f32[16,16]{1,0:T(8,128)S(1)}, f32[16,16]{1,0:T(8,128)}, u32[]{:S(2)}) copy-start(f32[16,16]{1,0:T(8,128)} %constant.42.clone.cos_ref) | copy-start | bytes 3076
  97.9 13.8 %copy-start.9 = (f32[16,128]{1,0:T(8,128)S(1)}, f32[16,128]{1,0:T(8,128)}, u32[]{:S(2)}) copy-start(f32[16,128]{1,0:T(8,128)} %constant.40.clone.member_ref) | copy-start | bytes 24580
  99.4 6.1 %collective-permute-start.12 = (f32[128,128]{1,0:T(8,128)S(1)}, f32[128,128]{1,0:T(8,128)S(1)}, u32[]{:S(2)}, u32[]{:S(2)}) collective-permute-start(f32[128,128]{1,0:T(8,128)S(1)} %get-tuple-element.75), channel_id=1, source_target_pairs={{0,1},{1,0},{2,3},{3,2},{4,5},{5,4},{6,7},{7,6},{8,9},{9,8},{10,11... | collective-permute-start | bytes 196616 | tf_op jit(solution)/shard_map/ppermute | solution.py:544
  99.4 7.9 %collective-permute-start.13 = (f32[128,128]{1,0:T(8,128)S(1)}, f32[128,128]{1,0:T(8,128)S(1)}, u32[]{:S(2)}, u32[]{:S(2)}) collective-permute-start(f32[128,128]{1,0:T(8,128)S(1)} %get-tuple-element.76), channel_id=1, source_target_pairs={{0,2},{1,3},{2,0},{3,1},{4,6},{5,7},{6,4},{7,5},{8,10},{9,11},{10,... | collective-permute-start | bytes 196616 | tf_op jit(solution)/shard_map/ppermute | solution.py:544
  103.5 4.6 %collective-permute-start.29 = (f32[128,128]{1,0:T(8,128)S(1)}, f32[128,128]{1,0:T(8,128)S(1)}, u32[]{:S(2)}, u32[]{:S(2)}) collective-permute-start(f32[128,128]{1,0:T(8,128)S(1)} %get-tuple-element.96), channel_id=1, source_target_pairs={{0,1},{1,0},{2,3},{3,2},{4,5},{5,4},{6,7},{7,6},{8,9},{9,8},{10,11... | collective-permute-start | bytes 196616 | tf_op jit(solution)/shard_map/ppermute | solution.py:544
  103.7 5.8 %collective-permute-start.30 = (f32[128,128]{1,0:T(8,128)S(1)}, f32[128,128]{1,0:T(8,128)S(1)}, u32[]{:S(2)}, u32[]{:S(2)}) collective-permute-start(f32[128,128]{1,0:T(8,128)S(1)} %get-tuple-element.97), channel_id=1, source_target_pairs={{0,2},{1,3},{2,0},{3,1},{4,6},{5,7},{6,4},{7,5},{8,10},{9,11},{10,... | collective-permute-start | bytes 196616 | tf_op jit(solution)/shard_map/ppermute | solution.py:544
  103.7 13.3 %collective-permute-start.31 = (f32[128,128]{1,0:T(8,128)S(1)}, f32[128,128]{1,0:T(8,128)S(1)}, u32[]{:S(2)}, u32[]{:S(2)}) collective-permute-start(f32[128,128]{1,0:T(8,128)S(1)} %get-tuple-element.98), channel_id=1, source_target_pairs={{0,3},{1,2},{2,1},{3,0},{4,7},{5,6},{6,5},{7,4},{8,11},{9,10},{10,... | collective-permute-start | bytes 196616 | tf_op jit(solution)/shard_map/ppermute | solution.py:544
  105.5 11.7 %collective-permute-start.32 = (f32[128,128]{1,0:T(8,128)S(1)}, f32[128,128]{1,0:T(8,128)S(1)}, u32[]{:S(2)}, u32[]{:S(2)}) collective-permute-start(f32[128,128]{1,0:T(8,128)S(1)} %get-tuple-element.99), channel_id=1, source_target_pairs={{0,4},{1,5},{2,6},{3,7},{4,0},{5,1},{6,2},{7,3},{8,12},{9,13},{10,... | collective-permute-start | bytes 196616 | tf_op jit(solution)/shard_map/ppermute | solution.py:544
  107.3 11.7 %collective-permute-start.33 = (f32[128,128]{1,0:T(8,128)S(1)}, f32[128,128]{1,0:T(8,128)S(1)}, u32[]{:S(2)}, u32[]{:S(2)}) collective-permute-start(f32[128,128]{1,0:T(8,128)S(1)} %get-tuple-element.100), channel_id=1, source_target_pairs={{0,5},{1,4},{2,7},{3,6},{4,1},{5,0},{6,3},{7,2},{8,13},{9,12},{10,... | collective-permute-start | bytes 196616 | tf_op jit(solution)/shard_map/ppermute | solution.py:544
  108.1 11.8 %collective-permute-start.34 = (f32[128,128]{1,0:T(8,128)S(1)}, f32[128,128]{1,0:T(8,128)S(1)}, u32[]{:S(2)}, u32[]{:S(2)}) collective-permute-start(f32[128,128]{1,0:T(8,128)S(1)} %get-tuple-element.101), channel_id=1, source_target_pairs={{0,6},{1,7},{2,4},{3,5},{4,2},{5,3},{6,0},{7,1},{8,14},{9,15},{10,... | collective-permute-start | bytes 196616 | tf_op jit(solution)/shard_map/ppermute | solution.py:544
  109.5 12.1 %collective-permute-start.35 = (f32[128,128]{1,0:T(8,128)S(1)}, f32[128,128]{1,0:T(8,128)S(1)}, u32[]{:S(2)}, u32[]{:S(2)}) collective-permute-start(f32[128,128]{1,0:T(8,128)S(1)} %get-tuple-element.102), channel_id=1, source_target_pairs={{0,7},{1,6},{2,5},{3,4},{4,3},{5,2},{6,1},{7,0},{8,15},{9,14},{10,... | collective-permute-start | bytes 196616 | tf_op jit(solution)/shard_map/ppermute | solution.py:544
  117.1 8.0 %collective-permute-start.14 = (f32[128,128]{1,0:T(8,128)S(1)}, f32[128,128]{1,0:T(8,128)S(1)}, u32[]{:S(2)}, u32[]{:S(2)}) collective-permute-start(f32[128,128]{1,0:T(8,128)S(1)} %get-tuple-element.77), channel_id=1, source_target_pairs={{0,3},{1,2},{2,1},{3,0},{4,7},{5,6},{6,5},{7,4},{8,11},{9,10},{10,... | collective-permute-start | bytes 196616 | tf_op jit(solution)/shard_map/ppermute | solution.py:544
  117.2 11.3 %collective-permute-start.15 = (f32[128,128]{1,0:T(8,128)S(1)}, f32[128,128]{1,0:T(8,128)S(1)}, u32[]{:S(2)}, u32[]{:S(2)}) collective-permute-start(f32[128,128]{1,0:T(8,128)S(1)} %get-tuple-element.78), channel_id=1, source_target_pairs={{0,4},{1,5},{2,6},{3,7},{4,0},{5,1},{6,2},{7,3},{8,12},{9,13},{10,... | collective-permute-start | bytes 196616 | tf_op jit(solution)/shard_map/ppermute | solution.py:544
  119.1 10.3 %collective-permute-start.16 = (f32[128,128]{1,0:T(8,128)S(1)}, f32[128,128]{1,0:T(8,128)S(1)}, u32[]{:S(2)}, u32[]{:S(2)}) collective-permute-start(f32[128,128]{1,0:T(8,128)S(1)} %get-tuple-element.79), channel_id=1, source_target_pairs={{0,5},{1,4},{2,7},{3,6},{4,1},{5,0},{6,3},{7,2},{8,13},{9,12},{10,... | collective-permute-start | bytes 196616 | tf_op jit(solution)/shard_map/ppermute | solution.py:544
  119.9 9.5 %collective-permute-start.17 = (f32[128,128]{1,0:T(8,128)S(1)}, f32[128,128]{1,0:T(8,128)S(1)}, u32[]{:S(2)}, u32[]{:S(2)}) collective-permute-start(f32[128,128]{1,0:T(8,128)S(1)} %get-tuple-element.80), channel_id=1, source_target_pairs={{0,6},{1,7},{2,4},{3,5},{4,2},{5,3},{6,0},{7,1},{8,14},{9,15},{10,... | collective-permute-start | bytes 196616 | tf_op jit(solution)/shard_map/ppermute | solution.py:544
  121.6 7.7 %collective-permute-start.18 = (f32[128,128]{1,0:T(8,128)S(1)}, f32[128,128]{1,0:T(8,128)S(1)}, u32[]{:S(2)}, u32[]{:S(2)}) collective-permute-start(f32[128,128]{1,0:T(8,128)S(1)} %get-tuple-element.81), channel_id=1, source_target_pairs={{0,7},{1,6},{2,5},{3,4},{4,3},{5,2},{6,1},{7,0},{8,15},{9,14},{10,... | collective-permute-start | bytes 196616 | tf_op jit(solution)/shard_map/ppermute | solution.py:544

commit v4 on v3

--- a/solution.py
+++ b/solution.py
@@ -442,38 +442,54 @@
     )(here, *blocks, *matrices)
 
 
-def gather_rows(here, bands, blocks, gathered):
+def gather_rows(places, blocks, gathered):
     band, columns = blocks[0].shape
-    for shift in range(bands):
-        source = jnp.bitwise_xor(here, shift)
-        at = pl.ds(pl.multiple_of(source * columns, columns), columns)
-        hi, lo = split(blocks[shift][...])
+    for place, block in zip(places, blocks):
+        at = pl.ds(pl.multiple_of(place * columns, columns), columns)
+        hi, lo = split(block[...])
         gathered[:band, at] = hi
         gathered[band:, at] = lo
 
 
 def lon_product(band, hi, lo, gathered):
     dot = functools.partial(jnp.dot, preferred_element_type=jnp.float32)
-    both = dot(gathered[...], hi[...])
-    return both[:band] + both[band:] + dot(gathered[:band], lo[...])
-
-
-def lon_even_kernel(bands, here_ref, *refs):
-    blocks, (hi, lo, out, gathered) = refs[:bands], refs[bands:]
-    gather_rows(here_ref[0], bands, blocks, gathered)
-    out[...] = lon_product(blocks[0].shape[0], hi, lo, gathered)
-
-
-def lon_odd_kernel(bands, here_ref, *refs):
-    blocks, (hi, lo, even, field, out, gathered, result, sems) = refs[:bands], refs[bands:]
-    gather_rows(here_ref[0], bands, blocks, gathered)
-    half = hi.shape[0]
-    band, parts = blocks[0].shape[0], sems.shape[0]
+    both = dot(gathered[...], hi)
+    return both[:band] + both[band:] + dot(gathered[:band], lo)
+
+
+def lon_even_kernel(here_ref, *refs):
+    blocks, (hi, lo, out, gathered) = refs[:-4], refs[-4:]
+    gather_rows([jnp.bitwise_xor(here_ref[0], shift) for shift in range(len(blocks))], blocks, gathered)
+    out[...] = lon_product(blocks[0].shape[0], hi[...], lo[...], gathered)
+
+
+def lon_half(here, count, far):
+    half = jnp.bitwise_and(here, count)
+    first = count - half if far else half
+    return [jnp.bitwise_xor(jnp.bitwise_and(here, count - 1), shift) for shift in range(count)], first
+
+
+def lon_near_kernel(here_ref, *refs):
+    blocks, (hi, lo, out, gathered) = refs[:-4], refs[-4:]
+    band, columns = blocks[0].shape
+    places, first = lon_half(here_ref[0], len(blocks), False)
+    gather_rows(places, blocks, gathered)
+    rows = pl.ds(pl.multiple_of(first * columns, columns), len(blocks) * columns)
+    out[...] = lon_product(band, hi[rows], lo[rows], gathered)
+
+
+def lon_far_kernel(here_ref, *refs):
+    blocks, (hi, lo, even, near, field, out, gathered, result, sems) = refs[:-9], refs[-9:]
+    band, columns = blocks[0].shape
+    places, first = lon_half(here_ref[0], len(blocks), True)
+    gather_rows(places, blocks, gathered)
+    rows = pl.ds(pl.multiple_of(first * columns, columns), len(blocks) * columns)
+    half, parts = hi.shape[0], sems.shape[0]
     chunk = half // parts
     copies = []
     for part in range(parts):
         cols = slice(part * chunk, (part + 1) * chunk)
-        odd = lon_product(band, hi.at[:, cols], lo.at[:, cols], gathered)
+        odd = near[:, cols] + lon_product(band, hi[rows, cols], lo[rows, cols], gathered)
         for side, value in enumerate((even[:, cols] + odd, even[:, cols] - odd)):
             at = slice(side * half + part * chunk, side * half + (part + 1) * chunk)
             result[:, at] = field[:, at] + 0.5 * value
@@ -483,22 +499,22 @@
         copy.wait()
 
 
-def lon_apply(here, blocks, matrices, extra=()):
-    bands = len(blocks)
-    band, _ = blocks[0].shape
+def lon_apply(kernel, here, blocks, matrices, extra=()):
+    band, columns = blocks[0].shape
     half = matrices[0].shape[0]
-    scratch = [pltpu.VMEM((2 * band, half), jnp.bfloat16)]
+    depth = len(blocks) * columns
+    scratch = [pltpu.VMEM((2 * band, depth), jnp.bfloat16)]
     if extra:
         scratch += [pltpu.VMEM((band, 2 * half), jnp.float32), pltpu.SemaphoreType.DMA((4, 2))]
     return pl.pallas_call(
-        functools.partial(lon_odd_kernel if extra else lon_even_kernel, bands),
+        kernel,
         out_shape=jax.ShapeDtypeStruct((band, 2 * half if extra else half), jnp.float32),
-        in_specs=[SMEM] + [VMEM] * (bands + 2 + len(extra)),
+        in_specs=[SMEM] + [VMEM] * (len(blocks) + 2 + len(extra)),
         out_specs=ANY if extra else VMEM,
         scratch_shapes=scratch,
         compiler_params=LIMIT,
         cost_estimate=pl.CostEstimate(
-            flops=6 * band * half * half, bytes_accessed=4 * half * half, transcendentals=0
+            flops=6 * band * depth * half, bytes_accessed=4 * depth * half, transcendentals=0
         ),
         name="lon_apply",
     )(here, *blocks, *matrices, *extra)
@@ -572,9 +588,9 @@
     x, mult = state[0, 0], multipliers[0, 0]
     rims = jnp.concatenate([x[:2], x[-2:]])
     edges = (
+        lax.ppermute(rims, "lat", [pair for i in range(1, bands - 1, 2) for pair in ((i, i + 1), (i + 1, i))]),
         lax.ppermute(rims, "lat", [(i, i ^ 1) for i in range(bands)]),
-        lax.ppermute(rims, "lat", [pair for i in range(1, bands - 1, 2) for pair in ((i, i + 1), (i + 1, i))]),
-    )
+    )[::-1]
     x, own, x1, plus, minus, near, side = forecast(here, bands, jnp.concatenate([speed, drift, kappa]), x, mult, edges)
     near = hop(near, [(0, 1), (1, 0), (2, 3)])
     side = hop(side, [(0, 2), (1, 3)])
@@ -593,9 +609,11 @@
     odd = resid_blocks(here, bands, ODD, base_minus, side, cross, third)
     even, odd = exchange(even), exchange(odd)
     even = lat_apply(here, even, lat_matrices)
-    even, odd = exchange(even), exchange(lat_apply(here, odd, lat_matrices))
-    even = lon_apply(here, even, lon_matrices[:2])
-    field = lon_apply(here, odd, lon_matrices[2:], (even, x))
+    odd = lat_apply(here, odd, lat_matrices)
+    even, odd = exchange(even), exchange(odd)
+    even = lon_apply(lon_even_kernel, here, even, lon_matrices[:2])
+    near_odd = lon_apply(lon_near_kernel, here, odd[:bands // 2], lon_matrices[2:])
+    field = lon_apply(lon_far_kernel, here, odd[bands // 2:], lon_matrices[2:], (even, near_odd, x))
     lam = new_multipliers(here, own, plus, minus, near, direct)
     return (field[None, None], lam[None, None])
 

time: 134 us -> 134 us (level)
    pallas_call x2 -> x3, Pallas kernels: 4.27 us -> 4.9 us  [lon_apply(): pl.pallas_call(kernel, out_shape=jax.ShapeDtypeStruct((band, 2 * half if...]
  transfers between devices with their start and end apart: 38 -> 38, of which waited for: 9 -> 9; matrix products, arithmetic and copies ran while one was open for 0% -> 0% of each run, Pallas kernels for 12% -> 13%
where the time goes in v4:
time: 134 us; the launch traced here: 133 us
  starting transfers between devices  65.3 us (49%)
  waiting for transfers between devices  37.9 us (28%)
  Pallas kernels  23.4 us (17%)
  between operations  3.22 us (2%)
  local copies, waits for them, and re-layouts  2.72 us (2%)
    ppermute x28, starting transfers between devices, exchange(): moved[shift] = lax.ppermute(blocks[shift], 'lat', route)  36.1 us
    ppermute x8, waiting for transfers between devices, hop(): return lax.ppermute(value, 'win', pairs)  26.2 us
    ppermute x8, starting transfers between devices, hop(): return lax.ppermute(value, 'win', pairs)  24.1 us
    ppermute x28, waiting for transfers between devices, exchange(): moved[shift] = lax.ppermute(blocks[shift], 'lat', route)  11.7 us
    pallas_call x2, Pallas kernels, build(): pl.pallas_call(functools.partial(build_kernel, count), out_shape=[shape]...  5.3 us
    pallas_call x3, Pallas kernels, lon_apply(): pl.pallas_call(kernel, out_shape=jax.ShapeDtypeStruct((band, 2 * half if...  4.9 us
    ppermute x1, starting transfers between devices, per_device_hops(): lax.ppermute(rims, 'lat', [(i, i ^ 1) for i in range(bands)])  4.48 us
    pallas_call x1, Pallas kernels, forecast(): pl.pallas_call(functools.partial(forecast_kernel, bands), out_shape=[whol...  4.44 us
  transfers between devices with their start and end apart: 38, of which 9 were waited for; matrix products, arithmetic and copies ran while one was open for 0% of the time, Pallas kernels for 13%

profile of v4, /device:TPU:0, one launch (start us, length us, event | category | flops | bytes accessed | tf_op | source)
XLA Modules:
  0.0 132.7 jit_solution(9027121393878216732)
XLA Ops:
  0.6 1.0 slice_bitcast_fusion.1
  1.7 0.7 collective-permute-start.1
  2.4 4.5 %collective-permute-start = (f32[4,2048]{1,0:T(4,128)S(1)}, f32[4,2048]{1,0:T(4,128)S(1)}, u32[]{:S(2)}, u32[]{:S(2)}) collective-permute-start(f32[4,2048]{1,0:T(4,128)S(1)} %pad_maximum_fusion), channel_id=1, source_target_pairs={{0,1},{1,0},{2,3},{3,2},{4,5},{5,4},{6,7},{7,6},{8,9},{9,8},{10,11... | collective-permute-start | bytes 98312 | tf_op jit(solution)/shard_map/ppermute | solution.py:592
  8.8 0.1 pad_add_fusion.here_ref
  8.9 0.1 pad_maximum_fusion.1.model
  9.0 4.4 %forecast.1 = (f32[128,2048]{1,0:T(8,128)S(1)}, f32[128,2048]{1,0:T(8,128)S(1)}, f32[128,2048]{1,0:T(8,128)S(1)}, f32[128,1024]{1,0:T(8,128)S(1)}, f32[128,1024]...) custom-call(s32[2]{0:T(128)S(1)} %pad_add_fusion.here_ref, f32[3]{0:T(128)S(1)} %pad_maximum_fusion.1.model, ...), custom_call_target="tpu_custom_call" | custom-call | flops 10485760 | bytes 5242880 | tf_op jit(solution)/shard_map/forecast/pallas_call | solution.py:298
  13.4 3.5 %collective-permute-start.2 = (f32[128,1024]{1,0:T(8,128)S(1)}, f32[128,1024]{1,0:T(8,128)S(1)}, u32[]{:S(2)}, u32[]{:S(2)}) collective-permute-start(f32[128,1024]{1,0:T(8,128)S(1)} %get-tuple-element.59), channel_id=1, source_target_pairs={{0,16},{8,24},{1,17},{9,25},{2,18},{10,26},{3,19},{11,27},{4,20},{... | collective-permute-start | bytes 1572872 | tf_op jit(solution)/shard_map/ppermute | solution.py:565
  16.9 3.4 %collective-permute-start.16 = (f32[128,1024]{1,0:T(8,128)S(1)}, f32[128,1024]{1,0:T(8,128)S(1)}, u32[]{:S(2)}, u32[]{:S(2)}) collective-permute-start(f32[128,1024]{1,0:T(8,128)S(1)} %get-tuple-element.81), channel_id=1, source_target_pairs={{0,8},{8,0},{16,24},{1,9},{9,1},{17,25},{2,10},{10,2},{18,26},{3,1... | collective-permute-start | bytes 1572872 | tf_op jit(solution)/shard_map/ppermute | solution.py:565
  20.3 1.6 %copy-done.1 = s32[1,2,128,2048]{3,2,1,0:T(8,128)S(1)} copy-done((s32[1,2,128,2048]{3,2,1,0:T(8,128)S(1)}, s32[1,2,128,2048]{3,2,1,0:T(8,128)}, u32[]{:S(2)}) %copy-start.1) | copy-done | bytes 2097176
  21.9 1.4 %defect.1 = (f32[128,1024]{1,0:T(8,128)S(1)}, f32[128,1024]{1,0:T(8,128)S(1)}, f32[128,1024]{1,0:T(8,128)S(1)}, f32[128,1024]{1,0:T(8,128)S(1)}, f32[128,1024]{1,0:T(8,128)S(1)}) custom-call(s32[2]{0:T(128)S(1)} %pad_add_fusion.here_ref, f32[128,2048]{1,0:T(8,128)S(1)} %get-tuple-element.54.own_ref, f32[2,128,2048]{2,1,0:T(8,128)S(1)} %bitcast.12, ...), custom_call_target="tpu_custom_call" | custom-call | flops 7864320 | bytes 10485760 | tf_op jit(solution)/shard_map/defect/pallas_call | solution.py:341
  23.3 2.5 %collective-permute-start.4 = (f32[128,1024]{1,0:T(8,128)S(1)}, f32[128,1024]{1,0:T(8,128)S(1)}, u32[]{:S(2)}, u32[]{:S(2)}) collective-permute-start(f32[128,1024]{1,0:T(8,128)S(1)} %get-tuple-element.61), channel_id=1, source_target_pairs={{0,8},{8,24},{1,9},{9,25},{2,10},{10,26},{3,11},{11,27},{4,12},{12... | collective-permute-start | bytes 1572872 | tf_op jit(solution)/shard_map/ppermute | solution.py:565
  25.8 2.4 %collective-permute-done.2.other_ref.refs_0_ = f32[128,1024]{1,0:T(8,128)S(1)} collective-permute-done((f32[128,1024]{1,0:T(8,128)S(1)}, f32[128,1024]{1,0:T(8,128)S(1)}, u32[]{:S(2)}, u32[]{:S(2)}) %collective-permute-start.2) | collective-permute-done | bytes 524320 | tf_op jit(solution)/shard_map/ppermute | solution.py:565
  28.2 0.6 mix.2
  28.8 0.7 collective-permute-start.3
  29.5 4.4 %collective-permute-start.18 = (f32[128,1024]{1,0:T(8,128)S(1)}, f32[128,1024]{1,0:T(8,128)S(1)}, u32[]{:S(2)}, u32[]{:S(2)}) collective-permute-start(f32[128,1024]{1,0:T(8,128)S(1)} %get-tuple-element.60.one_ref), channel_id=1, source_target_pairs={{0,8},{1,9},{2,10},{3,11},{4,12},{5,13},{6,14},{7,15}} | collective-permute-start | bytes 1572872 | tf_op jit(solution)/shard_map/ppermute | solution.py:565
  33.9 0.6 mix.3
  34.5 4.4 %collective-permute-start.17 = (f32[128,1024]{1,0:T(8,128)S(1)}, f32[128,1024]{1,0:T(8,128)S(1)}, u32[]{:S(2)}, u32[]{:S(2)}) collective-permute-start(f32[128,1024]{1,0:T(8,128)S(1)} %mix.3), channel_id=1, source_target_pairs={{0,16},{8,24},{1,17},{9,25},{2,18},{10,26},{3,19},{11,27},{4,20},{... | collective-permute-start | bytes 1572872 | tf_op jit(solution)/shard_map/ppermute | solution.py:565
  38.9 0.7 collective-permute-start.36
  39.6 4.2 %collective-permute-done.4.refs_2_ = f32[128,1024]{1,0:T(8,128)S(1)} collective-permute-done((f32[128,1024]{1,0:T(8,128)S(1)}, f32[128,1024]{1,0:T(8,128)S(1)}, u32[]{:S(2)}, u32[]{:S(2)}) %collective-permute-start.4) | collective-permute-done | bytes 524320 | tf_op jit(solution)/shard_map/ppermute | solution.py:565
  43.8 4.6 %collective-permute-start.37 = (f32[128,1024]{1,0:T(8,128)S(1)}, f32[128,1024]{1,0:T(8,128)S(1)}, u32[]{:S(2)}, u32[]{:S(2)}) collective-permute-start(f32[128,1024]{1,0:T(8,128)S(1)} %get-tuple-element.57.minus_ref), channel_id=1, source_target_pairs={{0,8},{8,16},{16,24},{1,9},{9,17},{17,25},{2,10},{10,18},{18,26},{... | collective-permute-start | bytes 1572872 | tf_op jit(solution)/shard_map/ppermute | solution.py:565
  48.4 0.0 copy-start.2
  48.4 0.0 copy-start.10
  48.4 0.0 copy-start.11
  48.5 0.8 resid_blocks.2
  49.3 0.1 collective-permute-start.5
  49.4 5.6 %collective-permute-done.18.refs_2_.direct_ref = f32[128,1024]{1,0:T(8,128)S(1)} collective-permute-done((f32[128,1024]{1,0:T(8,128)S(1)}, f32[128,1024]{1,0:T(8,128)S(1)}, u32[]{:S(2)}, u32[]{:S(2)}) %collective-permute-start.18) | collective-permute-done | bytes 524320 | tf_op jit(solution)/shard_map/ppermute | solution.py:565
  55.0 1.6 %collective-permute-start.6 = (f32[128,128]{1,0:T(8,128)S(1)}, f32[128,128]{1,0:T(8,128)S(1)}, u32[]{:S(2)}, u32[]{:S(2)}) collective-permute-start(f32[128,128]{1,0:T(8,128)S(1)} %get-tuple-element.64), channel_id=1, source_target_pairs={{0,2},{1,3},{2,0},{3,1},{4,6},{5,7},{6,4},{7,5},{8,10},{9,11},{10,... | collective-permute-start | bytes 196616 | tf_op jit(solution)/shard_map/ppermute | solution.py:560
  56.6 14.0 %collective-permute-done.17.refs_1_ = f32[128,1024]{1,0:T(8,128)S(1)} collective-permute-done((f32[128,1024]{1,0:T(8,128)S(1)}, f32[128,1024]{1,0:T(8,128)S(1)}, u32[]{:S(2)}, u32[]{:S(2)}) %collective-permute-start.17) | collective-permute-done | bytes 524320 | tf_op jit(solution)/shard_map/ppermute | solution.py:565
  70.6 2.6 %collective-permute-start.8 = (f32[128,128]{1,0:T(8,128)S(1)}, f32[128,128]{1,0:T(8,128)S(1)}, u32[]{:S(2)}, u32[]{:S(2)}) collective-permute-start(f32[128,128]{1,0:T(8,128)S(1)} %get-tuple-element.66), channel_id=1, source_target_pairs={{0,4},{1,5},{2,6},{3,7},{4,0},{5,1},{6,2},{7,3},{8,12},{9,13},{10,... | collective-permute-start | bytes 196616 | tf_op jit(solution)/shard_map/ppermute | solution.py:560
  73.2 1.3 %collective-permute-start.9 = (f32[128,128]{1,0:T(8,128)S(1)}, f32[128,128]{1,0:T(8,128)S(1)}, u32[]{:S(2)}, u32[]{:S(2)}) collective-permute-start(f32[128,128]{1,0:T(8,128)S(1)} %get-tuple-element.67), channel_id=1, source_target_pairs={{0,5},{1,4},{2,7},{3,6},{4,1},{5,0},{6,3},{7,2},{8,13},{9,12},{10,... | collective-permute-start | bytes 196616 | tf_op jit(solution)/shard_map/ppermute | solution.py:560
  74.5 0.8 resid_blocks.3
  75.4 2.5 %collective-permute-start.10 = (f32[128,128]{1,0:T(8,128)S(1)}, f32[128,128]{1,0:T(8,128)S(1)}, u32[]{:S(2)}, u32[]{:S(2)}) collective-permute-start(f32[128,128]{1,0:T(8,128)S(1)} %get-tuple-element.68), channel_id=1, source_target_pairs={{0,6},{1,7},{2,4},{3,5},{4,2},{5,3},{6,0},{7,1},{8,14},{9,15},{10,... | collective-permute-start | bytes 196616 | tf_op jit(solution)/shard_map/ppermute | solution.py:560
  77.9 4.0 %collective-permute-start.11 = (f32[128,128]{1,0:T(8,128)S(1)}, f32[128,128]{1,0:T(8,128)S(1)}, u32[]{:S(2)}, u32[]{:S(2)}) collective-permute-start(f32[128,128]{1,0:T(8,128)S(1)} %get-tuple-element.69), channel_id=1, source_target_pairs={{0,7},{1,6},{2,5},{3,4},{4,3},{5,2},{6,1},{7,0},{8,15},{9,14},{10,... | collective-permute-start | bytes 196616 | tf_op jit(solution)/shard_map/ppermute | solution.py:560
  81.9 0.2 collective-permute-done.9.refs_5_
  82.2 2.5 %collective-permute-start.20 = (f32[128,128]{1,0:T(8,128)S(1)}, f32[128,128]{1,0:T(8,128)S(1)}, u32[]{:S(2)}, u32[]{:S(2)}) collective-permute-start(f32[128,128]{1,0:T(8,128)S(1)} %get-tuple-element.85), channel_id=1, source_target_pairs={{0,2},{1,3},{2,0},{3,1},{4,6},{5,7},{6,4},{7,5},{8,10},{9,11},{10,... | collective-permute-start | bytes 196616 | tf_op jit(solution)/shard_map/ppermute | solution.py:560
  84.7 1.8 %collective-permute-start.21 = (f32[128,128]{1,0:T(8,128)S(1)}, f32[128,128]{1,0:T(8,128)S(1)}, u32[]{:S(2)}, u32[]{:S(2)}) collective-permute-start(f32[128,128]{1,0:T(8,128)S(1)} %get-tuple-element.86), channel_id=1, source_target_pairs={{0,3},{1,2},{2,1},{3,0},{4,7},{5,6},{6,5},{7,4},{8,11},{9,10},{10,... | collective-permute-start | bytes 196616 | tf_op jit(solution)/shard_map/ppermute | solution.py:560
  86.5 1.6 %collective-permute-start.22 = (f32[128,128]{1,0:T(8,128)S(1)}, f32[128,128]{1,0:T(8,128)S(1)}, u32[]{:S(2)}, u32[]{:S(2)}) collective-permute-start(f32[128,128]{1,0:T(8,128)S(1)} %get-tuple-element.87), channel_id=1, source_target_pairs={{0,4},{1,5},{2,6},{3,7},{4,0},{5,1},{6,2},{7,3},{8,12},{9,13},{10,... | collective-permute-start | bytes 196616 | tf_op jit(solution)/shard_map/ppermute | solution.py:560
  88.1 1.2 collective-permute-start.23
  89.2 1.9 %collective-permute-start.24 = (f32[128,128]{1,0:T(8,128)S(1)}, f32[128,128]{1,0:T(8,128)S(1)}, u32[]{:S(2)}, u32[]{:S(2)}) collective-permute-start(f32[128,128]{1,0:T(8,128)S(1)} %get-tuple-element.89), channel_id=1, source_target_pairs={{0,6},{1,7},{2,4},{3,5},{4,2},{5,3},{6,0},{7,1},{8,14},{9,15},{10,... | collective-permute-start | bytes 196616 | tf_op jit(solution)/shard_map/ppermute | solution.py:560
  91.1 4.9 %collective-permute-done.22.refs_4_ = f32[128,128]{1,0:T(8,128)S(1)} collective-permute-done((f32[128,128]{1,0:T(8,128)S(1)}, f32[128,128]{1,0:T(8,128)S(1)}, u32[]{:S(2)}, u32[]{:S(2)}) %collective-permute-start.22) | collective-permute-done | bytes 65568 | tf_op jit(solution)/shard_map/ppermute | solution.py:560
  96.1 1.6 %shard_map.212 = (bf16[512,512]{1,0:T(8,128)(2,1)S(1)}, bf16[512,512]{1,0:T(8,128)(2,1)S(1)}, bf16[512,512]{1,0:T(8,128)(2,1)S(1)}, bf16[512,512]{1,0:T(8,128)(2,1)S(1)}) custom-call(f32[1,1024]{1,0:T(1,128)S(1)} %copy-done.12, f32[8,256]{1,0:T(8,128)S(1)} %copy-done.11, f32[128,256]{1,0:T(8,128)S(1)} %copy-done.2, f32[8,128]{1,0:T(8,128)S(1)} %copy-done.15, ...), custom_call_target="tpu_custom_call" | custom-call | flops 4194304 | bytes 2097152 | tf_op jit(solution)/shard_map/pallas_call | solution.py:110
  97.9 1.5 %lat_apply.2 = (f32[128,128]{1,0:T(8,128)S(1)}, f32[128,128]{1,0:T(8,128)S(1)}, f32[128,128]{1,0:T(8,128)S(1)}, f32[128,128]{1,0:T(8,128)S(1)}, f32[128,128]{1,0...) custom-call(s32[2]{0:T(128)S(1)} %pad_add_fusion.here_ref, ...), custom_call_target="tpu_custom_call" | custom-call | flops 402653184 | bytes 2097152 | tf_op jit(solution)/shard_map/lat_apply/pallas_call | solution.py:428
  99.3 0.1 collective-permute-start.33
  99.4 0.2 collective-permute-start.34
  99.6 2.4 %collective-permute-done.25.refs_7_ = f32[128,128]{1,0:T(8,128)S(1)} collective-permute-done((f32[128,128]{1,0:T(8,128)S(1)}, f32[128,128]{1,0:T(8,128)S(1)}, u32[]{:S(2)}, u32[]{:S(2)}) %collective-permute-start.25) | collective-permute-done | bytes 65568 | tf_op jit(solution)/shard_map/ppermute | solution.py:560
  102.1 1.4 %lat_apply.3 = (f32[128,128]{1,0:T(8,128)S(1)}, f32[128,128]{1,0:T(8,128)S(1)}, f32[128,128]{1,0:T(8,128)S(1)}, f32[128,128]{1,0:T(8,128)S(1)}, f32[128,128]{1,0...) custom-call(s32[2]{0:T(128)S(1)} %pad_add_fusion.here_ref, ...), custom_call_target="tpu_custom_call" | custom-call | flops 402653184 | bytes 2097152 | tf_op jit(solution)/shard_map/lat_apply/pallas_call | solution.py:428
  103.5 0.2 collective-permute-start.26
  103.7 2.0 %collective-permute-start.27 = (f32[128,128]{1,0:T(8,128)S(1)}, f32[128,128]{1,0:T(8,128)S(1)}, u32[]{:S(2)}, u32[]{:S(2)}) collective-permute-start(f32[128,128]{1,0:T(8,128)S(1)} %get-tuple-element.93), channel_id=1, source_target_pairs={{0,2},{1,3},{2,0},{3,1},{4,6},{5,7},{6,4},{7,5},{8,10},{9,11},{10,... | collective-permute-start | bytes 196616 | tf_op jit(solution)/shard_map/ppermute | solution.py:560
  105.8 1.9 %collective-permute-start.29 = (f32[128,128]{1,0:T(8,128)S(1)}, f32[128,128]{1,0:T(8,128)S(1)}, u32[]{:S(2)}, u32[]{:S(2)}) collective-permute-start(f32[128,128]{1,0:T(8,128)S(1)} %get-tuple-element.95), channel_id=1, source_target_pairs={{0,4},{1,5},{2,6},{3,7},{4,0},{5,1},{6,2},{7,3},{8,12},{9,13},{10,... | collective-permute-start | bytes 196616 | tf_op jit(solution)/shard_map/ppermute | solution.py:560
  107.7 0.5 collective-permute-start.30
  108.2 3.2 %collective-permute-start.31 = (f32[128,128]{1,0:T(8,128)S(1)}, f32[128,128]{1,0:T(8,128)S(1)}, u32[]{:S(2)}, u32[]{:S(2)}) collective-permute-start(f32[128,128]{1,0:T(8,128)S(1)} %get-tuple-element.97), channel_id=1, source_target_pairs={{0,6},{1,7},{2,4},{3,5},{4,2},{5,3},{6,0},{7,1},{8,14},{9,15},{10,... | collective-permute-start | bytes 196616 | tf_op jit(solution)/shard_map/ppermute | solution.py:560
  111.4 0.6 collective-permute-start.32
  112.1 3.7 %shard_map.213 = (bf16[1024,1024]{1,0:T(8,128)(2,1)S(1)}, bf16[1024,1024]{1,0:T(8,128)(2,1)S(1)}, bf16[1024,1024]{1,0:T(8,128)(2,1)S(1)}, bf16[1024,1024]{1,0:T(8,128)(2,1)S(1)}) custom-call(f32[1,2048]{1,0:T(1,128)S(1)} %copy-done.6, f32[16,256]{1,0:T(8,128)S(1)} %copy-done.5, f32[128,256]{1,0:T(8,128)S(1)} %copy-done.3, f32[16,128]{1,0:T(8,128)S(1)} %copy-done.9, ...), custom_call_target="tpu_custom_call" | custom-call | flops 16777216 | bytes 8388608 | tf_op jit(solution)/shard_map/pallas_call | solution.py:110
  115.7 1.6 %new_multipliers.1 = f32[128,2048]{1,0:T(8,128)} custom-call(s32[2]{0:T(128)S(1)} %pad_add_fusion.here_ref, f32[128,2048]{1,0:T(8,128)S(1)} %get-tuple-element.54.own_ref, f32[128,1024]{1,0:T(8,128)S(1)} %collective-permute-done.36.plus_ref, f32[128,1024]{1,0:T(8,128)S(1)} %collective-permute-done.37.minus_ref, ...), custom_call_target="tpu_custom_call" | custom-call | flops 1572864 | bytes 5242880 | tf_op jit(solution)/shard_map/new_multipliers/pallas_call | solution.py:543
  117.3 1.1 lon_apply.4.refs_7_
  118.5 0.1 collective-permute-start.12
  118.6 2.3 %collective-permute-start.13 = (f32[128,128]{1,0:T(8,128)S(1)}, f32[128,128]{1,0:T(8,128)S(1)}, u32[]{:S(2)}, u32[]{:S(2)}) collective-permute-start(f32[128,128]{1,0:T(8,128)S(1)} %get-tuple-element.75), channel_id=1, source_target_pairs={{0,5},{1,4},{2,7},{3,6},{4,1},{5,0},{6,3},{7,2},{8,13},{9,12},{10,... | collective-permute-start | bytes 196616 | tf_op jit(solution)/shard_map/ppermute | solution.py:560
  120.9 3.2 %collective-permute-start.14 = (f32[128,128]{1,0:T(8,128)S(1)}, f32[128,128]{1,0:T(8,128)S(1)}, u32[]{:S(2)}, u32[]{:S(2)}) collective-permute-start(f32[128,128]{1,0:T(8,128)S(1)} %get-tuple-element.76), channel_id=1, source_target_pairs={{0,6},{1,7},{2,4},{3,5},{4,2},{5,3},{6,0},{7,1},{8,14},{9,15},{10,... | collective-permute-start | bytes 196616 | tf_op jit(solution)/shard_map/ppermute | solution.py:560
  124.2 0.6 collective-permute-start.15
  124.8 1.7 %lon_apply.3.refs_6_ = f32[128,1024]{1,0:T(8,128)S(1)} custom-call(s32[2]{0:T(128)S(1)} %pad_add_fusion.here_ref, f32[128,128]{1,0:T(8,128)S(1)} %get-tuple-element.91.refs_0_, f32[128,128]{1,0:T(8,128)S(1)} %collective-permute-done.26.refs_1_, f32[128,128]{1,0:T(8,128)S(1)} %collective-permute-done.27.refs_2_, ...), custom_call_target="tpu_custom_call" | custom-call | flops 805306368 | bytes 4194304 | tf_op jit(solution)/shard_map/lon_apply/pallas_call | solution.py:509
  126.4 2.0 %collective-permute-done.12.refs_0_ = f32[128,128]{1,0:T(8,128)S(1)} collective-permute-done((f32[128,128]{1,0:T(8,128)S(1)}, f32[128,128]{1,0:T(8,128)S(1)}, u32[]{:S(2)}, u32[]{:S(2)}) %collective-permute-start.12) | collective-permute-done | bytes 65568 | tf_op jit(solution)/shard_map/ppermute | solution.py:560
  128.5 0.0 collective-permute-done.13.refs_1_
  128.5 1.9 %collective-permute-done.15.refs_3_ = f32[128,128]{1,0:T(8,128)S(1)} collective-permute-done((f32[128,128]{1,0:T(8,128)S(1)}, f32[128,128]{1,0:T(8,128)S(1)}, u32[]{:S(2)}, u32[]{:S(2)}) %collective-permute-start.15) | collective-permute-done | bytes 65568 | tf_op jit(solution)/shard_map/ppermute | solution.py:560
  130.5 2.1 %lon_apply.5 = f32[128,2048]{1,0:T(8,128)} custom-call(s32[2]{0:T(128)S(1)} %pad_add_fusion.here_ref, f32[128,128]{1,0:T(8,128)S(1)} %collective-permute-done.12.refs_0_, f32[128,128]{1,0:T(8,128)S(1)} %collective-permute-done.13.refs_1_, f32[128,128]{1,0:T(8,128)S(1)} %collective-permute-done.14.refs_2_, f32[128,128]{1,0:T(8,128)S(1)} %collective-permute-done.15.refs_3_, ...), custom_call_target="tpu_custom_call" | custom-call | flops 402653184 | bytes 2097152 | tf_op jit(solution)/shard_map/lon_apply/pallas_call | solution.py:509
  (62 shorter events, 0.2 us)
Async XLA Ops:
  0.6 19.6 %copy-start = (f32[1,2,1,128,2048]{4,3,2,1,0:T(8,128)S(1)}, f32[1,2,1,128,2048]{4,3,2,1,0:T(8,128)}, u32[]{:S(2)}) copy-start(f32[1,2,1,128,2048]{4,3,2,1,0:T(8,128)} %param.23) | copy-start | bytes 6291460
  1.7 7.2 %collective-permute-start.1 = (f32[4,2048]{1,0:T(4,128)S(1)}, f32[4,2048]{1,0:T(4,128)S(1)}, u32[]{:S(2)}, u32[]{:S(2)}) collective-permute-start(f32[4,2048]{1,0:T(4,128)S(1)} %pad_maximum_fusion), channel_id=1, source_target_pairs={{1,2},{2,1},{3,4},{4,3},{5,6},{6,5},{9,10},{10,9},{11,12},{12,11},... | collective-permute-start | bytes 98312 | tf_op jit(solution)/shard_map/ppermute | solution.py:591
  2.4 6.6 %collective-permute-start = (f32[4,2048]{1,0:T(4,128)S(1)}, f32[4,2048]{1,0:T(4,128)S(1)}, u32[]{:S(2)}, u32[]{:S(2)}) collective-permute-start(f32[4,2048]{1,0:T(4,128)S(1)} %pad_maximum_fusion), channel_id=1, source_target_pairs={{0,1},{1,0},{2,3},{3,2},{4,5},{5,4},{6,7},{7,6},{8,9},{9,8},{10,11... | collective-permute-start | bytes 98312 | tf_op jit(solution)/shard_map/ppermute | solution.py:592
  13.4 14.8 %collective-permute-start.2 = (f32[128,1024]{1,0:T(8,128)S(1)}, f32[128,1024]{1,0:T(8,128)S(1)}, u32[]{:S(2)}, u32[]{:S(2)}) collective-permute-start(f32[128,1024]{1,0:T(8,128)S(1)} %get-tuple-element.59), channel_id=1, source_target_pairs={{0,16},{8,24},{1,17},{9,25},{2,18},{10,26},{3,19},{11,27},{4,20},{... | collective-permute-start | bytes 1572872 | tf_op jit(solution)/shard_map/ppermute | solution.py:565
  16.9 17.0 %collective-permute-start.16 = (f32[128,1024]{1,0:T(8,128)S(1)}, f32[128,1024]{1,0:T(8,128)S(1)}, u32[]{:S(2)}, u32[]{:S(2)}) collective-permute-start(f32[128,1024]{1,0:T(8,128)S(1)} %get-tuple-element.81), channel_id=1, source_target_pairs={{0,8},{8,0},{16,24},{1,9},{9,1},{17,25},{2,10},{10,2},{18,26},{3,1... | collective-permute-start | bytes 1572872 | tf_op jit(solution)/shard_map/ppermute | solution.py:565
  20.3 1.6 %copy-start.1 = (s32[1,2,128,2048]{3,2,1,0:T(8,128)S(1)}, s32[1,2,128,2048]{3,2,1,0:T(8,128)}, u32[]{:S(2)}) copy-start(s32[1,2,128,2048]{3,2,1,0:T(8,128)} %param.24) | copy-start | bytes 6291460
  23.3 20.5 %collective-permute-start.4 = (f32[128,1024]{1,0:T(8,128)S(1)}, f32[128,1024]{1,0:T(8,128)S(1)}, u32[]{:S(2)}, u32[]{:S(2)}) collective-permute-start(f32[128,1024]{1,0:T(8,128)S(1)} %get-tuple-element.61), channel_id=1, source_target_pairs={{0,8},{8,24},{1,9},{9,25},{2,10},{10,26},{3,11},{11,27},{4,12},{12... | collective-permute-start | bytes 1572872 | tf_op jit(solution)/shard_map/ppermute | solution.py:565
  28.8 19.6 %collective-permute-start.3 = (f32[128,1024]{1,0:T(8,128)S(1)}, f32[128,1024]{1,0:T(8,128)S(1)}, u32[]{:S(2)}, u32[]{:S(2)}) collective-permute-start(f32[128,1024]{1,0:T(8,128)S(1)} %mix.2), channel_id=1, source_target_pairs={{16,24},{24,16},{17,25},{25,17},{18,26},{26,18},{19,27},{27,19},{2... | collective-permute-start | bytes 1572872 | tf_op jit(solution)/shard_map/ppermute | solution.py:565
  29.5 25.5 %collective-permute-start.18 = (f32[128,1024]{1,0:T(8,128)S(1)}, f32[128,1024]{1,0:T(8,128)S(1)}, u32[]{:S(2)}, u32[]{:S(2)}) collective-permute-start(f32[128,1024]{1,0:T(8,128)S(1)} %get-tuple-element.60.one_ref), channel_id=1, source_target_pairs={{0,8},{1,9},{2,10},{3,11},{4,12},{5,13},{6,14},{7,15}} | collective-permute-start | bytes 1572872 | tf_op jit(solution)/shard_map/ppermute | solution.py:565
  34.5 36.1 %collective-permute-start.17 = (f32[128,1024]{1,0:T(8,128)S(1)}, f32[128,1024]{1,0:T(8,128)S(1)}, u32[]{:S(2)}, u32[]{:S(2)}) collective-permute-start(f32[128,1024]{1,0:T(8,128)S(1)} %mix.3), channel_id=1, source_target_pairs={{0,16},{8,24},{1,17},{9,25},{2,18},{10,26},{3,19},{11,27},{4,20},{... | collective-permute-start | bytes 1572872 | tf_op jit(solution)/shard_map/ppermute | solution.py:565
  38.9 64.6 %collective-permute-start.36 = (f32[128,1024]{1,0:T(8,128)S(1)}, f32[128,1024]{1,0:T(8,128)S(1)}, u32[]{:S(2)}, u32[]{:S(2)}) collective-permute-start(f32[128,1024]{1,0:T(8,128)S(1)} %get-tuple-element.56.plus_ref), channel_id=1, source_target_pairs={{8,16},{16,24},{9,17},{17,25},{10,18},{18,26},{11,19},{19,27},{12,... | collective-permute-start | bytes 1572872 | tf_op jit(solution)/shard_map/ppermute | solution.py:565
  43.8 59.9 %collective-permute-start.37 = (f32[128,1024]{1,0:T(8,128)S(1)}, f32[128,1024]{1,0:T(8,128)S(1)}, u32[]{:S(2)}, u32[]{:S(2)}) collective-permute-start(f32[128,1024]{1,0:T(8,128)S(1)} %get-tuple-element.57.minus_ref), channel_id=1, source_target_pairs={{0,8},{8,16},{16,24},{1,9},{9,17},{17,25},{2,10},{10,18},{18,26},{... | collective-permute-start | bytes 1572872 | tf_op jit(solution)/shard_map/ppermute | solution.py:565
  48.4 47.7 %copy-start.2 = (f32[128,256]{1,0:T(8,128)S(1)}, f32[128,256]{1,0:T(8,128)}, u32[]{:S(2)}) copy-start(f32[128,256]{1,0:T(8,128)} %constant.33.clone.middle_ref) | copy-start | bytes 393220
  48.4 47.7 %copy-start.10 = (f32[8,256]{1,0:T(8,128)S(1)}, f32[8,256]{1,0:T(8,128)}, u32[]{:S(2)}) copy-start(f32[8,256]{1,0:T(8,128)} %constant.35.clone.twist_ref) | copy-start | bytes 24580
  48.4 47.7 %copy-start.11 = (f32[8,256]{1,0:T(8,128)S(1)}, f32[8,256]{1,0:T(8,128)}, u32[]{:S(2)}) copy-start(f32[8,256]{1,0:T(8,128)} %constant.32.clone.inner_ref) | copy-start | bytes 24580
  48.4 47.6 %copy-start.12 = (f32[1,1024]{1,0:T(1,128)S(1)}, f32[1,1024]{1,0:T(1,128)}, u32[]{:S(2)}) copy-start(f32[1,1024]{1,0:T(1,128)} %d_ref.2) | copy-start | bytes 12292
  48.5 47.6 %copy-start.13 = (f32[8,8]{1,0:T(8,128)S(1)}, f32[8,8]{1,0:T(8,128)}, u32[]{:S(2)}) copy-start(f32[8,8]{1,0:T(8,128)} %constant.37.clone.sin_ref) | copy-start | bytes 772
  48.5 47.6 %copy-start.14 = (f32[8,8]{1,0:T(8,128)S(1)}, f32[8,8]{1,0:T(8,128)}, u32[]{:S(2)}) copy-start(f32[8,8]{1,0:T(8,128)} %constant.36.clone.cos_ref) | copy-start | bytes 772
  48.5 47.6 %copy-start.15 = (f32[8,128]{1,0:T(8,128)S(1)}, f32[8,128]{1,0:T(8,128)}, u32[]{:S(2)}) copy-start(f32[8,128]{1,0:T(8,128)} %constant.34.clone.member_ref) | copy-start | bytes 12292
  49.3 21.3 %collective-permute-start.5 = (f32[128,128]{1,0:T(8,128)S(1)}, f32[128,128]{1,0:T(8,128)S(1)}, u32[]{:S(2)}, u32[]{:S(2)}) collective-permute-start(f32[128,128]{1,0:T(8,128)S(1)} %get-tuple-element.63), channel_id=1, source_target_pairs={{0,1},{1,0},{2,3},{3,2},{4,5},{5,4},{6,7},{7,6},{8,9},{9,8},{10,11... | collective-permute-start | bytes 196616 | tf_op jit(solution)/shard_map/ppermute | solution.py:560
  55.0 18.1 %collective-permute-start.6 = (f32[128,128]{1,0:T(8,128)S(1)}, f32[128,128]{1,0:T(8,128)S(1)}, u32[]{:S(2)}, u32[]{:S(2)}) collective-permute-start(f32[128,128]{1,0:T(8,128)S(1)} %get-tuple-element.64), channel_id=1, source_target_pairs={{0,2},{1,3},{2,0},{3,1},{4,6},{5,7},{6,4},{7,5},{8,10},{9,11},{10,... | collective-permute-start | bytes 196616 | tf_op jit(solution)/shard_map/ppermute | solution.py:560
  70.6 4.8 %collective-permute-start.7 = (f32[128,128]{1,0:T(8,128)S(1)}, f32[128,128]{1,0:T(8,128)S(1)}, u32[]{:S(2)}, u32[]{:S(2)}) collective-permute-start(f32[128,128]{1,0:T(8,128)S(1)} %get-tuple-element.65), channel_id=1, source_target_pairs={{0,3},{1,2},{2,1},{3,0},{4,7},{5,6},{6,5},{7,4},{8,11},{9,10},{10,... | collective-permute-start | bytes 196616 | tf_op jit(solution)/shard_map/ppermute | solution.py:560
  70.6 7.3 %collective-permute-start.8 = (f32[128,128]{1,0:T(8,128)S(1)}, f32[128,128]{1,0:T(8,128)S(1)}, u32[]{:S(2)}, u32[]{:S(2)}) collective-permute-start(f32[128,128]{1,0:T(8,128)S(1)} %get-tuple-element.66), channel_id=1, source_target_pairs={{0,4},{1,5},{2,6},{3,7},{4,0},{5,1},{6,2},{7,3},{8,12},{9,13},{10,... | collective-permute-start | bytes 196616 | tf_op jit(solution)/shard_map/ppermute | solution.py:560
  73.2 9.0 %collective-permute-start.9 = (f32[128,128]{1,0:T(8,128)S(1)}, f32[128,128]{1,0:T(8,128)S(1)}, u32[]{:S(2)}, u32[]{:S(2)}) collective-permute-start(f32[128,128]{1,0:T(8,128)S(1)} %get-tuple-element.67), channel_id=1, source_target_pairs={{0,5},{1,4},{2,7},{3,6},{4,1},{5,0},{6,3},{7,2},{8,13},{9,12},{10,... | collective-permute-start | bytes 196616 | tf_op jit(solution)/shard_map/ppermute | solution.py:560
  75.4 6.8 %collective-permute-start.10 = (f32[128,128]{1,0:T(8,128)S(1)}, f32[128,128]{1,0:T(8,128)S(1)}, u32[]{:S(2)}, u32[]{:S(2)}) collective-permute-start(f32[128,128]{1,0:T(8,128)S(1)} %get-tuple-element.68), channel_id=1, source_target_pairs={{0,6},{1,7},{2,4},{3,5},{4,2},{5,3},{6,0},{7,1},{8,14},{9,15},{10,... | collective-permute-start | bytes 196616 | tf_op jit(solution)/shard_map/ppermute | solution.py:560
  77.9 6.8 %collective-permute-start.11 = (f32[128,128]{1,0:T(8,128)S(1)}, f32[128,128]{1,0:T(8,128)S(1)}, u32[]{:S(2)}, u32[]{:S(2)}) collective-permute-start(f32[128,128]{1,0:T(8,128)S(1)} %get-tuple-element.69), channel_id=1, source_target_pairs={{0,7},{1,6},{2,5},{3,4},{4,3},{5,2},{6,1},{7,0},{8,15},{9,14},{10,... | collective-permute-start | bytes 196616 | tf_op jit(solution)/shard_map/ppermute | solution.py:560
  82.2 4.4 %collective-permute-start.19 = (f32[128,128]{1,0:T(8,128)S(1)}, f32[128,128]{1,0:T(8,128)S(1)}, u32[]{:S(2)}, u32[]{:S(2)}) collective-permute-start(f32[128,128]{1,0:T(8,128)S(1)} %get-tuple-element.84), channel_id=1, source_target_pairs={{0,1},{1,0},{2,3},{3,2},{4,5},{5,4},{6,7},{7,6},{8,9},{9,8},{10,11... | collective-permute-start | bytes 196616 | tf_op jit(solution)/shard_map/ppermute | solution.py:560
  82.2 5.9 %collective-permute-start.20 = (f32[128,128]{1,0:T(8,128)S(1)}, f32[128,128]{1,0:T(8,128)S(1)}, u32[]{:S(2)}, u32[]{:S(2)}) collective-permute-start(f32[128,128]{1,0:T(8,128)S(1)} %get-tuple-element.85), channel_id=1, source_target_pairs={{0,2},{1,3},{2,0},{3,1},{4,6},{5,7},{6,4},{7,5},{8,10},{9,11},{10,... | collective-permute-start | bytes 196616 | tf_op jit(solution)/shard_map/ppermute | solution.py:560
  84.7 4.6 %collective-permute-start.21 = (f32[128,128]{1,0:T(8,128)S(1)}, f32[128,128]{1,0:T(8,128)S(1)}, u32[]{:S(2)}, u32[]{:S(2)}) collective-permute-start(f32[128,128]{1,0:T(8,128)S(1)} %get-tuple-element.86), channel_id=1, source_target_pairs={{0,3},{1,2},{2,1},{3,0},{4,7},{5,6},{6,5},{7,4},{8,11},{9,10},{10,... | collective-permute-start | bytes 196616 | tf_op jit(solution)/shard_map/ppermute | solution.py:560
  86.5 9.6 %collective-permute-start.22 = (f32[128,128]{1,0:T(8,128)S(1)}, f32[128,128]{1,0:T(8,128)S(1)}, u32[]{:S(2)}, u32[]{:S(2)}) collective-permute-start(f32[128,128]{1,0:T(8,128)S(1)} %get-tuple-element.87), channel_id=1, source_target_pairs={{0,4},{1,5},{2,6},{3,7},{4,0},{5,1},{6,2},{7,3},{8,12},{9,13},{10,... | collective-permute-start | bytes 196616 | tf_op jit(solution)/shard_map/ppermute | solution.py:560
  88.1 11.2 %collective-permute-start.23 = (f32[128,128]{1,0:T(8,128)S(1)}, f32[128,128]{1,0:T(8,128)S(1)}, u32[]{:S(2)}, u32[]{:S(2)}) collective-permute-start(f32[128,128]{1,0:T(8,128)S(1)} %get-tuple-element.88), channel_id=1, source_target_pairs={{0,5},{1,4},{2,7},{3,6},{4,1},{5,0},{6,3},{7,2},{8,13},{9,12},{10,... | collective-permute-start | bytes 196616 | tf_op jit(solution)/shard_map/ppermute | solution.py:560
  89.2 10.2 %collective-permute-start.24 = (f32[128,128]{1,0:T(8,128)S(1)}, f32[128,128]{1,0:T(8,128)S(1)}, u32[]{:S(2)}, u32[]{:S(2)}) collective-permute-start(f32[128,128]{1,0:T(8,128)S(1)} %get-tuple-element.89), channel_id=1, source_target_pairs={{0,6},{1,7},{2,4},{3,5},{4,2},{5,3},{6,0},{7,1},{8,14},{9,15},{10,... | collective-permute-start | bytes 196616 | tf_op jit(solution)/shard_map/ppermute | solution.py:560
  96.1 6.0 %collective-permute-start.25 = (f32[128,128]{1,0:T(8,128)S(1)}, f32[128,128]{1,0:T(8,128)S(1)}, u32[]{:S(2)}, u32[]{:S(2)}) collective-permute-start(f32[128,128]{1,0:T(8,128)S(1)} %get-tuple-element.90), channel_id=1, source_target_pairs={{0,7},{1,6},{2,5},{3,4},{4,3},{5,2},{6,1},{7,0},{8,15},{9,14},{10,... | collective-permute-start | bytes 196616 | tf_op jit(solution)/shard_map/ppermute | solution.py:560
  97.8 14.3 %copy-start.3 = (f32[128,256]{1,0:T(8,128)S(1)}, f32[128,256]{1,0:T(8,128)}, u32[]{:S(2)}) copy-start(f32[128,256]{1,0:T(8,128)} %constant.39.clone.middle_ref) | copy-start | bytes 393220
  97.8 14.2 %copy-start.4 = (f32[16,256]{1,0:T(8,128)S(1)}, f32[16,256]{1,0:T(8,128)}, u32[]{:S(2)}) copy-start(f32[16,256]{1,0:T(8,128)} %constant.41.clone.twist_ref) | copy-start | bytes 49156
  97.8 14.2 %copy-start.5 = (f32[16,256]{1,0:T(8,128)S(1)}, f32[16,256]{1,0:T(8,128)}, u32[]{:S(2)}) copy-start(f32[16,256]{1,0:T(8,128)} %constant.38.clone.inner_ref) | copy-start | bytes 49156
  97.8 14.2 %copy-start.6 = (f32[1,2048]{1,0:T(1,128)S(1)}, f32[1,2048]{1,0:T(1,128)}, u32[]{:S(2)}) copy-start(f32[1,2048]{1,0:T(1,128)} %d_ref.3) | copy-start | bytes 24580
  97.8 14.2 %copy-start.7 = (f32[16,16]{1,0:T(8,128)S(1)}, f32[16,16]{1,0:T(8,128)}, u32[]{:S(2)}) copy-start(f32[16,16]{1,0:T(8,128)} %constant.43.clone.sin_ref) | copy-start | bytes 3076
  97.8 14.2 %copy-start.8 = (f32[16,16]{1,0:T(8,128)S(1)}, f32[16,16]{1,0:T(8,128)}, u32[]{:S(2)}) copy-start(f32[16,16]{1,0:T(8,128)} %constant.42.clone.cos_ref) | copy-start | bytes 3076
  97.8 14.2 %copy-start.9 = (f32[16,128]{1,0:T(8,128)S(1)}, f32[16,128]{1,0:T(8,128)}, u32[]{:S(2)}) copy-start(f32[16,128]{1,0:T(8,128)} %constant.40.clone.member_ref) | copy-start | bytes 24580
  99.3 6.4 %collective-permute-start.33 = (f32[128,128]{1,0:T(8,128)S(1)}, f32[128,128]{1,0:T(8,128)S(1)}, u32[]{:S(2)}, u32[]{:S(2)}) collective-permute-start(f32[128,128]{1,0:T(8,128)S(1)} %get-tuple-element.102), channel_id=1, source_target_pairs={{0,1},{1,0},{2,3},{3,2},{4,5},{5,4},{6,7},{7,6},{8,9},{9,8},{10,11... | collective-permute-start | bytes 196616 | tf_op jit(solution)/shard_map/ppermute | solution.py:560
  99.4 6.3 %collective-permute-start.34 = (f32[128,128]{1,0:T(8,128)S(1)}, f32[128,128]{1,0:T(8,128)S(1)}, u32[]{:S(2)}, u32[]{:S(2)}) collective-permute-start(f32[128,128]{1,0:T(8,128)S(1)} %get-tuple-element.103), channel_id=1, source_target_pairs={{0,2},{1,3},{2,0},{3,1},{4,6},{5,7},{6,4},{7,5},{8,10},{9,11},{10,... | collective-permute-start | bytes 196616 | tf_op jit(solution)/shard_map/ppermute | solution.py:560
  102.1 5.6 %collective-permute-start.35 = (f32[128,128]{1,0:T(8,128)S(1)}, f32[128,128]{1,0:T(8,128)S(1)}, u32[]{:S(2)}, u32[]{:S(2)}) collective-permute-start(f32[128,128]{1,0:T(8,128)S(1)} %get-tuple-element.104), channel_id=1, source_target_pairs={{0,3},{1,2},{2,1},{3,0},{4,7},{5,6},{6,5},{7,4},{8,11},{9,10},{10,... | collective-permute-start | bytes 196616 | tf_op jit(solution)/shard_map/ppermute | solution.py:560
  103.5 4.7 %collective-permute-start.26 = (f32[128,128]{1,0:T(8,128)S(1)}, f32[128,128]{1,0:T(8,128)S(1)}, u32[]{:S(2)}, u32[]{:S(2)}) collective-permute-start(f32[128,128]{1,0:T(8,128)S(1)} %get-tuple-element.92), channel_id=1, source_target_pairs={{0,1},{1,0},{2,3},{3,2},{4,5},{5,4},{6,7},{7,6},{8,9},{9,8},{10,11... | collective-permute-start | bytes 196616 | tf_op jit(solution)/shard_map/ppermute | solution.py:560
  103.7 7.7 %collective-permute-start.27 = (f32[128,128]{1,0:T(8,128)S(1)}, f32[128,128]{1,0:T(8,128)S(1)}, u32[]{:S(2)}, u32[]{:S(2)}) collective-permute-start(f32[128,128]{1,0:T(8,128)S(1)} %get-tuple-element.93), channel_id=1, source_target_pairs={{0,2},{1,3},{2,0},{3,1},{4,6},{5,7},{6,4},{7,5},{8,10},{9,11},{10,... | collective-permute-start | bytes 196616 | tf_op jit(solution)/shard_map/ppermute | solution.py:560
  105.7 12.7 %collective-permute-start.28 = (f32[128,128]{1,0:T(8,128)S(1)}, f32[128,128]{1,0:T(8,128)S(1)}, u32[]{:S(2)}, u32[]{:S(2)}) collective-permute-start(f32[128,128]{1,0:T(8,128)S(1)} %get-tuple-element.94), channel_id=1, source_target_pairs={{0,3},{1,2},{2,1},{3,0},{4,7},{5,6},{6,5},{7,4},{8,11},{9,10},{10,... | collective-permute-start | bytes 196616 | tf_op jit(solution)/shard_map/ppermute | solution.py:560
  105.8 12.9 %collective-permute-start.29 = (f32[128,128]{1,0:T(8,128)S(1)}, f32[128,128]{1,0:T(8,128)S(1)}, u32[]{:S(2)}, u32[]{:S(2)}) collective-permute-start(f32[128,128]{1,0:T(8,128)S(1)} %get-tuple-element.95), channel_id=1, source_target_pairs={{0,4},{1,5},{2,6},{3,7},{4,0},{5,1},{6,2},{7,3},{8,12},{9,13},{10,... | collective-permute-start | bytes 196616 | tf_op jit(solution)/shard_map/ppermute | solution.py:560
  107.7 13.3 %collective-permute-start.30 = (f32[128,128]{1,0:T(8,128)S(1)}, f32[128,128]{1,0:T(8,128)S(1)}, u32[]{:S(2)}, u32[]{:S(2)}) collective-permute-start(f32[128,128]{1,0:T(8,128)S(1)} %get-tuple-element.96), channel_id=1, source_target_pairs={{0,5},{1,4},{2,7},{3,6},{4,1},{5,0},{6,3},{7,2},{8,13},{9,12},{10,... | collective-permute-start | bytes 196616 | tf_op jit(solution)/shard_map/ppermute | solution.py:560
  108.2 16.0 %collective-permute-start.31 = (f32[128,128]{1,0:T(8,128)S(1)}, f32[128,128]{1,0:T(8,128)S(1)}, u32[]{:S(2)}, u32[]{:S(2)}) collective-permute-start(f32[128,128]{1,0:T(8,128)S(1)} %get-tuple-element.97), channel_id=1, source_target_pairs={{0,6},{1,7},{2,4},{3,5},{4,2},{5,3},{6,0},{7,1},{8,14},{9,15},{10,... | collective-permute-start | bytes 196616 | tf_op jit(solution)/shard_map/ppermute | solution.py:560
  111.4 13.3 %collective-permute-start.32 = (f32[128,128]{1,0:T(8,128)S(1)}, f32[128,128]{1,0:T(8,128)S(1)}, u32[]{:S(2)}, u32[]{:S(2)}) collective-permute-start(f32[128,128]{1,0:T(8,128)S(1)} %get-tuple-element.98), channel_id=1, source_target_pairs={{0,7},{1,6},{2,5},{3,4},{4,3},{5,2},{6,1},{7,0},{8,15},{9,14},{10,... | collective-permute-start | bytes 196616 | tf_op jit(solution)/shard_map/ppermute | solution.py:560
  118.5 10.0 %collective-permute-start.12 = (f32[128,128]{1,0:T(8,128)S(1)}, f32[128,128]{1,0:T(8,128)S(1)}, u32[]{:S(2)}, u32[]{:S(2)}) collective-permute-start(f32[128,128]{1,0:T(8,128)S(1)} %get-tuple-element.74), channel_id=1, source_target_pairs={{0,4},{1,5},{2,6},{3,7},{4,0},{5,1},{6,2},{7,3},{8,12},{9,13},{10,... | collective-permute-start | bytes 196616 | tf_op jit(solution)/shard_map/ppermute | solution.py:560
  118.6 9.9 %collective-permute-start.13 = (f32[128,128]{1,0:T(8,128)S(1)}, f32[128,128]{1,0:T(8,128)S(1)}, u32[]{:S(2)}, u32[]{:S(2)}) collective-permute-start(f32[128,128]{1,0:T(8,128)S(1)} %get-tuple-element.75), channel_id=1, source_target_pairs={{0,5},{1,4},{2,7},{3,6},{4,1},{5,0},{6,3},{7,2},{8,13},{9,12},{10,... | collective-permute-start | bytes 196616 | tf_op jit(solution)/shard_map/ppermute | solution.py:560
  120.9 7.6 %collective-permute-start.14 = (f32[128,128]{1,0:T(8,128)S(1)}, f32[128,128]{1,0:T(8,128)S(1)}, u32[]{:S(2)}, u32[]{:S(2)}) collective-permute-start(f32[128,128]{1,0:T(8,128)S(1)} %get-tuple-element.76), channel_id=1, source_target_pairs={{0,6},{1,7},{2,4},{3,5},{4,2},{5,3},{6,0},{7,1},{8,14},{9,15},{10,... | collective-permute-start | bytes 196616 | tf_op jit(solution)/shard_map/ppermute | solution.py:560
  124.2 6.3 %collective-permute-start.15 = (f32[128,128]{1,0:T(8,128)S(1)}, f32[128,128]{1,0:T(8,128)S(1)}, u32[]{:S(2)}, u32[]{:S(2)}) collective-permute-start(f32[128,128]{1,0:T(8,128)S(1)} %get-tuple-element.77), channel_id=1, source_target_pairs={{0,7},{1,6},{2,5},{3,4},{4,3},{5,2},{6,1},{7,0},{8,15},{9,14},{10,... | collective-permute-start | bytes 196616 | tf_op jit(solution)/shard_map/ppermute | solution.py:560
